TPU v7x, 32 devices: a whole 2x2x4 slice. The times are simulated.
32 devices in a mesh: dp: 2 (over x), ctx: 4 (over y, core), tp: 4 (over z).
Axes of the slice: x: 2, y: 2, z: 4, core: 2. Of those that a mesh axis runs over, the one named last changes fastest.
Arguments:
- block_in: bfloat16 [4, 2048, 2048], P(None, ('dp', 'ctx', 'tp')), may hold values from -6 to 6
- segments: int32 [4, 2048], P(None, 'dp'), may hold values from 0 to 1023, as said below
- positions: int32 [4, 2048], P(None, 'dp'), may hold values from 0 to 1023, as said below
- attention_gain: bfloat16 [2048], P(('dp', 'ctx')), may hold values from 0.5 to 1.5
- query_weight: bfloat16 [2048, 2048], P(('dp', 'ctx'), 'tp'), may hold values from -0.125 to 0.125
- key_weight: bfloat16 [2048, 512], P(('dp', 'ctx'), 'tp'), may hold values from -0.125 to 0.125
- value_weight: bfloat16 [2048, 512], P(('dp', 'ctx'), 'tp'), may hold values from -0.125 to 0.125
- query_gain: bfloat16 [64], replicated, may hold values from 1 to 2
- key_gain: bfloat16 [64], replicated, may hold values from 0.25 to 1.75
- output_weight: bfloat16 [2048, 2048], P('tp', ('dp', 'ctx')), may hold values from -0.75 to 0.75
- hidden_gain: bfloat16 [2048], P(('dp', 'ctx')), may hold values from 0.5 to 1.5
- gate_weight: bfloat16 [2048, 8192], P(('dp', 'ctx'), 'tp'), may hold values from -0.125 to 0.125
- up_weight: bfloat16 [2048, 8192], P(('dp', 'ctx'), 'tp'), may hold values from -0.125 to 0.125
- down_weight: bfloat16 [8192, 2048], P('tp', ('dp', 'ctx')), may hold values from -0.125 to 0.125
- cotangent: bfloat16 [4, 2048, 2048], P(None, ('dp', 'ctx', 'tp')), may hold values from -6 to 6
Outputs:
- block_out: bfloat16 [4, 2048, 2048], P(None, ('dp', 'ctx', 'tp'))
- input_grad: float32 [4, 2048, 2048], P(None, ('dp', 'ctx', 'tp'))
- attention_gain_grad: float32 [2048], P(('dp', 'ctx'))
- query_weight_grad: float32 [2048, 2048], P(('dp', 'ctx'), 'tp')
- key_weight_grad: float32 [2048, 512], P(('dp', 'ctx'), 'tp')
- value_weight_grad: float32 [2048, 512], P(('dp', 'ctx'), 'tp')
- query_gain_grad: float32 [64], replicated
- key_gain_grad: float32 [64], replicated
- output_weight_grad: float32 [2048, 2048], P('tp', ('dp', 'ctx'))
- hidden_gain_grad: float32 [2048], P(('dp', 'ctx'))
- gate_weight_grad: float32 [2048, 8192], P(('dp', 'ctx'), 'tp')
- up_weight_grad: float32 [2048, 8192], P(('dp', 'ctx'), 'tp')
- down_weight_grad: float32 [8192, 2048], P('tp', ('dp', 'ctx'))
Inputs may be any that keep to these rules, and one draw needn't show every extreme that they name: `segments`: within each sequence of 1024 tokens a token's id is the place, counted from 0 in that sequence, of the first token of its document; ids never fall and a document is a run of equal ids. `positions`: each token's distance from the first token of its document.
All inputs are finite; a program needn't handle non-finite values.
Results may differ from a plain program's by a relative error of at most 0.019.
Values may be sent and summed in bfloat16 or wider, within the bound.
No kernel may reach another device: no remote copies, remote signals or barrier semaphores. Data moves between devices by JAX's collectives and lax.ppermute only.
A program may use at most 320 MiB of HBM per device.

v0:
```python
import math

import jax
import jax.numpy as jnp
from jax import lax
from jax.sharding import PartitionSpec as P

D = 2048
HD = 64


NORM_EPS = 1e-05
ROPE_BASE = 1000000.0
MASKED = -1e30


def matmul(left_mat, right_mat):
    return jnp.dot(left_mat, right_mat, preferred_element_type=jnp.float32)


def matmul_tn(left_mat, right_mat):
    return lax.dot_general(
        left_mat, right_mat, (((0,), (0,)), ((), ())), preferred_element_type=jnp.float32
    )


def matmul_nt(left_mat, right_mat):
    return lax.dot_general(
        left_mat, right_mat, (((1,), (1,)), ((), ())), preferred_element_type=jnp.float32
    )


def norm_forward(values, gain_vec):
    scale_rows = lax.rsqrt(jnp.mean(values * values, axis=-1, keepdims=True) + NORM_EPS)
    unit_rows = values * scale_rows
    return (unit_rows * gain_vec, unit_rows, scale_rows)


def norm_backward(grad_rows, unit_rows, scale_rows, gain_vec):
    scaled = grad_rows * gain_vec
    return scale_rows * (scaled - unit_rows * jnp.mean(scaled * unit_rows, axis=-1, keepdims=True))


def rope_tables(position, head_width):
    half_width = head_width // 2
    frequency = ROPE_BASE ** (-2.0 * jnp.arange(half_width, dtype=jnp.float32) / head_width)
    angles = position.astype(jnp.float32)[:, None, None] * frequency[None, None, :]
    return (jnp.cos(angles), jnp.sin(angles))


def rotate(values, cos_table, sin_table):
    half_width = values.shape[-1] // 2
    former = values[..., :half_width]
    latter = values[..., half_width:]
    return jnp.concatenate(
        [former * cos_table - latter * sin_table, latter * cos_table + former * sin_table], axis=-1
    )


def rotate_back(grad_rows, cos_table, sin_table):
    half_width = grad_rows.shape[-1] // 2
    former = grad_rows[..., :half_width]
    latter = grad_rows[..., half_width:]
    return jnp.concatenate(
        [former * cos_table + latter * sin_table, latter * cos_table - former * sin_table], axis=-1
    )


def attention_mask(query_segment, seq_segment, row_start):
    query_place = row_start + jnp.arange(query_segment.shape[0], dtype=jnp.int32)
    key_place = jnp.arange(seq_segment.shape[0], dtype=jnp.int32)
    return (query_segment[:, None] == seq_segment[None, :]) & (
        query_place[:, None] >= key_place[None, :]
    )


def score_block(query_groups, key_heads, allowed):
    inv_root = 1.0 / math.sqrt(query_groups.shape[-1])
    scores = (
        jnp.einsum("qngd,knd->ngqk", query_groups, key_heads, preferred_element_type=jnp.float32)
        * inv_root
    )
    return jnp.where(allowed[None, None], scores, MASKED)


def spread_rows(values):
    return lax.all_gather(values, "tp", axis=0, tiled=True)


def fold_rows(row_fn, own_rows):
    return lax.psum_scatter(
        row_fn(jnp.int32(0), lax.axis_size("tp") * own_rows), "tp", scatter_dimension=0, tiled=True
    )


def partial_rows(operand_pairs, backward):

    def row_terms(first_row, row_count):
        product_sum = None
        for operand, matrix in operand_pairs:
            product = matmul_nt(operand, matrix) if backward else matmul(operand, matrix)
            product_sum = product if product_sum is None else product_sum + product
        return product_sum

    return row_terms


def regather(
    attention_gain,
    query_weight,
    key_weight,
    value_weight,
    output_weight,
    hidden_gain,
    gate_weight,
    up_weight,
    down_weight,
):
    return (
        lax.all_gather(attention_gain, ("dp", "ctx"), axis=0, tiled=True),
        lax.all_gather(query_weight, ("dp", "ctx"), axis=0, tiled=True),
        lax.all_gather(key_weight, ("dp", "ctx"), axis=0, tiled=True),
        lax.all_gather(value_weight, ("dp", "ctx"), axis=0, tiled=True),
        lax.all_gather(output_weight, ("dp", "ctx"), axis=1, tiled=True),
        lax.all_gather(hidden_gain, ("dp", "ctx"), axis=0, tiled=True),
        lax.all_gather(gate_weight, ("dp", "ctx"), axis=0, tiled=True),
        lax.all_gather(up_weight, ("dp", "ctx"), axis=0, tiled=True),
        lax.all_gather(down_weight, ("dp", "ctx"), axis=1, tiled=True),
    )


def per_device(
    block_in,
    segments,
    positions,
    attention_gain,
    query_weight,
    key_weight,
    value_weight,
    query_gain,
    key_gain,
    output_weight,
    hidden_gain,
    gate_weight,
    up_weight,
    down_weight,
    cotangent,
):
    tp_count = lax.axis_size("tp")
    ctx_index = lax.axis_index("ctx")
    own_rows = block_in.shape[1]
    ctx_rows = own_rows * tp_count
    seq_len = segments.shape[1]
    row_start = ctx_index * ctx_rows
    query_gain_f = query_gain.astype(jnp.float32)
    key_gain_f = key_gain.astype(jnp.float32)
    query_grad = jnp.zeros((D, query_weight.shape[1]), jnp.float32)
    key_grad = jnp.zeros((D, key_weight.shape[1]), jnp.float32)
    value_grad = jnp.zeros((D, value_weight.shape[1]), jnp.float32)
    output_grad = jnp.zeros((output_weight.shape[0], D), jnp.float32)
    gate_grad = jnp.zeros((D, gate_weight.shape[1]), jnp.float32)
    up_grad = jnp.zeros((D, up_weight.shape[1]), jnp.float32)
    down_grad = jnp.zeros((down_weight.shape[0], D), jnp.float32)
    attention_gain_acc = jnp.zeros((D,), jnp.float32)
    hidden_gain_acc = jnp.zeros((D,), jnp.float32)
    query_gain_acc = jnp.zeros((HD,), jnp.float32)
    key_gain_acc = jnp.zeros((HD,), jnp.float32)
    outputs = []
    input_grads = []
    for batch_index in range(block_in.shape[0]):
        fetched = regather(
            attention_gain,
            query_weight,
            key_weight,
            value_weight,
            output_weight,
            hidden_gain,
            gate_weight,
            up_weight,
            down_weight,
        )
        (
            gain_attention,
            full_query,
            full_key,
            full_value,
            full_output,
            gain_hidden,
            full_gate,
            full_up,
            full_down,
        ) = fetched
        gain_attention = gain_attention.astype(jnp.float32)
        gain_hidden = gain_hidden.astype(jnp.float32)
        tokens = block_in[batch_index].astype(jnp.float32)
        seq_segment = segments[batch_index]
        query_segment = lax.dynamic_slice_in_dim(seq_segment, row_start, ctx_rows, 0)
        query_position = lax.dynamic_slice_in_dim(positions[batch_index], row_start, ctx_rows, 0)
        cos_table, sin_table = rope_tables(query_position, HD)
        normed, unit_attention, scale_attention = norm_forward(tokens, gain_attention)
        normed_rows = spread_rows(normed.astype(jnp.bfloat16))
        query_raw = matmul(normed_rows, full_query).reshape(ctx_rows, -1, HD)
        key_raw = matmul(normed_rows, full_key).reshape(ctx_rows, -1, HD)
        value_rows = matmul(normed_rows, full_value).astype(jnp.bfloat16)
        query_normed, query_unit, query_scale = norm_forward(query_raw, query_gain_f)
        key_normed, key_unit, key_scale = norm_forward(key_raw, key_gain_f)
        query_rot = rotate(query_normed, cos_table, sin_table).astype(jnp.bfloat16)
        key_rot = (
            rotate(key_normed, cos_table, sin_table).astype(jnp.bfloat16).reshape(ctx_rows, -1)
        )
        key_all, value_all = (
            lax.all_gather(key_rot, "ctx", axis=0, tiled=True),
            lax.all_gather(value_rows, "ctx", axis=0, tiled=True),
        )
        head_groups = key_rot.shape[1] // HD
        group_size = query_rot.shape[1] // head_groups
        query_groups = query_rot.reshape(ctx_rows, head_groups, group_size, HD)
        key_heads = key_all.reshape(seq_len, head_groups, HD)
        value_heads = value_all.reshape(seq_len, head_groups, HD)
        allowed = attention_mask(query_segment, seq_segment, row_start)
        scores = score_block(query_groups, key_heads, allowed)
        row_top = jnp.max(scores, axis=-1, keepdims=True)
        exp_scores = jnp.exp(scores - row_top)
        row_total = jnp.sum(exp_scores, axis=-1, keepdims=True)
        log_total = row_top + jnp.log(row_total)
        prob_low = (exp_scores / row_total).astype(jnp.bfloat16)
        attended = jnp.einsum(
            "ngqk,knd->qngd", prob_low, value_heads, preferred_element_type=jnp.float32
        )
        attended_low = attended.reshape(ctx_rows, -1).astype(jnp.bfloat16)
        mixed_in = fold_rows(partial_rows(((attended_low, full_output),), False), own_rows)
        hidden = tokens + mixed_in
        hidden_normed, unit_hidden, scale_hidden = norm_forward(hidden, gain_hidden)
        hidden_rows = spread_rows(hidden_normed.astype(jnp.bfloat16))
        gate_proj = matmul(hidden_rows, full_gate)
        up_proj = matmul(hidden_rows, full_up)
        sigmoid_gate = jax.nn.sigmoid(gate_proj)
        silu_gate = gate_proj * sigmoid_gate
        activation = (silu_gate * up_proj).astype(jnp.bfloat16)
        feed_out = fold_rows(partial_rows(((activation, full_down),), False), own_rows)
        outputs.append((hidden + feed_out).astype(jnp.bfloat16))
        fetched = regather(
            attention_gain,
            query_weight,
            key_weight,
            value_weight,
            output_weight,
            hidden_gain,
            gate_weight,
            up_weight,
            down_weight,
        )
        (
            gain_attention,
            full_query,
            full_key,
            full_value,
            full_output,
            gain_hidden,
            full_gate,
            full_up,
            full_down,
        ) = fetched
        gain_attention = gain_attention.astype(jnp.float32)
        gain_hidden = gain_hidden.astype(jnp.float32)
        grad_own = cotangent[batch_index]
        grad_rows = spread_rows(grad_own)
        down_grad = down_grad + matmul_tn(activation, grad_rows)
        grad_act = matmul_nt(grad_rows, full_down)
        grad_gate_low = (
            grad_act * up_proj * sigmoid_gate * (1.0 + gate_proj * (1.0 - sigmoid_gate))
        ).astype(jnp.bfloat16)
        grad_up_low = (grad_act * silu_gate).astype(jnp.bfloat16)
        gate_grad = gate_grad + matmul_tn(hidden_rows, grad_gate_low)
        up_grad = up_grad + matmul_tn(hidden_rows, grad_up_low)
        grad_hidden_normed = fold_rows(
            partial_rows(((grad_gate_low, full_gate), (grad_up_low, full_up)), True), own_rows
        )
        hidden_gain_acc = hidden_gain_acc + jnp.sum(grad_hidden_normed * unit_hidden, axis=0)
        grad_hidden = grad_own.astype(jnp.float32) + norm_backward(
            grad_hidden_normed, unit_hidden, scale_hidden, gain_hidden
        )
        branch_rows = spread_rows(grad_hidden.astype(jnp.bfloat16))
        output_grad = output_grad + matmul_tn(attended_low, branch_rows)
        grad_att = (
            matmul_nt(branch_rows, full_output)
            .astype(jnp.bfloat16)
            .reshape(ctx_rows, head_groups, group_size, HD)
        )
        scores = score_block(query_groups, key_heads, allowed)
        probability = jnp.exp(scores - log_total)
        prob_low = probability.astype(jnp.bfloat16)
        grad_prob = jnp.einsum(
            "qngd,knd->ngqk", grad_att, value_heads, preferred_element_type=jnp.float32
        )
        row_delta = jnp.sum(probability * grad_prob, axis=-1, keepdims=True)
        grad_scores = (probability * (grad_prob - row_delta)).astype(jnp.bfloat16)
        inv_root = 1.0 / math.sqrt(HD)
        grad_query = (
            jnp.einsum("ngqk,knd->qngd", grad_scores, key_heads, preferred_element_type=jnp.float32)
            * inv_root
        )
        grad_key_all = (
            jnp.einsum(
                "ngqk,qngd->knd", grad_scores, query_groups, preferred_element_type=jnp.float32
            )
            * inv_root
        )
        grad_value_all = jnp.einsum(
            "ngqk,qngd->knd", prob_low, grad_att, preferred_element_type=jnp.float32
        )
        grad_key, grad_value = (
            lax.psum_scatter(
                grad_key_all.reshape(seq_len, -1), "ctx", scatter_dimension=0, tiled=True
            ),
            lax.psum_scatter(
                grad_value_all.reshape(seq_len, -1), "ctx", scatter_dimension=0, tiled=True
            ),
        )
        grad_query_rot = rotate_back(grad_query.reshape(ctx_rows, -1, HD), cos_table, sin_table)
        query_gain_acc = query_gain_acc + jnp.sum(grad_query_rot * query_unit, axis=(0, 1))
        grad_query_low = (
            norm_backward(grad_query_rot, query_unit, query_scale, query_gain_f)
            .astype(jnp.bfloat16)
            .reshape(ctx_rows, -1)
        )
        grad_key_rot = rotate_back(grad_key.reshape(ctx_rows, -1, HD), cos_table, sin_table)
        key_gain_acc = key_gain_acc + jnp.sum(grad_key_rot * key_unit, axis=(0, 1))
        grad_key_low = (
            norm_backward(grad_key_rot, key_unit, key_scale, key_gain_f)
            .astype(jnp.bfloat16)
            .reshape(ctx_rows, -1)
        )
        grad_value_low = grad_value.astype(jnp.bfloat16)
        query_grad = query_grad + matmul_tn(normed_rows, grad_query_low)
        key_grad = key_grad + matmul_tn(normed_rows, grad_key_low)
        value_grad = value_grad + matmul_tn(normed_rows, grad_value_low)
        grad_normed = fold_rows(
            partial_rows(
                (
                    (grad_query_low, full_query),
                    (grad_key_low, full_key),
                    (grad_value_low, full_value),
                ),
                True,
            ),
            own_rows,
        )
        attention_gain_acc = attention_gain_acc + jnp.sum(grad_normed * unit_attention, axis=0)
        input_grads.append(
            grad_hidden
            + norm_backward(grad_normed, unit_attention, scale_attention, gain_attention)
        )
    gain_totals = lax.psum(
        (attention_gain_acc, hidden_gain_acc, query_gain_acc, key_gain_acc), ("dp", "ctx", "tp")
    )
    shard_width = attention_gain.shape[0]
    shard_index = lax.axis_index("dp") * lax.axis_size("ctx") + ctx_index
    attention_gain_grad = lax.dynamic_slice_in_dim(
        gain_totals[0], shard_index * shard_width, shard_width, 0
    )
    hidden_gain_grad = lax.dynamic_slice_in_dim(
        gain_totals[1], shard_index * shard_width, shard_width, 0
    )
    summed = (
        lax.psum_scatter(
            query_grad.astype(jnp.bfloat16), ("dp", "ctx"), scatter_dimension=0, tiled=True
        ).astype(jnp.float32),
        lax.psum_scatter(
            key_grad.astype(jnp.bfloat16), ("dp", "ctx"), scatter_dimension=0, tiled=True
        ).astype(jnp.float32),
        lax.psum_scatter(
            value_grad.astype(jnp.bfloat16), ("dp", "ctx"), scatter_dimension=0, tiled=True
        ).astype(jnp.float32),
        lax.psum_scatter(
            output_grad.astype(jnp.bfloat16), ("dp", "ctx"), scatter_dimension=1, tiled=True
        ).astype(jnp.float32),
        lax.psum_scatter(
            gate_grad.astype(jnp.bfloat16), ("dp", "ctx"), scatter_dimension=0, tiled=True
        ).astype(jnp.float32),
        lax.psum_scatter(
            up_grad.astype(jnp.bfloat16), ("dp", "ctx"), scatter_dimension=0, tiled=True
        ).astype(jnp.float32),
        lax.psum_scatter(
            down_grad.astype(jnp.bfloat16), ("dp", "ctx"), scatter_dimension=1, tiled=True
        ).astype(jnp.float32),
    )
    return (
        jnp.stack(outputs),
        jnp.stack(input_grads),
        attention_gain_grad,
        summed[0],
        summed[1],
        summed[2],
        gain_totals[2],
        gain_totals[3],
        summed[3],
        hidden_gain_grad,
        summed[4],
        summed[5],
        summed[6],
    )


def solution(mesh):
    in_specs = (
        P(None, ("dp", "ctx", "tp"), None),
        P(None, "dp"),
        P(None, "dp"),
        P(("dp", "ctx")),
        P(("dp", "ctx"), "tp"),
        P(("dp", "ctx"), "tp"),
        P(("dp", "ctx"), "tp"),
        P(),
        P(),
        P("tp", ("dp", "ctx")),
        P(("dp", "ctx")),
        P(("dp", "ctx"), "tp"),
        P(("dp", "ctx"), "tp"),
        P("tp", ("dp", "ctx")),
        P(None, ("dp", "ctx", "tp"), None),
    )
    out_specs = (
        P(None, ("dp", "ctx", "tp"), None),
        P(None, ("dp", "ctx", "tp"), None),
        P(("dp", "ctx")),
        P(("dp", "ctx"), "tp"),
        P(("dp", "ctx"), "tp"),
        P(("dp", "ctx"), "tp"),
        P(),
        P(),
        P("tp", ("dp", "ctx")),
        P(("dp", "ctx")),
        P(("dp", "ctx"), "tp"),
        P(("dp", "ctx"), "tp"),
        P("tp", ("dp", "ctx")),
    )
    return jax.shard_map(
        per_device, mesh=mesh, in_specs=in_specs, out_specs=out_specs, check_vma=False
    )
```

profile of v0, /device:TPU:0, one launch (start us, length us, event | category | flops | bytes accessed | tf_op | source)
XLA Modules:
  0.0 2066.8 jit_solution(4941779007642822085)
XLA Ops:
  53.1 27.7 %all-gather.42.cloned.1.call-done = bf16[256,2048]{1,0:T(8,128)(2,1)} async-done(((bf16[64,2048]{1,0:T(8,128)(2,1)}), bf16[256,2048]{1,0:T(8,128)(2,1)}) %all-gather.42.cloned.1.call-update) | async-done | bytes 1048592 | tf_op jit(solution)/shard_map/all_gather | solution.py:87
  82.6 27.8 %all-gather.46.cloned.1.call-done = bf16[256,2048]{1,0:T(8,128)(2,1)} async-done(((bf16[64,2048]{1,0:T(8,128)(2,1)}), bf16[256,2048]{1,0:T(8,128)(2,1)}) %all-gather.46.cloned.1.call-update) | async-done | bytes 1048592 | tf_op jit(solution)/shard_map/all_gather | solution.py:87
  112.2 27.7 %all-gather.28.cloned.1.call-done = bf16[256,2048]{1,0:T(8,128)(2,1)} async-done(((bf16[64,2048]{1,0:T(8,128)(2,1)}), bf16[256,2048]{1,0:T(8,128)(2,1)}) %all-gather.28.cloned.1.call-update) | async-done | bytes 1048592 | tf_op jit(solution)/shard_map/all_gather | solution.py:87
  299.3 46.1 %reduce-scatter.36.cloned.1.call-done = f32[64,2048]{1,0:T(8,128)} async-done(((f32[256,2048]{1,0:T(8,128)}), f32[64,2048]{1,0:T(8,128)}) %reduce-scatter.36.cloned.1.call-update) | async-done | bytes 524304 | tf_op jit(solution)/shard_map/reduce_scatter | solution.py:91
  345.4 46.0 %reduce-scatter.32.cloned.1.call-done = f32[64,2048]{1,0:T(8,128)} async-done(((f32[256,2048]{1,0:T(8,128)}), f32[64,2048]{1,0:T(8,128)}) %reduce-scatter.32.cloned.1.call-update) | async-done | bytes 524304 | tf_op jit(solution)/shard_map/reduce_scatter | solution.py:91
  422.3 55.7 %all-gather.38.cloned.1.call-done = bf16[2048,2048]{1,0:T(8,128)(2,1)} async-done(((bf16[256,2048]{1,0:T(8,128)(2,1)}), bf16[2048,2048]{1,0:T(8,128)(2,1)}) %all-gather.38.cloned.1.call-update) | async-done | bytes 8388624 | tf_op jit(solution)/shard_map/all_gather | solution.py:127
  485.3 48.9 %all-gather.36.cloned.1.call-done = bf16[2048,2048]{1,0:T(8,128)(2,1)} async-done(((bf16[256,2048]{1,0:T(8,128)(2,1)}), bf16[2048,2048]{1,0:T(8,128)(2,1)}) %all-gather.36.cloned.1.call-update) | async-done | bytes 8388624 | tf_op jit(solution)/shard_map/all_gather | solution.py:126
  541.3 22.9 %all-gather.66.cloned.1.call-done = bf16[1,256,2048]{2,1,0:T(8,128)(2,1)} async-done(((bf16[1,64,2048]{2,1,0:T(8,128)(2,1)}), bf16[1,256,2048]{2,1,0:T(8,128)(2,1)}) %all-gather.66.cloned.1.call-update) | async-done | bytes 1048592 | tf_op jit(solution)/shard_map/all_gather | solution.py:87
  564.2 57.2 %all-gather.40.cloned.1.call-done = bf16[2048,2048]{1,0:T(8,128)(2,1)} async-done(((bf16[2048,256]{1,0:T(8,128)(2,1)}), bf16[2048,2048]{1,0:T(8,128)(2,1)}) %all-gather.40.cloned.1.call-update) | async-done | bytes 8388624 | tf_op jit(solution)/shard_map/all_gather | solution.py:128
  702.9 23.4 %reduce-scatter.64.cloned.1.call-done = f32[64,2048]{1,0:T(8,128)} async-done(((f32[256,2048]{1,0:T(8,128)}), f32[64,2048]{1,0:T(8,128)}) %reduce-scatter.64.cloned.1.call-update) | async-done | bytes 524304 | tf_op jit(solution)/shard_map/reduce_scatter | solution.py:91
  726.4 46.2 %reduce-scatter.48.cloned.1.call-done = f32[64,2048]{1,0:T(8,128)} async-done(((f32[256,2048]{1,0:T(8,128)}), f32[64,2048]{1,0:T(8,128)}) %reduce-scatter.48.cloned.1.call-update) | async-done | bytes 524304 | tf_op jit(solution)/shard_map/reduce_scatter | solution.py:91
  778.0 25.0 %all-gather.52.cloned.1.call-done = bf16[256,2048]{1,0:T(8,128)(2,1)} async-done(((bf16[64,2048]{1,0:T(8,128)(2,1)}), bf16[256,2048]{1,0:T(8,128)(2,1)}) %all-gather.52.cloned.1.call-update) | async-done | bytes 1048592 | tf_op jit(solution)/shard_map/all_gather | solution.py:87
  936.7 46.2 %reduce-scatter.56.cloned.1.call-done = f32[64,2048]{1,0:T(8,128)} async-done(((f32[256,2048]{1,0:T(8,128)}), f32[64,2048]{1,0:T(8,128)}) %reduce-scatter.56.cloned.1.call-update) | async-done | bytes 524304 | tf_op jit(solution)/shard_map/reduce_scatter | solution.py:91
  986.1 42.8 %reduce-scatter.46.cloned.1.call-done = f32[64,2048]{1,0:T(8,128)} async-done(((f32[256,2048]{1,0:T(8,128)}), f32[64,2048]{1,0:T(8,128)}) %reduce-scatter.46.cloned.1.call-update) | async-done | bytes 524304 | tf_op jit(solution)/shard_map/reduce_scatter | solution.py:91
  1028.9 46.0 %reduce-scatter.38.cloned.1.call-done = f32[64,2048]{1,0:T(8,128)} async-done(((f32[256,2048]{1,0:T(8,128)}), f32[64,2048]{1,0:T(8,128)}) %reduce-scatter.38.cloned.1.call-update) | async-done | bytes 524304 | tf_op jit(solution)/shard_map/reduce_scatter | solution.py:91
  1137.3 27.5 %all-gather.58.cloned.1.call-done = bf16[256,2048]{1,0:T(8,128)(2,1)} async-done(((bf16[64,2048]{1,0:T(8,128)(2,1)}), bf16[256,2048]{1,0:T(8,128)(2,1)}) %all-gather.58.cloned.1.call-update) | async-done | bytes 1048592 | tf_op jit(solution)/shard_map/all_gather | solution.py:87
  1603.6 46.0 %reduce-scatter.70.cloned.1.call-done = f32[64,2048]{1,0:T(8,128)} async-done(((f32[256,2048]{1,0:T(8,128)}), f32[64,2048]{1,0:T(8,128)}) %reduce-scatter.70.cloned.1.call-update) | async-done | bytes 524304 | tf_op jit(solution)/shard_map/reduce_scatter | solution.py:91
  1649.6 46.0 %reduce-scatter.62.cloned.1.call-done = f32[64,2048]{1,0:T(8,128)} async-done(((f32[256,2048]{1,0:T(8,128)}), f32[64,2048]{1,0:T(8,128)}) %reduce-scatter.62.cloned.1.call-update) | async-done | bytes 524304 | tf_op jit(solution)/shard_map/reduce_scatter | solution.py:91
  1695.5 46.0 %reduce-scatter.54.cloned.1.call-done = f32[64,2048]{1,0:T(8,128)} async-done(((f32[256,2048]{1,0:T(8,128)}), f32[64,2048]{1,0:T(8,128)}) %reduce-scatter.54.cloned.1.call-update) | async-done | bytes 524304 | tf_op jit(solution)/shard_map/reduce_scatter | solution.py:91
  1743.9 43.7 %all-reduce = (f32[2048]{0:T(1024)S(1)}, f32[64]{0:T(128)}, f32[64]{0:T(128)}, f32[2048]{0:T(1024)S(1)}) all-reduce(f32[2048]{0:T(1024)S(1)} %add_add_fusion.1, f32[64]{0:T(128)S(1)} %add_add_fusion.3, f32[64]{0:T(128)S(1)} %add_add_fusion.2, f32[2048]{0:T(1024)S(1)} %add_add_fusion), channel_id=1, replica_groups=mesh['dp'=2,'ctx'=4,'tp'=4] {'dp','ctx','tp'}, use_global_device_ids=true, to_apply=%region_72.73 | all-reduce | flops 4224 | bytes 33792 | tf_op jit(solution)/shard_map/psum | solution.py:354
  1791.7 41.6 %reduce-scatter.42.cloned.1.call-done = f32[64,2048]{1,0:T(8,128)} async-done(((f32[256,2048]{1,0:T(8,128)}), f32[64,2048]{1,0:T(8,128)}) %reduce-scatter.42.cloned.1.call-update) | async-done | bytes 524304 | tf_op jit(solution)/shard_map/reduce_scatter | solution.py:91
  1839.8 67.6 %reduce-scatter.92.cloned.1.call-done = bf16[2048,256]{1,0:T(8,128)(2,1)} async-done(((bf16[2048,2048]{1,0:T(8,128)(2,1)}), bf16[2048,256]{1,0:T(8,128)(2,1)}) %reduce-scatter.92.cloned.1.call-update) | async-done | bytes 1048592 | tf_op jit(solution)/shard_map/reduce_scatter | solution.py:384
  1910.2 72.3 %reduce-scatter.90.cloned.1.call-done = bf16[256,2048]{1,0:T(8,128)(2,1)} async-done(((bf16[2048,2048]{1,0:T(8,128)(2,1)}), bf16[256,2048]{1,0:T(8,128)(2,1)}) %reduce-scatter.90.cloned.1.call-update) | async-done | bytes 1048592 | tf_op jit(solution)/shard_map/reduce_scatter | solution.py:381
  1985.3 72.0 %reduce-scatter.88.cloned.1.call-done = bf16[256,2048]{1,0:T(8,128)(2,1)} async-done(((bf16[2048,2048]{1,0:T(8,128)(2,1)}), bf16[256,2048]{1,0:T(8,128)(2,1)}) %reduce-scatter.88.cloned.1.call-update) | async-done | bytes 1048592 | tf_op jit(solution)/shard_map/reduce_scatter | solution.py:378
  (980 shorter events, 996.2 us)
Async XLA Ops:
  25.5 179.2 %all-gather.32.cloned.1.call-start = ((), (), s32[]{:S(2)}) async-start(), calls=%async_computation.33 | async-start | bytes 2359296 | tf_op jit(solution)/shard_map/all_gather | solution.py:124
  26.1 258.5 %reduce-scatter.44.cloned.1.call-start = ((), (), s32[]{:S(2)}) async-start(), calls=%async_computation.49 | async-start | bytes 2621440 | tf_op jit(solution)/shard_map/reduce_scatter | solution.py:91
  396.2 168.0 %all-gather.66.cloned.1.call-start = ((), (), s32[]{:S(2)}) async-start(), calls=%async_computation.81 | async-start | bytes 1310720 | tf_op jit(solution)/shard_map/all_gather | solution.py:87
  398.4 223.0 %all-gather.40.cloned.1.call-start = ((), (), s32[]{:S(2)}) async-start(), calls=%async_computation.38 | async-start | bytes 9437184 | tf_op jit(solution)/shard_map/all_gather | solution.py:128
  399.0 252.4 %all-gather.34.cloned.1.call-start = ((), (), s32[]{:S(2)}) async-start(), calls=%async_computation.35 | async-start | bytes 1310720 | tf_op jit(solution)/shard_map/all_gather | solution.py:87
  399.6 280.7 %all-gather.62.cloned.1.call-start = ((), (), s32[]{:S(2)}) async-start(), calls=%async_computation.79 | async-start | bytes 1310720 | tf_op jit(solution)/shard_map/all_gather | solution.py:87
  400.2 326.2 %reduce-scatter.64.cloned.1.call-start = ((), (), s32[]{:S(2)}) async-start(), calls=%async_computation.62 | async-start | bytes 2621440 | tf_op jit(solution)/shard_map/reduce_scatter | solution.py:91
  777.8 159.0 %reduce-scatter.72.cloned.1.call-start = ((), (), s32[]{:S(2)}) async-start(), calls=%async_computation.67 | async-start | bytes 2621440 | tf_op jit(solution)/shard_map/reduce_scatter | solution.py:91
  920.5 154.4 %reduce-scatter.38.cloned.1.call-start = ((), (), s32[]{:S(2)}) async-start(), calls=%async_computation.43 | async-start | bytes 2621440 | tf_op jit(solution)/shard_map/reduce_scatter | solution.py:91
  928.1 177.6 %all-gather.56.cloned.1.call-start = ((), (), s32[]{:S(2)}) async-start(), calls=%async_computation.58 | async-start | bytes 1310720 | tf_op jit(solution)/shard_map/all_gather | solution.py:87
  1085.2 200.4 %reduce-scatter.58.cloned.1.call-start = ((), (), s32[]{:S(2)}) async-start(), calls=%async_computation.59 | async-start | bytes 655360 | tf_op jit(solution)/shard_map/reduce_scatter | solution.py:313
  1277.0 313.5 %reduce-scatter.84.cloned.1.call-start = ((), (), s32[]{:S(2)}) async-start(), calls=%async_computation.74 | async-start | bytes 589824 | tf_op jit(solution)/shard_map/reduce_scatter | solution.py:372
  1371.0 221.0 %reduce-scatter.82.cloned.1.call-start = ((), (), s32[]{:S(2)}) async-start(), calls=%async_computation.73 | async-start | bytes 589824 | tf_op jit(solution)/shard_map/reduce_scatter | solution.py:369
  1405.9 187.8 %reduce-scatter.86.cloned.1.call-start = ((), (), s32[]{:S(2)}) async-start(), calls=%async_computation.75 | async-start | bytes 2359296 | tf_op jit(solution)/shard_map/reduce_scatter | solution.py:375
  1414.9 180.5 %reduce-scatter.80.cloned.1.call-start = ((), (), s32[]{:S(2)}) async-start(), calls=%async_computation.72 | async-start | bytes 2359296 | tf_op jit(solution)/shard_map/reduce_scatter | solution.py:366
  1448.4 155.2 %reduce-scatter.78.cloned.1.call-start = ((), (), s32[]{:S(2)}) async-start(), calls=%async_computation.71 | async-start | bytes 2621440 | tf_op jit(solution)/shard_map/reduce_scatter | solution.py:91
  1452.9 196.7 %reduce-scatter.70.cloned.1.call-start = ((), (), s32[]{:S(2)}) async-start(), calls=%async_computation.66 | async-start | bytes 2621440 | tf_op jit(solution)/shard_map/reduce_scatter | solution.py:91
  1457.0 238.6 %reduce-scatter.62.cloned.1.call-start = ((), (), s32[]{:S(2)}) async-start(), calls=%async_computation.61 | async-start | bytes 2621440 | tf_op jit(solution)/shard_map/reduce_scatter | solution.py:91
  1461.1 280.5 %reduce-scatter.54.cloned.1.call-start = ((), (), s32[]{:S(2)}) async-start(), calls=%async_computation.56 | async-start | bytes 2621440 | tf_op jit(solution)/shard_map/reduce_scatter | solution.py:91
  1465.1 323.9 %reduce-scatter.34.cloned.1.call-start = ((), (), s32[]{:S(2)}) async-start(), calls=%async_computation.39 | async-start | bytes 2621440 | tf_op jit(solution)/shard_map/reduce_scatter | solution.py:91
  1472.6 360.7 %reduce-scatter.42.cloned.1.call-start = ((), (), s32[]{:S(2)}) async-start(), calls=%async_computation.47 | async-start | bytes 2621440 | tf_op jit(solution)/shard_map/reduce_scatter | solution.py:91
  1479.9 427.6 %reduce-scatter.92.cloned.1.call-start = ((), (), s32[]{:S(2)}) async-start(), calls=%async_computation.78 | async-start | bytes 9437184 | tf_op jit(solution)/shard_map/reduce_scatter | solution.py:384
  1515.6 466.9 %reduce-scatter.90.cloned.1.call-start = ((), (), s32[]{:S(2)}) async-start(), calls=%async_computation.77 | async-start | bytes 9437184 | tf_op jit(solution)/shard_map/reduce_scatter | solution.py:381
  1553.1 504.2 %reduce-scatter.88.cloned.1.call-start = ((), (), s32[]{:S(2)}) async-start(), calls=%async_computation.76 | async-start | bytes 9437184 | tf_op jit(solution)/shard_map/reduce_scatter | solution.py:378
  (300 other events, 15703.4 us)
Sparse Core Ops, SparseCore 0:
  209.2 43.8 reduce-scatter.43
  256.1 43.1 reduce-scatter.39
  302.2 43.1 reduce-scatter.35
  348.2 43.1 reduce-scatter.31
  424.0 53.8 all-gather.37
  479.8 54.3 all-gather.35
  565.9 55.4 all-gather.39
  683.0 43.3 reduce-scatter.63
  729.3 43.1 reduce-scatter.47
  893.4 43.3 reduce-scatter.71
  939.7 43.1 reduce-scatter.55
  985.7 43.1 reduce-scatter.45
  1031.7 43.1 reduce-scatter.37
  1470.9 41.2 reduce-scatter.85
  1515.6 41.2 reduce-scatter.79
  1559.7 43.8 reduce-scatter.77
  1606.4 43.1 reduce-scatter.69
  1652.3 43.1 reduce-scatter.61
  1698.4 43.1 reduce-scatter.53
  1743.7 44.1 reduce-scatter.33
  1790.2 43.1 reduce-scatter.41
  1836.8 70.6 reduce-scatter.91
  1911.2 71.2 reduce-scatter.89
  1985.9 71.2 reduce-scatter.87
  (28 shorter events, 736.3 us)
where the time goes:
time: 2080 us; the launch traced here: 2070 us
  waiting for transfers between devices  1290 us (62%)
  matrix products  445 us (21%)
  blocking collectives  129 us (6%)
  other arithmetic  113 us (5%)
  local copies, waits for them, and re-layouts  62.4 us (3%)
    reduce_scatter x16, waiting for transfers between devices, fold_rows(): lax.psum_scatter(row_fn(jnp.int32(0), lax.axis_size('tp') * own_rows), 't...  506 us
    all_gather x16, waiting for transfers between devices, spread_rows(): return lax.all_gather(values, 'tp', axis=0, tiled=True)  299 us
    dot_general x28, matrix products, matmul_tn(): lax.dot_general(left_mat, right_mat, (((0,), (0,)), ((), ())), preferred_...  141 us
    dot_general x28, matrix products, matmul(): return jnp.dot(left_mat, right_mat, preferred_element_type=jnp.float32)  119 us
    dot_general x28, matrix products, matmul_nt(): lax.dot_general(left_mat, right_mat, (((1,), (1,)), ((), ())), preferred_...  110 us
    reduce_scatter x1, waiting for transfers between devices, per_device(): lax.psum_scatter(up_grad.astype(jnp.bfloat16), ('dp', 'ctx'), scatter_dim...  72.3 us
    reduce_scatter x1, waiting for transfers between devices, per_device(): lax.psum_scatter(gate_grad.astype(jnp.bfloat16), ('dp', 'ctx'), scatter_d...  72 us
    reduce_scatter x1, waiting for transfers between devices, per_device(): lax.psum_scatter(down_grad.astype(jnp.bfloat16), ('dp', 'ctx'), scatter_d...  67.6 us
  transfers between devices with their start and end apart: 52, of which 42 were waited for; matrix products, arithmetic and copies ran while one was open for 28% of the time, Pallas kernels for 0%

commit v1 on v0

v1 whole, which is shorter than its diff:
```python
import math

import jax
import jax.numpy as jnp
from jax import lax
from jax.sharding import PartitionSpec as P

D = 2048
HD = 64


NORM_EPS = 1e-05
ROPE_BASE = 1000000.0
MASKED = -1e30


def matmul(left_mat, right_mat):
    return jnp.dot(left_mat, right_mat, preferred_element_type=jnp.float32)


def matmul_tn(left_mat, right_mat):
    return lax.dot_general(
        left_mat, right_mat, (((0,), (0,)), ((), ())), preferred_element_type=jnp.float32
    )


def matmul_nt(left_mat, right_mat):
    return lax.dot_general(
        left_mat, right_mat, (((1,), (1,)), ((), ())), preferred_element_type=jnp.float32
    )


def norm_forward(values, gain_vec):
    scale_rows = lax.rsqrt(jnp.mean(values * values, axis=-1, keepdims=True) + NORM_EPS)
    unit_rows = values * scale_rows
    return (unit_rows * gain_vec, unit_rows, scale_rows)


def norm_backward(grad_rows, unit_rows, scale_rows, gain_vec):
    scaled = grad_rows * gain_vec
    return scale_rows * (scaled - unit_rows * jnp.mean(scaled * unit_rows, axis=-1, keepdims=True))


def rope_tables(position, head_width):
    half_width = head_width // 2
    frequency = ROPE_BASE ** (-2.0 * jnp.arange(half_width, dtype=jnp.float32) / head_width)
    angles = position.astype(jnp.float32)[:, None, None] * frequency[None, None, :]
    return (jnp.cos(angles), jnp.sin(angles))


def rotate(values, cos_table, sin_table):
    half_width = values.shape[-1] // 2
    former = values[..., :half_width]
    latter = values[..., half_width:]
    return jnp.concatenate(
        [former * cos_table - latter * sin_table, latter * cos_table + former * sin_table], axis=-1
    )


def rotate_back(grad_rows, cos_table, sin_table):
    half_width = grad_rows.shape[-1] // 2
    former = grad_rows[..., :half_width]
    latter = grad_rows[..., half_width:]
    return jnp.concatenate(
        [former * cos_table + latter * sin_table, latter * cos_table - former * sin_table], axis=-1
    )


def ring_hop(values):
    count = lax.axis_size("tp")
    return lax.ppermute(values, "tp", [(i, (i + 1) % count) for i in range(count)])


def ring_gather(own):
    chunks = [own]
    for _ in range(lax.axis_size("tp") - 1):
        chunks.append(ring_hop(chunks[-1]))
    return chunks


def ring_sum(term):
    count = lax.axis_size("tp")
    total = term(1).astype(jnp.bfloat16)
    for place in range(2, count):
        total = (ring_hop(total).astype(jnp.float32) + term(place)).astype(jnp.bfloat16)
    return ring_hop(total).astype(jnp.float32) + term(0)


def ctx_swap(values, mask):
    count = lax.axis_size("ctx")
    return lax.ppermute(values, "ctx", [(i, i ^ mask) for i in range(count)])


def ctx_masks():
    masks = [0]
    bit = lax.axis_size("ctx") // 2
    while bit:
        masks = masks + [mask ^ bit for mask in masks]
        bit //= 2
    return masks


def ctx_gather(own):
    blocks = [own]
    bit = lax.axis_size("ctx") // 2
    while bit:
        blocks = blocks + [ctx_swap(block, bit) for block in blocks]
        bit //= 2
    return blocks


def ctx_sum(blocks):
    bit = 1
    while len(blocks) > 1:
        half = len(blocks) // 2
        blocks = [
            blocks[i] + ctx_swap(blocks[half + i].astype(jnp.bfloat16), bit).astype(jnp.float32)
            for i in range(half)
        ]
        bit *= 2
    return blocks[0]


def gather_weight(shard):
    return lax.all_gather(shard, ("dp", "ctx"), axis=0, tiled=True)


def scatter_grad(grad):
    return lax.psum_scatter(
        grad.astype(jnp.bfloat16), ("dp", "ctx"), scatter_dimension=0, tiled=True
    ).astype(jnp.float32)


def per_device(
    block_in,
    segments,
    positions,
    attention_gain,
    query_weight,
    key_weight,
    value_weight,
    query_gain,
    key_gain,
    output_weight,
    hidden_gain,
    gate_weight,
    up_weight,
    down_weight,
    cotangent,
):
    tp_count = lax.axis_size("tp")
    tp_index = lax.axis_index("tp")
    ctx_index = lax.axis_index("ctx")
    batch, own_rows, width = block_in.shape
    rows = batch * own_rows
    ctx_rows = own_rows * tp_count
    places = range(tp_count)
    q_cols = query_weight.shape[1]
    k_cols = key_weight.shape[1]
    q_heads = q_cols // HD
    k_heads = k_cols // HD
    group = q_heads // k_heads
    query_gain_f = query_gain.astype(jnp.float32)
    key_gain_f = key_gain.astype(jnp.float32)
    inv_root = 1.0 / math.sqrt(HD)

    gains = lax.all_gather(
        jnp.stack([attention_gain, hidden_gain]), ("dp", "ctx"), axis=1, tiled=True
    ).astype(jnp.float32)
    gain_attention, gain_hidden = gains[0], gains[1]
    full_qkv = gather_weight(jnp.concatenate([query_weight, key_weight, value_weight], axis=1))
    full_out_t = gather_weight(output_weight.T)
    full_gate = gather_weight(gate_weight)
    full_up = gather_weight(up_weight)
    full_down_t = gather_weight(down_weight.T)

    def chunk_start(place):
        owner = lax.rem(tp_index - place + tp_count, tp_count)
        return owner * own_rows

    def own_part(table, start):
        return lax.dynamic_slice_in_dim(table, start, own_rows, 1)

    tokens = block_in.reshape(rows, width).astype(jnp.float32)
    normed, unit_attention, scale_attention = norm_forward(tokens, gain_attention)
    normed_rows = ring_gather(normed.astype(jnp.bfloat16))

    query_rot, key_value, saved = [], [], []
    for place in places:
        raw = matmul(normed_rows[place], full_qkv)
        position = own_part(positions, ctx_index * ctx_rows + chunk_start(place)).reshape(-1)
        cos_table, sin_table = rope_tables(position, HD)
        query_raw = raw[:, :q_cols].reshape(rows, q_heads, HD)
        key_raw = raw[:, q_cols : q_cols + k_cols].reshape(rows, k_heads, HD)
        query_normed, query_unit, query_scale = norm_forward(query_raw, query_gain_f)
        key_normed, key_unit, key_scale = norm_forward(key_raw, key_gain_f)
        query_rot.append(rotate(query_normed, cos_table, sin_table).astype(jnp.bfloat16))
        key_rot = rotate(key_normed, cos_table, sin_table).astype(jnp.bfloat16)
        value_low = raw[:, q_cols + k_cols :].astype(jnp.bfloat16)
        key_value.append(jnp.stack([key_rot.reshape(rows, k_cols), value_low]))
        saved.append((query_unit, query_scale, key_unit, key_scale, cos_table, sin_table))

    blocks = ctx_gather(jnp.stack(key_value))
    masks = ctx_masks()
    kv = jnp.stack(blocks).reshape(len(masks), tp_count, 2, batch, own_rows, k_heads, HD)
    kv = kv.transpose(2, 3, 5, 0, 1, 4, 6).reshape(2, batch, k_heads, -1, HD)
    key_heads, value_heads = kv[0], kv[1]

    def to_heads(chunks):
        stacked = jnp.stack(chunks).reshape(tp_count, batch, own_rows, k_heads, group, HD)
        return stacked.transpose(1, 3, 4, 0, 2, 5).reshape(batch, k_heads, -1, HD)

    def from_heads(heads):
        split = heads.reshape(batch, k_heads, group, tp_count, own_rows, HD)
        split = split.transpose(3, 0, 4, 1, 2, 5).reshape(tp_count, rows, q_cols)
        return [split[place] for place in places]

    query_heads = to_heads([q.reshape(rows, q_cols) for q in query_rot])
    place_q, segment_q, place_k, segment_k = [], [], [], []
    iota = jnp.arange(own_rows, dtype=jnp.int32)
    for place in places:
        start = ctx_index * ctx_rows + chunk_start(place)
        place_q.append(start + iota)
        segment_q.append(own_part(segments, start))
    for mask in masks:
        for place in places:
            start = jnp.bitwise_xor(ctx_index, mask) * ctx_rows + chunk_start(place)
            place_k.append(start + iota)
            segment_k.append(own_part(segments, start))
    place_q = jnp.concatenate(place_q)
    place_k = jnp.concatenate(place_k)
    segment_q = jnp.concatenate(segment_q, axis=1)
    segment_k = jnp.concatenate(segment_k, axis=1)
    allowed = (segment_q[:, :, None] == segment_k[:, None, :]) & (
        place_q[:, None] >= place_k[None, :]
    )

    def score():
        scores = (
            jnp.einsum("bnqd,bnkd->bnqk", query_heads, key_heads, preferred_element_type=jnp.float32)
            * inv_root
        )
        scores = scores.reshape(batch, k_heads, group, ctx_rows, -1)
        return jnp.where(allowed[:, None, None], scores, MASKED)

    scores = score()
    row_top = jnp.max(scores, axis=-1, keepdims=True)
    exp_scores = jnp.exp(scores - row_top)
    row_total = jnp.sum(exp_scores, axis=-1, keepdims=True)
    probability = exp_scores / row_total
    prob_low = probability.astype(jnp.bfloat16).reshape(batch, k_heads, group * ctx_rows, -1)
    attended = jnp.einsum(
        "bnqk,bnkd->bnqd", prob_low, value_heads, preferred_element_type=jnp.float32
    )
    attended_rows = from_heads(attended.astype(jnp.bfloat16))

    mixed_in = ring_sum(lambda place: matmul_nt(attended_rows[place], full_out_t))
    hidden = tokens + mixed_in
    hidden_normed, unit_hidden, scale_hidden = norm_forward(hidden, gain_hidden)
    hidden_rows = ring_gather(hidden_normed.astype(jnp.bfloat16))
    grad_own = cotangent.reshape(rows, width)
    grad_rows = ring_gather(grad_own)

    activation, grad_gate_low, grad_up_low = [], [], []
    for place in places:
        gate_proj = matmul(hidden_rows[place], full_gate)
        up_proj = matmul(hidden_rows[place], full_up)
        sigmoid_gate = jax.nn.sigmoid(gate_proj)
        silu_gate = gate_proj * sigmoid_gate
        activation.append((silu_gate * up_proj).astype(jnp.bfloat16))
        grad_act = matmul(grad_rows[place], full_down_t)
        grad_gate_low.append(
            (
                grad_act * up_proj * sigmoid_gate * (1.0 + gate_proj * (1.0 - sigmoid_gate))
            ).astype(jnp.bfloat16)
        )
        grad_up_low.append((grad_act * silu_gate).astype(jnp.bfloat16))

    grad_hidden_normed = ring_sum(
        lambda place: matmul_nt(grad_gate_low[place], full_gate)
        + matmul_nt(grad_up_low[place], full_up)
    )
    feed_out = ring_sum(lambda place: matmul_nt(activation[place], full_down_t))
    block_out = (hidden + feed_out).astype(jnp.bfloat16).reshape(block_in.shape)

    all_grad = jnp.concatenate(grad_rows)
    all_hidden = jnp.concatenate(hidden_rows)
    down_grad = scatter_grad(matmul_tn(all_grad, jnp.concatenate(activation))).T
    gate_grad = scatter_grad(matmul_tn(all_hidden, jnp.concatenate(grad_gate_low)))
    up_grad = scatter_grad(matmul_tn(all_hidden, jnp.concatenate(grad_up_low)))

    hidden_gain_sum = jnp.sum(grad_hidden_normed * unit_hidden, axis=0)
    grad_hidden = grad_own.astype(jnp.float32) + norm_backward(
        grad_hidden_normed, unit_hidden, scale_hidden, gain_hidden
    )
    branch_rows = ring_gather(grad_hidden.astype(jnp.bfloat16))
    grad_att = to_heads([matmul(branch, full_out_t).astype(jnp.bfloat16) for branch in branch_rows])
    output_grad = scatter_grad(
        matmul_tn(jnp.concatenate(branch_rows), jnp.concatenate(attended_rows))
    ).T

    grad_prob = jnp.einsum(
        "bnqd,bnkd->bnqk", grad_att, value_heads, preferred_element_type=jnp.float32
    ).reshape(probability.shape)
    row_delta = jnp.sum(probability * grad_prob, axis=-1, keepdims=True)
    grad_scores = (
        (probability * (grad_prob - row_delta))
        .astype(jnp.bfloat16)
        .reshape(batch, k_heads, group * ctx_rows, -1)
    )
    grad_query = from_heads(
        jnp.einsum("bnqk,bnkd->bnqd", grad_scores, key_heads, preferred_element_type=jnp.float32)
        * inv_root
    )
    grad_key = (
        jnp.einsum("bnqk,bnqd->bnkd", grad_scores, query_heads, preferred_element_type=jnp.float32)
        * inv_root
    )
    grad_value = jnp.einsum(
        "bnqk,bnqd->bnkd", prob_low, grad_att, preferred_element_type=jnp.float32
    )
    grad_kv = jnp.stack([grad_key, grad_value]).reshape(
        2, batch, k_heads, len(masks), tp_count, own_rows, HD
    )
    grad_kv = grad_kv.transpose(3, 4, 0, 1, 5, 2, 6).reshape(len(masks), tp_count, 2, rows, k_cols)
    own_kv = ctx_sum([grad_kv[i] for i in range(len(masks))])

    query_gain_sum = jnp.zeros((HD,), jnp.float32)
    key_gain_sum = jnp.zeros((HD,), jnp.float32)
    grad_qkv = []
    for place in places:
        query_unit, query_scale, key_unit, key_scale, cos_table, sin_table = saved[place]
        grad_query_rot = rotate_back(grad_query[place].reshape(rows, -1, HD), cos_table, sin_table)
        query_gain_sum = query_gain_sum + jnp.sum(grad_query_rot * query_unit, axis=(0, 1))
        grad_key_rot = rotate_back(own_kv[place, 0].reshape(rows, -1, HD), cos_table, sin_table)
        key_gain_sum = key_gain_sum + jnp.sum(grad_key_rot * key_unit, axis=(0, 1))
        grad_query_raw = norm_backward(grad_query_rot, query_unit, query_scale, query_gain_f)
        grad_key_raw = norm_backward(grad_key_rot, key_unit, key_scale, key_gain_f)
        grad_qkv.append(
            jnp.concatenate(
                [
                    grad_query_raw.reshape(rows, -1).astype(jnp.bfloat16),
                    grad_key_raw.reshape(rows, -1).astype(jnp.bfloat16),
                    own_kv[place, 1].astype(jnp.bfloat16),
                ],
                axis=1,
            )
        )
    grad_normed = ring_sum(lambda place: matmul_nt(grad_qkv[place], full_qkv))
    qkv_grad = scatter_grad(matmul_tn(jnp.concatenate(normed_rows), jnp.concatenate(grad_qkv)))
    attention_gain_sum = jnp.sum(grad_normed * unit_attention, axis=0)
    input_grad = grad_hidden + norm_backward(
        grad_normed, unit_attention, scale_attention, gain_attention
    )

    gain_totals = lax.psum(
        (attention_gain_sum, hidden_gain_sum, query_gain_sum, key_gain_sum), ("dp", "ctx", "tp")
    )
    shard_width = attention_gain.shape[0]
    shard_start = (lax.axis_index("dp") * lax.axis_size("ctx") + ctx_index) * shard_width
    return (
        block_out,
        input_grad.reshape(block_in.shape),
        lax.dynamic_slice_in_dim(gain_totals[0], shard_start, shard_width, 0),
        qkv_grad[:, :q_cols],
        qkv_grad[:, q_cols : q_cols + k_cols],
        qkv_grad[:, q_cols + k_cols :],
        gain_totals[2],
        gain_totals[3],
        output_grad,
        lax.dynamic_slice_in_dim(gain_totals[1], shard_start, shard_width, 0),
        gate_grad,
        up_grad,
        down_grad,
    )


def solution(mesh):
    in_specs = (
        P(None, ("dp", "ctx", "tp"), None),
        P(None, "dp"),
        P(None, "dp"),
        P(("dp", "ctx")),
        P(("dp", "ctx"), "tp"),
        P(("dp", "ctx"), "tp"),
        P(("dp", "ctx"), "tp"),
        P(),
        P(),
        P("tp", ("dp", "ctx")),
        P(("dp", "ctx")),
        P(("dp", "ctx"), "tp"),
        P(("dp", "ctx"), "tp"),
        P("tp", ("dp", "ctx")),
        P(None, ("dp", "ctx", "tp"), None),
    )
    out_specs = (
        P(None, ("dp", "ctx", "tp"), None),
        P(None, ("dp", "ctx", "tp"), None),
        P(("dp", "ctx")),
        P(("dp", "ctx"), "tp"),
        P(("dp", "ctx"), "tp"),
        P(("dp", "ctx"), "tp"),
        P(),
        P(),
        P("tp", ("dp", "ctx")),
        P(("dp", "ctx")),
        P(("dp", "ctx"), "tp"),
        P(("dp", "ctx"), "tp"),
        P("tp", ("dp", "ctx")),
    )
    return jax.shard_map(
        per_device, mesh=mesh, in_specs=in_specs, out_specs=out_specs, check_vma=False
    )
```

time: 2080 us -> 1260 us (0.61)
  waiting for transfers between devices: 1290 us -> 497 us
  local copies, waits for them, and re-layouts: 62.4 us -> 217 us
  matrix products: 445 us -> 315 us
  blocking collectives: 129 us -> 49 us
  other arithmetic: 113 us -> 143 us
    reduce_scatter x31 -> x5, waiting for transfers between devices: 810 us -> 82.2 us  [scatter_grad(): lax.psum_scatter(grad.astype(jnp.bfloat16), ('dp', 'ctx'), scatter_dimens...]
    all_gather x21 -> x5, waiting for transfers between devices: 475 us -> 0.05 us  [gather_weight(): return lax.all_gather(shard, ('dp', 'ctx'), axis=0, tiled=True)]
    ppermute x0 -> x30, waiting for transfers between devices: none -> 412 us  [the longest x24 398 us: ring_hop(): lax.ppermute(values, 'tp', [(i, (i + 1) % count) for i in range(count)])]
    dot_general x28 -> x5, matrix products: 141 us -> 54.5 us  [matmul_tn(): lax.dot_general(left_mat, right_mat, (((0,), (0,)), ((), ())), preferred_...]
    all_gather x12 -> x1, blocking collectives: 85.7 us -> 10.3 us  [per_device(): lax.all_gather(jnp.stack([attention_gain, hidden_gain]), ('dp', 'ctx'), a...]
    another operation x0 -> x25, local copies, waits for them, and re-layouts: none -> 49.9 us  [the longest x4 26 us: per_device(): jnp.stack([grad_key, grad_value])]
    slice x3 -> x42, local copies, waits for them, and re-layouts: 2.19 us -> 51.3 us  [the longest x6 17.3 us: from_heads(): return [split[place] for place in places]]
    transpose x0 -> x6, other arithmetic: none -> 33.2 us  [the longest x2 11.1 us: to_heads(): return stacked.transpose(1, 3, 4, 0, 2, 5).reshape(batch, k_heads, -1, HD)]
  transfers between devices with their start and end apart: 52 -> 40, of which waited for: 42 -> 24; matrix products, arithmetic and copies ran while one was open for 28% -> 40% of each run, Pallas kernels for 0% -> 0%
where the time goes in v1:
time: 1260 us
  waiting for transfers between devices  497 us (39%)
  matrix products  315 us (25%)
  local copies, waits for them, and re-layouts  217 us (17%)
  other arithmetic  143 us (11%)
  blocking collectives  49 us (4%)
  starting transfers between devices  19.8 us (2%)
  between operations  17.3 us (1%)
    ppermute x24, waiting for transfers between devices, ring_hop(): lax.ppermute(values, 'tp', [(i, (i + 1) % count) for i in range(count)])  398 us
    dot_general x20, matrix products, matmul(): return jnp.dot(left_mat, right_mat, preferred_element_type=jnp.float32)  95.5 us
    reduce_scatter x5, waiting for transfers between devices, scatter_grad(): lax.psum_scatter(grad.astype(jnp.bfloat16), ('dp', 'ctx'), scatter_dimens...  82.2 us
    dot_general x20, matrix products, matmul_nt(): lax.dot_general(left_mat, right_mat, (((1,), (1,)), ((), ())), preferred_...  79.6 us
    dot_general x5, matrix products, matmul_tn(): lax.dot_general(left_mat, right_mat, (((0,), (0,)), ((), ())), preferred_...  54.5 us
    psum x1, blocking collectives, per_device(): lax.psum((attention_gain_sum, hidden_gain_sum, query_gain_sum, key_gain_s...  38.7 us
    convert_element_type x1, other arithmetic, per_device(): grad_scores = (probability * (grad_prob - row_delta)).astype(jnp.bfloat16...  27.5 us
    another operation x4, local copies, waits for them, and re-layouts, per_device(): jnp.stack([grad_key, grad_value])  26 us
  transfers between devices with their start and end apart: 40, of which 24 were waited for; matrix products, arithmetic and copies ran while one was open for 40% of the time, Pallas kernels for 0%

profile of v1, /device:TPU:0, one launch (start us, length us, event | category | flops | bytes accessed | tf_op | source)
XLA Modules:
  0.0 1258.0 jit_solution(4866170057670419688)
XLA Ops:
  24.8 25.7 %collective-permute-done = bf16[256,2048]{1,0:T(8,128)(2,1)} collective-permute-done((bf16[256,2048]{1,0:T(8,128)(2,1)S(1)}, bf16[256,2048]{1,0:T(8,128)(2,1)}, u32[]{:S(2)}, u32[]{:S(2)}) %collective-permute-start) | collective-permute-done | bytes 1048608 | tf_op jit(solution)/shard_map/ppermute | solution.py:71
  50.8 26.5 %collective-permute-done.1 = bf16[256,2048]{1,0:T(8,128)(2,1)} collective-permute-done((bf16[256,2048]{1,0:T(8,128)(2,1)}, bf16[256,2048]{1,0:T(8,128)(2,1)}, u32[]{:S(2)}, u32[]{:S(2)}) %collective-permute-start.1) | collective-permute-done | bytes 1048608 | tf_op jit(solution)/shard_map/ppermute | solution.py:71
  213.9 18.8 %fusion.163 = (f32[4,2,1024]{2,1,0:T(2,128)S(1)}, f32[4,2,1024,1024]{2,3,1,0:T(8,128)}) fusion(pred[4,1024,1024]{1,2,0:T(8,128)(4,1)} %broadcast_in_dim.13, bf16[4,2,1024,64]{2,3,1,0:T(8,128)(2,1)} %reshape.803, bf16[4,2,1024,64]{2,3,1,0:T(8,128)(2,1)} %squeeze.30), kind=kOutput, calls=%fused_computation.391 | convolution fusion | flops 1107297280 | bytes 39878656 | tf_op jit(solution)/shard_map/sub | solution.py:248
  261.3 26.1 %collective-permute-done.6 = bf16[256,2048]{1,0:T(8,128)(2,1)} collective-permute-done((bf16[256,2048]{1,0:T(8,128)(2,1)}, bf16[256,2048]{1,0:T(8,128)(2,1)}, u32[]{:S(2)}, u32[]{:S(2)}) %collective-permute-start.6) | collective-permute-done | bytes 1048608 | tf_op jit(solution)/shard_map/ppermute | solution.py:71
  294.1 22.9 %collective-permute-done.7 = bf16[256,2048]{1,0:T(8,128)(2,1)} collective-permute-done((bf16[256,2048]{1,0:T(8,128)(2,1)}, bf16[256,2048]{1,0:T(8,128)(2,1)}, u32[]{:S(2)}, u32[]{:S(2)}) %collective-permute-start.7) | collective-permute-done | bytes 1048608 | tf_op jit(solution)/shard_map/ppermute | solution.py:71
  321.7 26.1 %collective-permute-done.8 = bf16[256,2048]{1,0:T(8,128)(2,1)} collective-permute-done((bf16[256,2048]{1,0:T(8,128)(2,1)}, bf16[256,2048]{1,0:T(8,128)(2,1)}, u32[]{:S(2)}, u32[]{:S(2)}) %collective-permute-start.8) | collective-permute-done | bytes 1048608 | tf_op jit(solution)/shard_map/ppermute | solution.py:71
  349.9 20.4 %collective-permute-done.15 = bf16[256,2048]{1,0:T(8,128)(2,1)} collective-permute-done((bf16[256,2048]{1,0:T(8,128)(2,1)}, bf16[256,2048]{1,0:T(8,128)(2,1)}, u32[]{:S(2)}, u32[]{:S(2)}) %collective-permute-start.15) | collective-permute-done | bytes 1048608 | tf_op jit(solution)/shard_map/ppermute | solution.py:71
  370.3 22.4 %collective-permute-done.9 = bf16[256,2048]{1,0:T(8,128)(2,1)S(1)} collective-permute-done((bf16[256,2048]{1,0:T(8,128)(2,1)S(1)}, bf16[256,2048]{1,0:T(8,128)(2,1)S(1)}, u32[]{:S(2)}, u32[]{:S(2)}) %collective-permute-start.9) | collective-permute-done | bytes 1048608 | tf_op jit(solution)/shard_map/ppermute | solution.py:71
  393.6 21.6 %collective-permute-done.17 = bf16[256,2048]{1,0:T(8,128)(2,1)} collective-permute-done((bf16[256,2048]{1,0:T(8,128)(2,1)}, bf16[256,2048]{1,0:T(8,128)(2,1)}, u32[]{:S(2)}, u32[]{:S(2)}) %collective-permute-start.17) | collective-permute-done | bytes 1048608 | tf_op jit(solution)/shard_map/ppermute | solution.py:71
  415.2 22.5 %collective-permute-done.11 = bf16[256,2048]{1,0:T(8,128)(2,1)} collective-permute-done((bf16[256,2048]{1,0:T(8,128)(2,1)S(1)}, bf16[256,2048]{1,0:T(8,128)(2,1)}, u32[]{:S(2)}, u32[]{:S(2)}) %collective-permute-start.11) | collective-permute-done | bytes 1048608 | tf_op jit(solution)/shard_map/ppermute | solution.py:71
  590.8 17.3 %collective-permute-done.12 = bf16[256,2048]{1,0:T(8,128)(2,1)S(1)} collective-permute-done((bf16[256,2048]{1,0:T(8,128)(2,1)S(1)}, bf16[256,2048]{1,0:T(8,128)(2,1)S(1)}, u32[]{:S(2)}, u32[]{:S(2)}) %collective-permute-start.12) | collective-permute-done | bytes 1048608 | tf_op jit(solution)/shard_map/ppermute | solution.py:71
  611.1 19.5 %collective-permute-done.20 = bf16[256,2048]{1,0:T(8,128)(2,1)S(1)} collective-permute-done((bf16[256,2048]{1,0:T(8,128)(2,1)S(1)}, bf16[256,2048]{1,0:T(8,128)(2,1)S(1)}, u32[]{:S(2)}, u32[]{:S(2)}) %collective-permute-start.20) | collective-permute-done | bytes 1048608 | tf_op jit(solution)/shard_map/ppermute | solution.py:71
  654.2 21.1 %collective-permute-done.21 = bf16[256,2048]{1,0:T(8,128)(2,1)S(1)} collective-permute-done((bf16[256,2048]{1,0:T(8,128)(2,1)S(1)}, bf16[256,2048]{1,0:T(8,128)(2,1)S(1)}, u32[]{:S(2)}, u32[]{:S(2)}) %collective-permute-start.21) | collective-permute-done | bytes 1048608 | tf_op jit(solution)/shard_map/ppermute | solution.py:71
  675.4 23.0 %collective-permute-done.22 = bf16[256,2048]{1,0:T(8,128)(2,1)} collective-permute-done((bf16[256,2048]{1,0:T(8,128)(2,1)S(1)}, bf16[256,2048]{1,0:T(8,128)(2,1)}, u32[]{:S(2)}, u32[]{:S(2)}) %collective-permute-start.22) | collective-permute-done | bytes 1048608 | tf_op jit(solution)/shard_map/ppermute | solution.py:71
  733.7 21.9 %multiply_reduce_fusion = (f32[4,2,1024]{2,1,0:T(2,128)S(1)}, f32[4,2,1024,1024]{2,3,1,0:T(8,128)}) fusion(f32[4,2,1024,1024]{2,3,1,0:T(8,128)} %get-tuple-element.206, f32[4,2,1024]{2,1,0:T(2,128)S(1)} %copy-done.117, bf16[4,2,1024,64]{2,3,1,0:T(8,128)(2,1)S(1)} %reshape.811, bf16[4,2,1024,64]{2,3,1,0:T(8,128)(2,1)S(1)} %copy-done.48), kind=kOutput, calls=%fused_computation.2 | convolution fusion | flops 1098899456 | bytes 69271552 | tf_op jit(solution)/shard_map/bnqd,bnkd->bnqk/dot_general | solution.py:302
  755.5 27.5 %multiply_convert_fusion = bf16[4,2,1024,1024]{2,3,1,0:T(8,128)(2,1)} fusion(f32[4,2,1024,1024]{2,3,1,0:T(8,128)} %get-tuple-element.209, f32[4,2,1024]{2,1,0:T(2,128)S(1)} %get-tuple-element.208, f32[4,2,1024,1024]{2,3,1,0:T(8,128)} %get-tuple-element.206, f32[4,2,1024]{2,1,0:T(2,128)S(1)} %copy-done.117), kind=kLoop, calls=%fused_computation.1 | loop fusion | flops 33554432 | bytes 83951616 | tf_op jit(solution)/shard_map/convert_element_type | solution.py:308
  801.7 15.0 %fusion.5 = f32[4,2,1024,64]{2,3,1,0:T(8,128)} fusion(bf16[4,2,1024,64]{2,3,1,0:T(8,128)(2,1)} %copy-done.51, f32[4,2,1024,1024]{2,3,1,0:T(8,128)} %get-tuple-element.206, f32[4,2,1024]{2,1,0:T(2,128)S(1)} %copy-done.117), kind=kOutput, calls=%fused_computation.11 | convolution fusion | flops 1090519040 | bytes 36732928 | tf_op jit(solution)/shard_map/bnqk,bnqd->bnkd/dot_general | solution.py:319
  979.7 14.4 %convolution_convert_fusion = bf16[2048,2048]{1,0:T(8,128)(2,1)} fusion(bf16[256,2048]{1,0:T(8,128)(2,1)} %collective-permute-done.19, bf16[256,2048]{1,0:T(8,128)(2,1)} %collective-permute-done.17, bf16[256,2048]{1,0:T(8,128)(2,1)} %collective-permute-done.15, bf16[256,2048]{1,0:T(8,128)(2,1)} %bitcast.33, bf16[256,2048]{1,0:T(8,128)(2,1)S(1)} %copy-done.165, ...), kind=kOutput, calls=%fused_computation.15 | convolution fusion | flops 8627683328 | bytes 16777216 | tf_op jit(solution)/shard_map/dot_general | solution.py:22
  1009.0 13.7 %convolution_convert_fusion.2 = bf16[2048,2048]{1,0:T(8,128)(2,1)} fusion(bf16[256,2048]{1,0:T(8,128)(2,1)} %get-tuple-element.89, bf16[256,2048]{1,0:T(8,128)(2,1)} %copy-done.163, bf16[256,2048]{1,0:T(8,128)(2,1)} %copy-done.161, bf16[256,2048]{1,0:T(8,128)(2,1)} %get-tuple-element.92, bf16[256,2048]{1,0:T(8,128)(2,1)} %collective-permute-done.13, ...), kind=kOutput, calls=%fused_computation.17 | convolution fusion | flops 8627683328 | bytes 16777216 | tf_op jit(solution)/shard_map/dot_general | solution.py:22
  1026.9 26.1 %collective-permute-done.27 = bf16[256,2048]{1,0:T(8,128)(2,1)S(1)} collective-permute-done((bf16[256,2048]{1,0:T(8,128)(2,1)S(1)}, bf16[256,2048]{1,0:T(8,128)(2,1)S(1)}, u32[]{:S(2)}, u32[]{:S(2)}) %collective-permute-start.27) | collective-permute-done | bytes 1048608 | tf_op jit(solution)/shard_map/ppermute | solution.py:71
  1054.2 25.2 %collective-permute-done.28 = bf16[256,2048]{1,0:T(8,128)(2,1)S(1)} collective-permute-done((bf16[256,2048]{1,0:T(8,128)(2,1)S(1)}, bf16[256,2048]{1,0:T(8,128)(2,1)S(1)}, u32[]{:S(2)}, u32[]{:S(2)}) %collective-permute-start.28) | collective-permute-done | bytes 1048608 | tf_op jit(solution)/shard_map/ppermute | solution.py:71
  1084.8 21.1 %collective-permute-done.29 = bf16[256,2048]{1,0:T(8,128)(2,1)} collective-permute-done((bf16[256,2048]{1,0:T(8,128)(2,1)}, bf16[256,2048]{1,0:T(8,128)(2,1)}, u32[]{:S(2)}, u32[]{:S(2)}) %collective-permute-start.29) | collective-permute-done | bytes 1048608 | tf_op jit(solution)/shard_map/ppermute | solution.py:71
  1111.9 38.7 %all-reduce = (f32[2048]{0:T(1024)S(1)}, f32[64]{0:T(128)}, f32[64]{0:T(128)}, f32[2048]{0:T(1024)S(1)}) all-reduce(f32[2048]{0:T(1024)} %get-tuple-element.54, f32[64]{0:T(128)S(1)} %add_add_fusion.1, f32[64]{0:T(128)} %add_add_fusion, f32[2048]{0:T(1024)} %get-tuple-element.52), channel_id=1, replica_groups=mesh['dp'=2,'ctx'=4,'tp'=4] {'dp','ctx','tp'}, use_global_device_ids=true, to_apply=%region_24.25 | all-reduce | flops 4224 | bytes 33792 | tf_op jit(solution)/shard_map/psum | solution.py:356
  1176.3 71.8 %reduce-scatter.10.cloned.1.call-done = bf16[256,2048]{1,0:T(8,128)(2,1)} async-done(((bf16[2048,2048]{1,0:T(8,128)(2,1)}), bf16[256,2048]{1,0:T(8,128)(2,1)}) %reduce-scatter.10.cloned.1.call-update) | async-done | bytes 1048592 | tf_op jit(solution)/shard_map/reduce_scatter | solution.py:129
  (759 shorter events, 651.8 us)
Async XLA Ops:
  7.2 95.9 %all-gather.6.cloned.1.call-start = ((), (), s32[]{:S(2)}) async-start(), calls=%async_computation.5 | async-start | bytes 3538944 | tf_op jit(solution)/shard_map/all_gather | solution.py:125
  9.2 247.3 %all-gather.8.cloned.1.call-start = ((), (), s32[]{:S(2)}) async-start(), calls=%async_computation.6 | async-start | bytes 2359296 | tf_op jit(solution)/shard_map/all_gather | solution.py:125
  9.9 428.2 %all-gather.10.cloned.1.call-start = ((), (), s32[]{:S(2)}) async-start(), calls=%async_computation.7 | async-start | bytes 9437184 | tf_op jit(solution)/shard_map/all_gather | solution.py:125
  10.7 434.9 %all-gather.12.cloned.1.call-start = ((), (), s32[]{:S(2)}) async-start(), calls=%async_computation.8 | async-start | bytes 9437184 | tf_op jit(solution)/shard_map/all_gather | solution.py:125
  11.3 441.6 %all-gather.14.cloned.1.call-start = ((), (), s32[]{:S(2)}) async-start(), calls=%async_computation.9 | async-start | bytes 9437184 | tf_op jit(solution)/shard_map/all_gather | solution.py:125
  24.7 1058.0 %reduce-scatter.8.cloned.1.call-start = ((), (), s32[]{:S(2)}) async-start(), calls=%async_computation.11 | async-start | bytes 2359296 | tf_op jit(solution)/shard_map/reduce_scatter | solution.py:129
  132.8 44.8 %collective-permute-start.4 = (bf16[4,2,256,128]{3,2,1,0:T(8,128)(2,1)}, bf16[4,2,256,128]{3,2,1,0:T(8,128)(2,1)}, u32[]{:S(2)}, u32[]{:S(2)}) collective-permute-start(bf16[4,2,256,128]{3,2,1,0:T(8,128)(2,1)} %pad_maximum_fusion.3), channel_id=1, source_target_pairs={{0,4},{4,0},{8,12},{12,8},{1,5},{5,1},{9,13},{13,9},{2,6},{6,2},{1... | collective-permute-start | bytes 1572872 | tf_op jit(solution)/shard_map/ppermute | solution.py:91
  143.1 37.0 %collective-permute-start.5 = (bf16[4,2,256,128]{3,2,1,0:T(8,128)(2,1)}, bf16[4,2,256,128]{3,2,1,0:T(8,128)(2,1)}, u32[]{:S(2)}, u32[]{:S(2)}) collective-permute-start(bf16[4,2,256,128]{3,2,1,0:T(8,128)(2,1)} %collective-permute-done.3), channel_id=1, source_target_pairs={{0,4},{4,0},{8,12},{12,8},{1,5},{5,1},{9,13},{13,9},{2,6},{6,2},{1... | collective-permute-start | bytes 1572872 | tf_op jit(solution)/shard_map/ppermute | solution.py:91
  319.6 28.2 %collective-permute-start.8 = (bf16[256,2048]{1,0:T(8,128)(2,1)}, bf16[256,2048]{1,0:T(8,128)(2,1)}, u32[]{:S(2)}, u32[]{:S(2)}) collective-permute-start(bf16[256,2048]{1,0:T(8,128)(2,1)} %add_convert_fusion.7), channel_id=1, source_target_pairs={{0,1},{1,2},{2,3},{3,0},{4,5},{5,6},{6,7},{7,4},{8,9},{9,10},{10,1... | collective-permute-start | bytes 3145736 | tf_op jit(solution)/shard_map/ppermute | solution.py:71
  319.6 50.7 %collective-permute-start.15 = (bf16[256,2048]{1,0:T(8,128)(2,1)}, bf16[256,2048]{1,0:T(8,128)(2,1)}, u32[]{:S(2)}, u32[]{:S(2)}) collective-permute-start(bf16[256,2048]{1,0:T(8,128)(2,1)} %bitcast.33), channel_id=1, source_target_pairs={{0,1},{1,2},{2,3},{3,0},{4,5},{5,6},{6,7},{7,4},{8,9},{9,10},{10,1... | collective-permute-start | bytes 3145736 | tf_op jit(solution)/shard_map/ppermute | solution.py:71
  349.8 42.8 %collective-permute-start.9 = (bf16[256,2048]{1,0:T(8,128)(2,1)S(1)}, bf16[256,2048]{1,0:T(8,128)(2,1)S(1)}, u32[]{:S(2)}, u32[]{:S(2)}) collective-permute-start(bf16[256,2048]{1,0:T(8,128)(2,1)S(1)} %multiply_convert_fusion.13), channel_id=1, source_target_pairs={{0,1},{1,2},{2,3},{3,0},{4,5},{5,6},{6,7},{7,4},{8,9},{9,10},{10,1... | collective-permute-start | bytes 3145736 | tf_op jit(solution)/shard_map/ppermute | solution.py:71
  370.3 44.9 %collective-permute-start.17 = (bf16[256,2048]{1,0:T(8,128)(2,1)}, bf16[256,2048]{1,0:T(8,128)(2,1)}, u32[]{:S(2)}, u32[]{:S(2)}) collective-permute-start(bf16[256,2048]{1,0:T(8,128)(2,1)} %collective-permute-done.15), channel_id=1, source_target_pairs={{0,1},{1,2},{2,3},{3,0},{4,5},{5,6},{6,7},{7,4},{8,9},{9,10},{10,1... | collective-permute-start | bytes 3145736 | tf_op jit(solution)/shard_map/ppermute | solution.py:71
  393.6 44.1 %collective-permute-start.11 = (bf16[256,2048]{1,0:T(8,128)(2,1)S(1)}, bf16[256,2048]{1,0:T(8,128)(2,1)}, u32[]{:S(2)}, u32[]{:S(2)}) collective-permute-start(bf16[256,2048]{1,0:T(8,128)(2,1)S(1)} %collective-permute-done.9), channel_id=1, source_target_pairs={{0,1},{1,2},{2,3},{3,0},{4,5},{5,6},{6,7},{7,4},{8,9},{9,10},{10,1... | collective-permute-start | bytes 3145736 | tf_op jit(solution)/shard_map/ppermute | solution.py:71
  415.2 89.9 %collective-permute-start.19 = (bf16[256,2048]{1,0:T(8,128)(2,1)}, bf16[256,2048]{1,0:T(8,128)(2,1)}, u32[]{:S(2)}, u32[]{:S(2)}) collective-permute-start(bf16[256,2048]{1,0:T(8,128)(2,1)} %collective-permute-done.17), channel_id=1, source_target_pairs={{0,1},{1,2},{2,3},{3,0},{4,5},{5,6},{6,7},{7,4},{8,9},{9,10},{10,1... | collective-permute-start | bytes 3145736 | tf_op jit(solution)/shard_map/ppermute | solution.py:71
  437.7 60.3 %collective-permute-start.13 = (bf16[256,2048]{1,0:T(8,128)(2,1)}, bf16[256,2048]{1,0:T(8,128)(2,1)}, u32[]{:S(2)}, u32[]{:S(2)}) collective-permute-start(bf16[256,2048]{1,0:T(8,128)(2,1)} %collective-permute-done.11), channel_id=1, source_target_pairs={{0,1},{1,2},{2,3},{3,0},{4,5},{5,6},{6,7},{7,4},{8,9},{9,10},{10,1... | collective-permute-start | bytes 3145736 | tf_op jit(solution)/shard_map/ppermute | solution.py:71
  468.0 101.2 %collective-permute-start.10 = (bf16[256,2048]{1,0:T(8,128)(2,1)S(1)}, bf16[256,2048]{1,0:T(8,128)(2,1)S(1)}, u32[]{:S(2)}, u32[]{:S(2)}) collective-permute-start(bf16[256,2048]{1,0:T(8,128)(2,1)S(1)} %convolution_convert_fusion.5), channel_id=1, source_target_pairs={{0,1},{1,2},{2,3},{3,0},{4,5},{5,6},{6,7},{7,4},{8,9},{9,10},{10,1... | collective-permute-start | bytes 3145736 | tf_op jit(solution)/shard_map/ppermute | solution.py:71
  476.3 78.8 %collective-permute-start.16 = (bf16[256,2048]{1,0:T(8,128)(2,1)S(1)}, bf16[256,2048]{1,0:T(8,128)(2,1)S(1)}, u32[]{:S(2)}, u32[]{:S(2)}) collective-permute-start(bf16[256,2048]{1,0:T(8,128)(2,1)S(1)} %fusion.61), channel_id=1, source_target_pairs={{0,1},{1,2},{2,3},{3,0},{4,5},{5,6},{6,7},{7,4},{8,9},{9,10},{10,1... | collective-permute-start | bytes 3145736 | tf_op jit(solution)/shard_map/ppermute | solution.py:71
  575.1 33.0 %collective-permute-start.12 = (bf16[256,2048]{1,0:T(8,128)(2,1)S(1)}, bf16[256,2048]{1,0:T(8,128)(2,1)S(1)}, u32[]{:S(2)}, u32[]{:S(2)}) collective-permute-start(bf16[256,2048]{1,0:T(8,128)(2,1)S(1)} %add_convert_fusion.6), channel_id=1, source_target_pairs={{0,1},{1,2},{2,3},{3,0},{4,5},{5,6},{6,7},{7,4},{8,9},{9,10},{10,1... | collective-permute-start | bytes 3145736 | tf_op jit(solution)/shard_map/ppermute | solution.py:71
  585.9 44.6 %collective-permute-start.20 = (bf16[256,2048]{1,0:T(8,128)(2,1)S(1)}, bf16[256,2048]{1,0:T(8,128)(2,1)S(1)}, u32[]{:S(2)}, u32[]{:S(2)}) collective-permute-start(bf16[256,2048]{1,0:T(8,128)(2,1)S(1)} %add_convert_fusion.2), channel_id=1, source_target_pairs={{0,1},{1,2},{2,3},{3,0},{4,5},{5,6},{6,7},{7,4},{8,9},{9,10},{10,1... | collective-permute-start | bytes 3145736 | tf_op jit(solution)/shard_map/ppermute | solution.py:71
  608.4 38.3 %collective-permute-start.14 = (bf16[256,2048]{1,0:T(8,128)(2,1)S(1)}, bf16[256,2048]{1,0:T(8,128)(2,1)S(1)}, u32[]{:S(2)}, u32[]{:S(2)}) collective-permute-start(bf16[256,2048]{1,0:T(8,128)(2,1)S(1)} %add_convert_fusion.5), channel_id=1, source_target_pairs={{0,1},{1,2},{2,3},{3,0},{4,5},{5,6},{6,7},{7,4},{8,9},{9,10},{10,1... | collective-permute-start | bytes 3145736 | tf_op jit(solution)/shard_map/ppermute | solution.py:71
  868.2 288.3 %reduce-scatter.6.cloned.1.call-start = ((), (), s32[]{:S(2)}) async-start(), calls=%async_computation.10 | async-start | bytes 3538944 | tf_op jit(solution)/shard_map/reduce_scatter | solution.py:129
  978.5 181.4 %reduce-scatter.14.cloned.1.call-start = ((), (), s32[]{:S(2)}) async-start(), calls=%async_computation.14 | async-start | bytes 9437184 | tf_op jit(solution)/shard_map/reduce_scatter | solution.py:129
  994.0 179.5 %reduce-scatter.12.cloned.1.call-start = ((), (), s32[]{:S(2)}) async-start(), calls=%async_computation.13 | async-start | bytes 9437184 | tf_op jit(solution)/shard_map/reduce_scatter | solution.py:129
  1009.0 239.2 %reduce-scatter.10.cloned.1.call-start = ((), (), s32[]{:S(2)}) async-start(), calls=%async_computation.12 | async-start | bytes 9437184 | tf_op jit(solution)/shard_map/reduce_scatter | solution.py:129
  (194 other events, 3699.9 us)
Sparse Core Ops, SparseCore 0:
  10.5 35.0 all-gather.5
  47.4 28.1 all-gather.7
  77.6 54.4 all-gather.9
  133.8 56.2 all-gather.11
  191.8 55.9 all-gather.13
  868.3 39.4 reduce-scatter.7
  978.6 44.2 reduce-scatter.5
  1026.3 71.3 reduce-scatter.13
  1101.6 71.9 reduce-scatter.11
  1176.9 71.2 reduce-scatter.9

commit v2 on v1

v2 whole, which is shorter than its diff:
```python
import functools
import math

import jax
import jax.numpy as jnp
from jax import lax
from jax.experimental import pallas as pl
from jax.experimental.pallas import tpu as pltpu
from jax.sharding import PartitionSpec as P

D = 2048
HD = 64


NORM_EPS = 1e-05
ROPE_BASE = 1000000.0
MASKED = -1e30


def matmul(left_mat, right_mat):
    return jnp.dot(left_mat, right_mat, preferred_element_type=jnp.float32)


def matmul_tn(left_mat, right_mat):
    return lax.dot_general(
        left_mat, right_mat, (((0,), (0,)), ((), ())), preferred_element_type=jnp.float32
    )


def matmul_nt(left_mat, right_mat):
    return lax.dot_general(
        left_mat, right_mat, (((1,), (1,)), ((), ())), preferred_element_type=jnp.float32
    )


def norm_forward(values, gain_vec):
    scale_rows = lax.rsqrt(jnp.mean(values * values, axis=-1, keepdims=True) + NORM_EPS)
    unit_rows = values * scale_rows
    return (unit_rows * gain_vec, unit_rows, scale_rows)


def norm_backward(grad_rows, unit_rows, scale_rows, gain_vec):
    scaled = grad_rows * gain_vec
    return scale_rows * (scaled - unit_rows * jnp.mean(scaled * unit_rows, axis=-1, keepdims=True))


def ring_hop(values):
    count = lax.axis_size("tp")
    return lax.ppermute(values, "tp", [(i, (i + 1) % count) for i in range(count)])


def ctx_swap(values, mask):
    count = lax.axis_size("ctx")
    return lax.ppermute(values, "ctx", [(i, i ^ mask) for i in range(count)])


def ctx_masks():
    masks = [0]
    bit = lax.axis_size("ctx") // 2
    while bit:
        masks = masks + [mask ^ bit for mask in masks]
        bit //= 2
    return masks


def ctx_gather(own):
    blocks = [own]
    bit = lax.axis_size("ctx") // 2
    while bit:
        blocks = blocks + [ctx_swap(block, bit) for block in blocks]
        bit //= 2
    return blocks


def gather_weight(shard):
    return lax.all_gather(shard, ("dp", "ctx"), axis=0, tiled=True)


def scatter_grad(grad):
    return lax.psum_scatter(
        grad.astype(jnp.bfloat16), ("dp", "ctx"), scatter_dimension=0, tiled=True
    ).astype(jnp.float32)


def all_sum(values, axes):
    for axis in axes:
        count = lax.axis_size(axis)
        bit = 1
        while bit < count:
            values = values + lax.ppermute(values, axis, [(i, i ^ bit) for i in range(count)])
            bit *= 2
    return values


def together(*values):
    return lax.optimization_barrier(values)


def lane_iota(shape):
    return lax.broadcasted_iota(jnp.int32, shape, 1)


def head_means(values):
    width = values.shape[1]
    row = lax.broadcasted_iota(jnp.int32, (width, width), 0) // HD
    col = lax.broadcasted_iota(jnp.int32, (width, width), 1) // HD
    pick = jnp.where(row == col, 1.0 / HD, 0.0).astype(jnp.float32)
    return jnp.dot(
        values, pick, precision=lax.Precision.HIGHEST, preferred_element_type=jnp.float32
    )


def half_swap(values):
    width, half = values.shape[1], HD // 2
    first = lax.rem(lane_iota(values.shape), HD) < half
    return jnp.where(
        first, pltpu.roll(values, width - half, 1), pltpu.roll(values, half, 1)
    )


def other_head(values):
    return pltpu.roll(values, HD, 1)


def twice(values, head):
    wide = values.astype(jnp.float32)
    low = lane_iota(wide.shape) < HD
    other = other_head(wide)
    both = jnp.where(low, wide, other) if head == 0 else jnp.where(low, other, wide)
    return both.astype(values.dtype)


def apart(values):
    wide = values.astype(jnp.float32)
    low = lane_iota(wide.shape) < HD
    zero = jnp.zeros_like(wide)
    return jnp.concatenate(
        [jnp.where(low, wide, zero), jnp.where(low, zero, wide)], axis=0
    ).astype(values.dtype)


def heads_kernel(raw_ref, cos_ref, sin_ref, q_gain_ref, k_gain_ref, q_ref, kv_ref):
    pair = 2 * HD
    q_cols = q_ref.shape[1]
    k_cols = kv_ref.shape[1] // 2
    cos, sin = cos_ref[...], sin_ref[...]
    for first in range(0, q_cols + k_cols, pair):
        values = raw_ref[:, first : first + pair]
        gain = q_gain_ref[...] if first < q_cols else k_gain_ref[...]
        normed = values * lax.rsqrt(head_means(values * values) + NORM_EPS) * gain
        turned = (normed * cos + half_swap(normed) * sin).astype(jnp.bfloat16)
        if first < q_cols:
            q_ref[:, first : first + pair] = turned
        else:
            kv_ref[:, first - q_cols : first - q_cols + pair] = turned
    kv_ref[:, k_cols:] = raw_ref[:, q_cols + k_cols :].astype(jnp.bfloat16)


def make_heads(raw, cos_wide, sin_wide, q_gain, k_gain, q_cols, k_cols):
    rows = raw.shape[0]
    return pl.pallas_call(
        heads_kernel,
        out_shape=(
            jax.ShapeDtypeStruct((rows, q_cols), jnp.bfloat16),
            jax.ShapeDtypeStruct((rows, 2 * k_cols), jnp.bfloat16),
        ),
        cost_estimate=pl.CostEstimate(
            flops=rows * raw.shape[1] * 400, bytes_accessed=rows * raw.shape[1] * 7, transcendentals=0
        ),
        name="make_heads",
    )(raw, cos_wide, sin_wide, q_gain, k_gain)


def turn_back(grad, values, gain, cos, sin):
    turned = grad * cos - half_swap(grad) * sin
    scale = lax.rsqrt(head_means(values * values) + NORM_EPS)
    unit = values * scale
    scaled = turned * gain
    return scale * (scaled - unit * head_means(scaled * unit)), turned * unit


def fill_bias(starts_ref, low_ref, high_ref, bias_ref, piece):
    low, high = low_ref[0], high_ref[0]
    for i in range(bias_ref.shape[0] // piece):
        place = starts_ref[i] + lax.broadcasted_iota(jnp.int32, (piece, low.shape[1]), 0)
        linked = (place >= low) & (place <= high)
        bias_ref[i * piece : (i + 1) * piece, :] = jnp.where(linked, 0.0, MASKED)


def attend_kernel(places, blocks, block_keys, skip, *refs):
    starts_ref, low_ref, high_ref = refs[:3]
    q_refs = refs[3 : 3 + places]
    kv_refs = refs[3 + places : 3 + places + blocks]
    refs = refs[3 + places + blocks + skip :]
    out_refs = refs[:places]
    total_ref, bias_ref, key_ref, value_ref = refs[places:]
    pair = 2 * HD
    piece, q_cols = q_refs[0].shape
    rows = places * piece
    k_cols = kv_refs[0].shape[2] // 2
    k_heads = k_cols // HD
    group = q_cols // k_cols
    scale = math.log2(math.e) / math.sqrt(HD)
    fill_bias(starts_ref, low_ref, high_ref, bias_ref, piece)
    for block in range(blocks):
        for head in range(k_heads):
            cols = slice(head // 2 * pair, head // 2 * pair + pair)
            vcols = slice(k_cols + head // 2 * pair, k_cols + head // 2 * pair + pair)
            where = slice(block * block_keys, (block + 1) * block_keys)
            keys = kv_refs[block][:, :, cols].reshape(block_keys, pair)
            key_ref[head, where, :] = twice(keys, head % 2)
            if head % 2 == 0:
                values = kv_refs[block][:, :, vcols].reshape(block_keys, pair)
                value_ref[head // 2, :, where] = values.astype(jnp.float32).T.astype(jnp.bfloat16)
    for first in range(0, q_cols, pair):
        head = first // HD // group
        queries = apart(jnp.concatenate([q_ref[:, first : first + pair] for q_ref in q_refs], axis=0))

        def step(block, carry):
            mixed, total = carry
            where = pl.ds(pl.multiple_of(block * block_keys, block_keys), block_keys)
            scores = matmul_nt(key_ref[head, where, :], queries)
            bias = bias_ref[where, :]
            weight = jnp.exp2(scores * scale + jnp.concatenate([bias, bias], axis=1))
            total = total + jnp.sum(weight, axis=0, keepdims=True)
            values = value_ref[head // 2, head % 2 * HD : (head % 2 + 1) * HD, where]
            return mixed + matmul(values, weight.astype(jnp.bfloat16)), total

        mixed, total = lax.fori_loop(
            0,
            blocks,
            step,
            (jnp.zeros((HD, 2 * rows), jnp.float32), jnp.zeros((1, 2 * rows), jnp.float32)),
        )
        mixed = mixed / total
        out = jnp.concatenate([mixed[:, :rows], mixed[:, rows:]], axis=0).T.astype(jnp.bfloat16)
        for place in range(places):
            out_refs[place][:, first : first + pair] = out[place * piece : (place + 1) * piece]
        total_ref[0, first // pair, :] = jnp.log2(total)[0]


def attend(starts, low, high, q_chunks, kv_blocks, batch, part, parts, before):
    places, blocks = len(q_chunks), len(kv_blocks)
    count = batch // parts
    base = part * count
    rows, q_cols = q_chunks[0].shape
    piece = rows // batch
    kv_cols = kv_blocks[0].shape[2]
    k_cols = kv_cols // 2
    keys = blocks * places * piece
    q_rows = places * piece
    pairs = q_cols // (2 * HD)
    q_spec = pl.BlockSpec((piece, q_cols), lambda b: (base + b, 0))
    kv_spec = pl.BlockSpec((places, piece, kv_cols), lambda b: (0, base + b, 0))
    line_spec = pl.BlockSpec((1, 1, q_rows), lambda b: (base + b, 0, 0))
    work = count * q_cols // HD * q_rows * keys
    results = pl.pallas_call(
        functools.partial(attend_kernel, places, blocks, places * piece, len(before)),
        grid=(count,),
        out_shape=tuple(
            [jax.ShapeDtypeStruct((rows, q_cols), jnp.bfloat16)] * places
            + [jax.ShapeDtypeStruct((batch, pairs, 2 * q_rows), jnp.float32)]
        ),
        in_specs=[
            pl.BlockSpec(memory_space=pltpu.SMEM),
            line_spec,
            pl.BlockSpec((1, 1, q_rows), lambda b: (0, 0, 0)),
        ]
        + [q_spec] * places
        + [kv_spec] * blocks
        + [pl.BlockSpec(memory_space=pl.ANY)] * len(before),
        out_specs=tuple(
            [q_spec] * places + [pl.BlockSpec((1, pairs, 2 * q_rows), lambda b: (base + b, 0, 0))]
        ),
        input_output_aliases={3 + places + blocks + i: i for i in range(len(before))},
        scratch_shapes=[
            pltpu.VMEM((keys, q_rows), jnp.float32),
            pltpu.VMEM((k_cols // HD, keys, 2 * HD), jnp.bfloat16),
            pltpu.VMEM((k_cols // HD // 2, 2 * HD, keys), jnp.bfloat16),
        ],
        cost_estimate=pl.CostEstimate(
            flops=work * 4 * HD * 4, bytes_accessed=count * q_rows * q_cols * 8, transcendentals=work
        ),
        name="attend",
    )(starts, low, high, *q_chunks, *kv_blocks, *before)
    return list(results)


def attend_back_kernel(places, blocks, block_keys, skip, *refs):
    starts_ref, low_ref, high_ref, total_ref, cos_ref, sin_ref, gain_ref = refs[:7]
    refs = refs[7:]
    q_refs, refs = refs[:places], refs[places:]
    raw_refs, refs = refs[:places], refs[places:]
    grad_refs, refs = refs[:places], refs[places:]
    kv_refs, refs = refs[:blocks], refs[blocks + skip :]
    dq_refs, refs = refs[:places], refs[places:]
    dkv_refs, refs = refs[:blocks], refs[blocks:]
    gain_sum_ref, bias_ref, key_ref, turned_ref, value_ref, prob_ref, dprob_ref, dkey_ref, dvalue_ref = refs
    pair = 2 * HD
    piece, q_cols = q_refs[0].shape
    rows = places * piece
    k_cols = kv_refs[0].shape[2] // 2
    k_heads = k_cols // HD
    group = q_cols // k_cols
    inv_root = 1.0 / math.sqrt(HD)
    scale = math.log2(math.e) * inv_root
    fill_bias(starts_ref, low_ref, high_ref, bias_ref, piece)

    @pl.when(pl.program_id(0) == 0)
    def _():
        gain_sum_ref[...] = jnp.zeros_like(gain_sum_ref)

    for block in range(blocks):
        for head in range(k_heads):
            cols = slice(head // 2 * pair, head // 2 * pair + pair)
            vcols = slice(k_cols + head // 2 * pair, k_cols + head // 2 * pair + pair)
            where = slice(block * block_keys, (block + 1) * block_keys)
            keys = kv_refs[block][:, :, cols].reshape(block_keys, pair)
            values = kv_refs[block][:, :, vcols].reshape(block_keys, pair)
            key_ref[head, where, :] = twice(keys, head % 2)
            value_ref[head, where, :] = twice(values, head % 2)
            if head % 2 == 0:
                turned_ref[head // 2, :, where] = keys.astype(jnp.float32).T.astype(jnp.bfloat16)
    for first in range(0, q_cols, pair):
        head = first // HD // group
        fresh = first % (group * HD) == 0
        queries = apart(jnp.concatenate([q_ref[:, first : first + pair] for q_ref in q_refs], axis=0))
        grads = apart(jnp.concatenate([g_ref[:, first : first + pair] for g_ref in grad_refs], axis=0))
        total = total_ref[0, first // pair : first // pair + 1, :]

        def look(block, delta):
            where = pl.ds(pl.multiple_of(block * block_keys, block_keys), block_keys)
            scores = matmul_nt(key_ref[head, where, :], queries)
            bias = bias_ref[where, :]
            prob = jnp.exp2(scores * scale + jnp.concatenate([bias, bias], axis=1) - total)
            dprob = matmul_nt(value_ref[head, where, :], grads)
            prob_ref[where, :] = prob
            dprob_ref[where, :] = dprob
            return delta + jnp.sum(prob * dprob, axis=0, keepdims=True)

        delta = lax.fori_loop(0, blocks, look, jnp.zeros((1, 2 * rows), jnp.float32))

        def step(block, dquery):
            where = pl.ds(pl.multiple_of(block * block_keys, block_keys), block_keys)
            prob = prob_ref[where, :]
            dscore = (prob * (dprob_ref[where, :] - delta)).astype(jnp.bfloat16)
            dvalue = matmul(prob.astype(jnp.bfloat16), grads)
            dkey = matmul(dscore, queries)
            if fresh:
                dvalue_ref[head, where, :] = dvalue
                dkey_ref[head, where, :] = dkey
            else:
                dvalue_ref[head, where, :] += dvalue
                dkey_ref[head, where, :] += dkey
            keys = turned_ref[head // 2, head % 2 * HD : (head % 2 + 1) * HD, where]
            return dquery + matmul(keys, dscore)

        dquery = lax.fori_loop(0, blocks, step, jnp.zeros((HD, 2 * rows), jnp.float32)) * inv_root
        dquery = jnp.concatenate([dquery[:, :rows], dquery[:, rows:]], axis=0).T
        raw = jnp.concatenate([raw_ref[:, first : first + pair] for raw_ref in raw_refs], axis=0)
        dq, addend = turn_back(
            dquery, raw, gain_ref[...], cos_ref[...].reshape(rows, pair), sin_ref[...].reshape(rows, pair)
        )
        gain_sum_ref[...] += jnp.sum(addend.reshape(-1, 8, pair), axis=0)
        for place in range(places):
            dq_refs[place][:, first : first + pair] = dq[place * piece : (place + 1) * piece].astype(
                jnp.bfloat16
            )
    low = lane_iota((block_keys, pair)) < HD
    for block in range(blocks):
        where = slice(block * block_keys, (block + 1) * block_keys)
        for first in range(0, k_heads, 2):
            for shift, ref, factor in ((0, dkey_ref, inv_root), (k_cols, dvalue_ref, 1.0)):
                one, two = ref[first, where, :], ref[first + 1, where, :]
                sums = jnp.where(low, one + other_head(one), two + other_head(two)) * factor
                cols = slice(shift + first // 2 * pair, shift + first // 2 * pair + pair)
                dkv_refs[block][:, :, cols] = sums.reshape(places, piece, pair).astype(
                    dkv_refs[block].dtype
                )


def attend_back(
    starts,
    low,
    high,
    totals,
    cos_wide,
    sin_wide,
    q_gain,
    q_chunks,
    raw_chunks,
    grad_chunks,
    kv_blocks,
    kinds,
    batch,
    part,
    parts,
    before,
):
    places, blocks = len(q_chunks), len(kv_blocks)
    count = batch // parts
    base = part * count
    rows, q_cols = q_chunks[0].shape
    piece = rows // batch
    kv_cols = kv_blocks[0].shape[2]
    k_cols = kv_cols // 2
    keys = blocks * places * piece
    q_rows = places * piece
    pairs = q_cols // (2 * HD)
    k_heads = k_cols // HD
    q_spec = pl.BlockSpec((piece, q_cols), lambda b: (base + b, 0))
    kv_spec = pl.BlockSpec((places, piece, kv_cols), lambda b: (0, base + b, 0))
    line_spec = pl.BlockSpec((1, 1, q_rows), lambda b: (base + b, 0, 0))
    turn_spec = pl.BlockSpec((places, piece, 2 * HD), lambda b: (0, base + b, 0))
    work = count * q_cols // HD * q_rows * keys
    results = pl.pallas_call(
        functools.partial(attend_back_kernel, places, blocks, places * piece, len(before)),
        grid=(count,),
        out_shape=tuple(
            [jax.ShapeDtypeStruct((rows, q_cols), jnp.bfloat16)] * places
            + [jax.ShapeDtypeStruct((places, rows, kv_cols), kind) for kind in kinds]
            + [jax.ShapeDtypeStruct((8, 2 * HD), jnp.float32)]
        ),
        in_specs=[
            pl.BlockSpec(memory_space=pltpu.SMEM),
            line_spec,
            pl.BlockSpec((1, 1, q_rows), lambda b: (0, 0, 0)),
            pl.BlockSpec((1, pairs, 2 * q_rows), lambda b: (base + b, 0, 0)),
            turn_spec,
            turn_spec,
            pl.BlockSpec((1, 2 * HD), lambda b: (0, 0)),
        ]
        + [q_spec] * (3 * places)
        + [kv_spec] * blocks
        + [pl.BlockSpec(memory_space=pl.ANY)] * len(before),
        out_specs=tuple(
            [q_spec] * places + [kv_spec] * blocks + [pl.BlockSpec((8, 2 * HD), lambda b: (0, 0))]
        ),
        input_output_aliases={7 + 3 * places + blocks + i: i for i in range(len(before))},
        scratch_shapes=[
            pltpu.VMEM((keys, q_rows), jnp.float32),
            pltpu.VMEM((k_heads, keys, 2 * HD), jnp.bfloat16),
            pltpu.VMEM((k_heads // 2, 2 * HD, keys), jnp.bfloat16),
            pltpu.VMEM((k_heads, keys, 2 * HD), jnp.bfloat16),
            pltpu.VMEM((keys, 2 * q_rows), jnp.float32),
            pltpu.VMEM((keys, 2 * q_rows), jnp.float32),
            pltpu.VMEM((k_heads, keys, 2 * HD), jnp.float32),
            pltpu.VMEM((k_heads, keys, 2 * HD), jnp.float32),
        ],
        cost_estimate=pl.CostEstimate(
            flops=work * 10 * HD * 4, bytes_accessed=count * q_rows * q_cols * 16, transcendentals=work
        ),
        name="attend_back",
    )(
        starts,
        low,
        high,
        totals,
        cos_wide,
        sin_wide,
        q_gain,
        *q_chunks,
        *raw_chunks,
        *grad_chunks,
        *kv_blocks,
        *before,
    )
    return list(results[:-1]), results[-1]


def keys_back_kernel(own_ref, came_ref, raw_ref, cos_ref, sin_ref, gain_ref, out_ref, gain_sum_ref):
    k_cols = own_ref.shape[2] // 2
    pair = 2 * HD
    addends = jnp.zeros((8, pair), jnp.float32)
    for first in range(0, k_cols, pair):
        cols = slice(first, first + pair)
        grad = own_ref[0, :, cols] + came_ref[0, :, cols].astype(jnp.float32)
        dk, addend = turn_back(grad, raw_ref[:, cols], gain_ref[...], cos_ref[0], sin_ref[0])
        out_ref[:, cols] = dk.astype(jnp.bfloat16)
        addends = addends + jnp.sum(addend.reshape(-1, 8, pair), axis=0)
    rest = slice(k_cols, 2 * k_cols)
    out_ref[:, rest] = (own_ref[0, :, rest] + came_ref[0, :, rest].astype(jnp.float32)).astype(
        jnp.bfloat16
    )
    gain_sum_ref[...] = addends


def keys_back(place, own, came, raw, cos_wide, sin_wide, k_gain, q_cols):
    _, rows, kv_cols = own.shape
    kv_spec = pl.BlockSpec((1, rows, kv_cols), lambda i: (place, 0, 0))
    turn_spec = pl.BlockSpec((1, rows, 2 * HD), lambda i: (place, 0, 0))
    k_cols = kv_cols // 2
    return pl.pallas_call(
        keys_back_kernel,
        grid=(1,),
        out_shape=(
            jax.ShapeDtypeStruct((rows, kv_cols), jnp.bfloat16),
            jax.ShapeDtypeStruct((8, 2 * HD), jnp.float32),
        ),
        in_specs=[
            kv_spec,
            kv_spec,
            pl.BlockSpec((rows, k_cols), lambda i: (0, q_cols // k_cols)),
            turn_spec,
            turn_spec,
            pl.BlockSpec((1, 2 * HD), lambda i: (0, 0)),
        ],
        out_specs=(
            pl.BlockSpec((rows, kv_cols), lambda i: (0, 0)),
            pl.BlockSpec((8, 2 * HD), lambda i: (0, 0)),
        ),
        cost_estimate=pl.CostEstimate(
            flops=rows * kv_cols * 400, bytes_accessed=rows * kv_cols * 10, transcendentals=0
        ),
        name="keys_back",
    )(own, came, raw, cos_wide, sin_wide, k_gain)


def per_device(
    block_in,
    segments,
    positions,
    attention_gain,
    query_weight,
    key_weight,
    value_weight,
    query_gain,
    key_gain,
    output_weight,
    hidden_gain,
    gate_weight,
    up_weight,
    down_weight,
    cotangent,
):
    tp_count = lax.axis_size("tp")
    tp_index = lax.axis_index("tp")
    ctx_index = lax.axis_index("ctx")
    batch, own_rows, width = block_in.shape
    rows = batch * own_rows
    ctx_rows = own_rows * tp_count
    places = range(tp_count)
    order = [*range(1, tp_count), 0]
    masks = ctx_masks()
    q_cols = query_weight.shape[1]
    k_cols = key_weight.shape[1]
    qkv_cols = q_cols + 2 * k_cols
    hidden_cols = gate_weight.shape[1]
    q_gain = jnp.tile(query_gain.astype(jnp.float32), 2)[None]
    k_gain = jnp.tile(key_gain.astype(jnp.float32), 2)[None]

    gains = lax.all_gather(
        jnp.stack([attention_gain, hidden_gain]), ("dp", "ctx"), axis=1, tiled=True
    ).astype(jnp.float32)
    gain_attention, gain_hidden = gains[0], gains[1]
    qkv_weight = jnp.concatenate([query_weight, key_weight, value_weight], axis=1)
    full_first = gather_weight(jnp.concatenate([qkv_weight, output_weight.T], axis=1))
    full_second = gather_weight(jnp.concatenate([gate_weight, up_weight, down_weight.T], axis=1))
    full_qkv, full_out_t = full_first[:, :qkv_cols], full_first[:, qkv_cols:]
    full_gate = full_second[:, :hidden_cols]
    full_up = full_second[:, hidden_cols : 2 * hidden_cols]
    full_down_t = full_second[:, 2 * hidden_cols :]

    def chunk_start(place):
        owner = lax.rem(tp_index - place + tp_count, tp_count)
        return owner * own_rows

    def own_part(table, start):
        return lax.dynamic_slice_in_dim(table, start, own_rows, 1)

    iota = jnp.arange(own_rows, dtype=jnp.int32)
    row_starts = [ctx_index * ctx_rows + chunk_start(place) for place in places]
    low = jnp.concatenate([own_part(segments, start) for start in row_starts], axis=1)[:, None]
    high = jnp.concatenate([start + iota for start in row_starts])[None, None]
    starts = jnp.stack(
        [
            jnp.bitwise_xor(ctx_index, mask) * ctx_rows + chunk_start(place)
            for mask in masks
            for place in places
        ]
    ).astype(jnp.int32)
    position = jnp.stack([own_part(positions, start).reshape(rows) for start in row_starts])
    half = HD // 2
    frequency = ROPE_BASE ** (-2.0 * jnp.arange(half, dtype=jnp.float32) / HD)
    sign = jnp.where(jnp.arange(2 * HD) % HD < half, -1.0, 1.0).astype(jnp.float32)
    angles = position.astype(jnp.float32)[..., None] * jnp.tile(frequency, 4)
    cos_wide, sin_wide = jnp.cos(angles), jnp.sin(angles) * sign

    def project(place):
        values = matmul(normed_rows[place], full_qkv)
        query_rot, kv = make_heads(
            values, cos_wide[place], sin_wide[place], q_gain, k_gain, q_cols, k_cols
        )
        return values, query_rot, kv

    tokens = block_in.reshape(rows, width).astype(jnp.float32)
    normed, unit_attention, scale_attention = norm_forward(tokens, gain_attention)
    normed_rows, heads = [normed.astype(jnp.bfloat16)], []
    for place in range(1, tp_count):
        came = ring_hop(normed_rows[-1])
        if place > 1:
            heads.append(project(place - 2))
            came, heads[-1] = together(came, heads[-1])
        normed_rows.append(came)

    grad_own, normed_rows[-1] = together(cotangent.reshape(rows, width), normed_rows[-1])
    came = ring_hop(grad_own)
    heads.append(project(tp_count - 2))
    heads.append(project(tp_count - 1))
    raw, queries, key_value = ([h[i] for h in heads] for i in range(3))
    blocks = ctx_gather(jnp.stack(key_value))
    came, blocks = together(came, blocks)
    grad_rows = [grad_own, came]
    attended = []
    parts = tp_count - 2
    for part in range(parts):
        came = ring_hop(grad_rows[-1])
        attended = attend(starts, low, high, queries, blocks, batch, part, parts, attended)
        came, attended = together(came, attended)
        grad_rows.append(came)
    attended_rows, totals = attended[:tp_count], attended[tp_count]

    def ring_sum(term, extra):
        total = term(order[0]).astype(jnp.bfloat16)
        done = []
        for step, place in enumerate(order[1:]):
            came = ring_hop(total)
            came, addend, work = together(came, term(place), extra(step, done))
            done.append(work)
            total = came.astype(jnp.float32) + addend
            if place:
                total = total.astype(jnp.bfloat16)
        return total, done

    grad_acts = {}

    def mixed_extra(step, done):
        last = step == tp_count - 2
        mine = order[step : step + 2] if last else order[step : step + 1]
        return [matmul(grad_rows[place], full_down_t) for place in mine]

    mixed_in, done = ring_sum(lambda place: matmul_nt(attended_rows[place], full_out_t), mixed_extra)
    for place, value in zip(order, [value for work in done for value in work]):
        grad_acts[place] = value
    hidden = tokens + mixed_in
    hidden_normed, unit_hidden, scale_hidden = norm_forward(hidden, gain_hidden)

    def feed(place):
        gate_proj = matmul(hidden_rows[place], full_gate)
        up_proj = matmul(hidden_rows[place], full_up)
        sigmoid_gate = jax.nn.sigmoid(gate_proj)
        silu_gate = gate_proj * sigmoid_gate
        grad_act = grad_acts[place]
        grad_gate = grad_act * up_proj * sigmoid_gate * (1.0 + gate_proj * (1.0 - sigmoid_gate))
        return (
            (silu_gate * up_proj).astype(jnp.bfloat16),
            grad_gate.astype(jnp.bfloat16),
            (grad_act * silu_gate).astype(jnp.bfloat16),
        )

    hidden_rows, fed = [hidden_normed.astype(jnp.bfloat16)], []
    for place in range(1, tp_count):
        came = ring_hop(hidden_rows[-1])
        fed.append(feed(place - 1))
        came, fed[-1] = together(came, fed[-1])
        hidden_rows.append(came)

    def hidden_term(place):
        return matmul_nt(fed[place][1], full_gate) + matmul_nt(fed[place][2], full_up)

    products = {}

    def hidden_sum():
        total = hidden_term(1).astype(jnp.bfloat16)
        came = ring_hop(total)
        last = feed(tp_count - 1)
        came, addend, last = together(came, hidden_term(2), last)
        fed.append(last)
        total = (came.astype(jnp.float32) + addend).astype(jnp.bfloat16)
        for place in order[2:]:
            came = ring_hop(total)
            if place:
                work = matmul_tn(
                    jnp.concatenate(grad_rows), jnp.concatenate([f[0] for f in fed])
                ).astype(jnp.bfloat16)
            else:
                pair = jnp.concatenate([jnp.concatenate([f[1], f[2]], axis=1) for f in fed])
                work = matmul_tn(jnp.concatenate(hidden_rows), pair).astype(jnp.bfloat16)
            came, addend, work = together(came, hidden_term(place), work)
            products[place] = work
            total = came.astype(jnp.float32) + addend
            if place:
                total = total.astype(jnp.bfloat16)
        return total

    grad_hidden_normed = hidden_sum()
    down_shard = lax.psum_scatter(products[3], ("dp", "ctx"), scatter_dimension=0, tiled=True)
    pair_shard = lax.psum_scatter(products[0], ("dp", "ctx"), scatter_dimension=0, tiled=True)

    grad_hidden = grad_own.astype(jnp.float32) + norm_backward(
        grad_hidden_normed, unit_hidden, scale_hidden, gain_hidden
    )
    branch_rows, grad_att = [grad_hidden.astype(jnp.bfloat16)], []
    for place in range(1, tp_count):
        came = ring_hop(branch_rows[-1])
        grad_att.append(matmul(branch_rows[-1], full_out_t).astype(jnp.bfloat16))
        came, grad_att[-1] = together(came, grad_att[-1])
        branch_rows.append(came)
    grad_att.append(matmul(branch_rows[-1], full_out_t).astype(jnp.bfloat16))
    down_shard, grad_att[-1] = together(down_shard, grad_att[-1])

    kinds = [jnp.float32] * (len(masks) // 2) + [jnp.bfloat16] * (len(masks) - len(masks) // 2)
    query_gain_sum = jnp.zeros((8, 2 * HD), jnp.float32)

    def feed_extra(step, done):
        nonlocal query_gain_sum
        if step < 2:
            back, addend = attend_back(
                starts,
                low,
                high,
                totals,
                cos_wide,
                sin_wide,
                q_gain,
                queries,
                raw,
                grad_att,
                blocks,
                kinds,
                batch,
                step,
                2,
                done[-1] if done else [],
            )
            query_gain_sum = query_gain_sum + addend
            return back
        nonlocal pair_shard
        pair_shard, done[-1] = together(pair_shard, done[-1])
        grad_blocks = done[-1][tp_count:]
        bit = 1
        while len(grad_blocks) > 2:
            half_count = len(grad_blocks) // 2
            grad_blocks = [
                grad_blocks[i]
                + ctx_swap(grad_blocks[half_count + i].astype(jnp.bfloat16), bit).astype(jnp.float32)
                for i in range(half_count)
            ]
            bit *= 2
        came = ctx_swap(grad_blocks[1].astype(jnp.bfloat16), bit)
        return [
            keys_back(place, grad_blocks[0], came, raw[place], cos_wide, sin_wide, k_gain, q_cols)
            for place in places
        ]

    activation_1, grad_att[0] = together(fed[1][0], grad_att[0])
    activation = [f[0] for f in fed]
    activation[1] = activation_1
    feed_out, done = ring_sum(lambda place: matmul_nt(activation[place], full_down_t), feed_extra)
    block_out = (hidden + feed_out).astype(jnp.bfloat16).reshape(block_in.shape)
    grad_query = done[1][:tp_count]
    grad_kv = [pair[0] for pair in done[2]]
    key_gain_sum = sum(pair[1] for pair in done[2])
    grad_qkv = [jnp.concatenate([grad_query[i], grad_kv[i]], axis=1) for i in places]

    def last_extra(step, done):
        if step:
            return []
        return [
            jnp.concatenate(
                [
                    matmul_tn(jnp.concatenate(normed_rows), jnp.concatenate(grad_qkv)),
                    matmul_tn(jnp.concatenate(branch_rows), jnp.concatenate(attended_rows)),
                ],
                axis=1,
            ).astype(jnp.bfloat16)
        ]

    grad_normed, done = ring_sum(lambda place: matmul_nt(grad_qkv[place], full_qkv), last_extra)
    last_shard = scatter_grad(done[0][0])
    input_grad = grad_hidden + norm_backward(
        grad_normed, unit_attention, scale_attention, gain_attention
    )
    down_grad = down_shard.astype(jnp.float32).T
    gate_grad = pair_shard[:, :hidden_cols].astype(jnp.float32)
    up_grad = pair_shard[:, hidden_cols:].astype(jnp.float32)
    qkv_grad = last_shard[:, :qkv_cols]
    output_grad = last_shard[:, qkv_cols:].T

    head_sums = jnp.stack([query_gain_sum, key_gain_sum]).sum(axis=1).reshape(2, 2, HD).sum(axis=1)
    head_sums = all_sum(head_sums, ("tp", "ctx", "dp"))
    attention_sum = jnp.sum(qkv_grad * qkv_weight.astype(jnp.float32), axis=1)
    hidden_sums = jnp.sum(
        gate_grad * gate_weight.astype(jnp.float32) + up_grad * up_weight.astype(jnp.float32), axis=1
    )
    attention_gain_grad = all_sum(attention_sum, ("tp",)) / attention_gain.astype(jnp.float32)
    hidden_gain_grad = all_sum(hidden_sums, ("tp",)) / hidden_gain.astype(jnp.float32)
    return (
        block_out,
        input_grad.reshape(block_in.shape),
        attention_gain_grad,
        qkv_grad[:, :q_cols],
        qkv_grad[:, q_cols : q_cols + k_cols],
        qkv_grad[:, q_cols + k_cols :],
        head_sums[0],
        head_sums[1],
        output_grad,
        hidden_gain_grad,
        gate_grad,
        up_grad,
        down_grad,
    )


def solution(mesh):
    in_specs = (
        P(None, ("dp", "ctx", "tp"), None),
        P(None, "dp"),
        P(None, "dp"),
        P(("dp", "ctx")),
        P(("dp", "ctx"), "tp"),
        P(("dp", "ctx"), "tp"),
        P(("dp", "ctx"), "tp"),
        P(),
        P(),
        P("tp", ("dp", "ctx")),
        P(("dp", "ctx")),
        P(("dp", "ctx"), "tp"),
        P(("dp", "ctx"), "tp"),
        P("tp", ("dp", "ctx")),
        P(None, ("dp", "ctx", "tp"), None),
    )
    out_specs = (
        P(None, ("dp", "ctx", "tp"), None),
        P(None, ("dp", "ctx", "tp"), None),
        P(("dp", "ctx")),
        P(("dp", "ctx"), "tp"),
        P(("dp", "ctx"), "tp"),
        P(("dp", "ctx"), "tp"),
        P(),
        P(),
        P("tp", ("dp", "ctx")),
        P(("dp", "ctx")),
        P(("dp", "ctx"), "tp"),
        P(("dp", "ctx"), "tp"),
        P("tp", ("dp", "ctx")),
    )
    return jax.shard_map(
        per_device, mesh=mesh, in_specs=in_specs, out_specs=out_specs, check_vma=False
    )
```

time: 1260 us -> 769 us (0.61)
  waiting for transfers between devices: 497 us -> 267 us
  local copies, waits for them, and re-layouts: 217 us -> 27.3 us
  Pallas kernels: 0 us -> 112 us
  other arithmetic: 143 us -> 57.4 us
  matrix products: 315 us -> 246 us
  blocking collectives: 49 us -> 10.4 us
    ppermute x24, waiting for transfers between devices: 398 us -> 214 us  [ring_hop(): lax.ppermute(values, 'tp', [(i, (i + 1) % count) for i in range(count)])]
    pallas_call x0 -> x12, Pallas kernels: none -> 112 us  [the longest x2 58.5 us: attend_back(): pl.pallas_call(functools.partial(attend_back_kernel, places, blocks, plac...]
    reduce_scatter x5 -> x1, waiting for transfers between devices: 82.2 us -> 0.01 us  [scatter_grad(): lax.psum_scatter(grad.astype(jnp.bfloat16), ('dp', 'ctx'), scatter_dimens...]
    dot_general x5 -> x0, matrix products: 66.4 us -> none  [the longest x1 21.9 us: per_device(): jnp.einsum('bnqd,bnkd->bnqk', grad_att, value_heads, preferred_element_ty...]
    another operation x23 -> x10, local copies, waits for them, and re-layouts: 49.9 us -> 2.3 us  [the longest x2 0.69 us: per_device(): k_gain = jnp.tile(key_gain.astype(jnp.float32), 2)[None]]
    slice x39 -> x0, local copies, waits for them, and re-layouts: 47.3 us -> none  [the longest x6 17.3 us: from_heads(): return [split[place] for place in places]]
    psum x1 -> x0, blocking collectives: 38.7 us -> none  [per_device(): lax.psum((attention_gain_sum, hidden_gain_sum, query_gain_sum, key_gain_s...]
    transpose x6 -> x1, other arithmetic: 33.2 us -> 1.54 us  [per_device(): down_grad = down_shard.astype(jnp.float32).T]
  transfers between devices with their start and end apart: 40 -> 44, of which waited for: 24 -> 26; matrix products, arithmetic and copies ran while one was open for 40% -> 40% of each run, Pallas kernels for 0% -> 15%
where the time goes in v2:
time: 769 us; the launch traced here: 763 us
  waiting for transfers between devices  267 us (35%)
  matrix products  246 us (32%)
  Pallas kernels  112 us (15%)
  other arithmetic  57.4 us (7%)
  local copies, waits for them, and re-layouts  27.3 us (4%)
  starting transfers between devices  26.6 us (3%)
  between operations  15.8 us (2%)
  blocking collectives  10.4 us (1%)
    ppermute x24, waiting for transfers between devices, ring_hop(): lax.ppermute(values, 'tp', [(i, (i + 1) % count) for i in range(count)])  214 us
    dot_general x20, matrix products, matmul_nt(): lax.dot_general(left_mat, right_mat, (((1,), (1,)), ((), ())), preferred_...  105 us
    dot_general x20, matrix products, matmul(): return jnp.dot(left_mat, right_mat, preferred_element_type=jnp.float32)  92.4 us
    pallas_call x2, Pallas kernels, attend_back(): pl.pallas_call(functools.partial(attend_back_kernel, places, blocks, plac...  58.5 us
    dot_general x4, matrix products, matmul_tn(): lax.dot_general(left_mat, right_mat, (((0,), (0,)), ((), ())), preferred_...  48.6 us
    ppermute x6, waiting for transfers between devices, ctx_swap(): return lax.ppermute(values, 'ctx', [(i, i ^ mask) for i in range(count)])  33.7 us
    pallas_call x2, Pallas kernels, attend(): pl.pallas_call(functools.partial(attend_kernel, places, blocks, places *...  32.5 us
    unnamed x231, local copies, waits for them, and re-layouts  20.4 us
  transfers between devices with their start and end apart: 44, of which 26 were waited for; matrix products, arithmetic and copies ran while one was open for 40% of the time, Pallas kernels for 15%

profile of v2, /device:TPU:0, one launch (start us, length us, event | category | flops | bytes accessed | tf_op | source)
XLA Modules:
  0.0 762.7 jit_solution(11170502694007784125)
XLA Ops:
  18.0 10.4 %all_gather.9 = bf16[2,2048]{1,0:T(2,128)(2,1)S(1)} all-gather(bf16[2,256]{1,0:T(2,128)(2,1)S(1)} %pad_maximum_fusion.4), channel_id=1, replica_groups=mesh['dp'=2,'ctx'=4,'tp'=4] {'dp','ctx'}, dimensions={1}, use_global_device_ids=true | all-gather | bytes 9216 | tf_op jit(solution)/shard_map/all_gather | solution.py:552
  32.2 23.9 %collective-permute-done = bf16[256,2048]{1,0:T(8,128)(2,1)} collective-permute-done((bf16[256,2048]{1,0:T(8,128)(2,1)S(1)}, bf16[256,2048]{1,0:T(8,128)(2,1)}, u32[]{:S(2)}, u32[]{:S(2)}) %collective-permute-start) | collective-permute-done | bytes 1048608 | tf_op jit(solution)/shard_map/ppermute | solution.py:49
  67.2 15.7 %collective-permute-done.1 = bf16[256,2048]{1,0:T(8,128)(2,1)} collective-permute-done((bf16[256,2048]{1,0:T(8,128)(2,1)}, bf16[256,2048]{1,0:T(8,128)(2,1)}, u32[]{:S(2)}, u32[]{:S(2)}) %collective-permute-start.1) | collective-permute-done | bytes 1048608 | tf_op jit(solution)/shard_map/ppermute | solution.py:49
  97.0 11.9 %collective-permute-done.2 = bf16[256,2048]{1,0:T(8,128)(2,1)S(1)} collective-permute-done((bf16[256,2048]{1,0:T(8,128)(2,1)}, bf16[256,2048]{1,0:T(8,128)(2,1)S(1)}, u32[]{:S(2)}, u32[]{:S(2)}) %collective-permute-start.2) | collective-permute-done | bytes 1048608 | tf_op jit(solution)/shard_map/ppermute | solution.py:49
  119.5 23.3 %collective-permute-done.4.refs_8_.refs_20_ = bf16[4,256,256]{2,1,0:T(8,128)(2,1)S(1)} collective-permute-done((bf16[4,256,256]{2,1,0:T(8,128)(2,1)S(1)}, bf16[4,256,256]{2,1,0:T(8,128)(2,1)S(1)}, u32[]{:S(2)}, u32[]{:S(2)}) %collective-permute-start.4) | collective-permute-done | bytes 524320 | tf_op jit(solution)/shard_map/ppermute | solution.py:54
  147.5 16.2 %attend.2 = (bf16[256,512]{1,0:T(8,128)(2,1)}, bf16[256,512]{1,0:T(8,128)(2,1)}, bf16[256,512]{1,0:T(8,128)(2,1)}, bf16[256,512]{1,0:T(8,128)(2,1)}, f32[4,4,512]{2,1,0:T(4,128)}) custom-call(s32[16]{0:T(128)} %stack.124.refs_0_, s32[4,1,256]{2,1,0:T(1,128)} %broadcast_in_dim.22.refs_1_, s32[1,1,256]{2,1,0:T(1,128)} %bitcast.140, ...), custom_call_target="tpu_custom_call" | custom-call | flops 4294967296 | bytes 2097152 | tf_op jit(solution)/shard_map/attend/pallas_call | solution.py:257
  163.8 9.1 %collective-permute-done.7 = bf16[256,2048]{1,0:T(8,128)(2,1)} collective-permute-done((bf16[256,2048]{1,0:T(8,128)(2,1)}, bf16[256,2048]{1,0:T(8,128)(2,1)}, u32[]{:S(2)}, u32[]{:S(2)}) %collective-permute-start.7) | collective-permute-done | bytes 1048608 | tf_op jit(solution)/shard_map/ppermute | solution.py:49
  172.8 16.2 %attend.3 = (bf16[256,512]{1,0:T(8,128)(2,1)}, bf16[256,512]{1,0:T(8,128)(2,1)}, bf16[256,512]{1,0:T(8,128)(2,1)}, bf16[256,512]{1,0:T(8,128)(2,1)}, f32[4,4,512]{2,1,0:T(4,128)}) custom-call(s32[16]{0:T(128)} %stack.124.refs_0_, ...), custom_call_target="tpu_custom_call", output_to_operand_aliasing={{0}: (11, {}), {1}: (12, {}), {2}: (13, {}), {3}: (14, {}),... | custom-call | flops 4294967296 | bytes 2097152 | tf_op jit(solution)/shard_map/attend/pallas_call | solution.py:257
  189.1 10.1 %collective-permute-done.8 = bf16[256,2048]{1,0:T(8,128)(2,1)S(1)} collective-permute-done((bf16[256,2048]{1,0:T(8,128)(2,1)}, bf16[256,2048]{1,0:T(8,128)(2,1)S(1)}, u32[]{:S(2)}, u32[]{:S(2)}) %collective-permute-start.8) | collective-permute-done | bytes 1048608 | tf_op jit(solution)/shard_map/ppermute | solution.py:49
  215.7 13.3 %collective-permute-done.9 = bf16[256,2048]{1,0:T(8,128)(2,1)} collective-permute-done((bf16[256,2048]{1,0:T(8,128)(2,1)}, bf16[256,2048]{1,0:T(8,128)(2,1)}, u32[]{:S(2)}, u32[]{:S(2)}) %collective-permute-start.9) | collective-permute-done | bytes 1048608 | tf_op jit(solution)/shard_map/ppermute | solution.py:49
  239.0 15.9 %collective-permute-done.10 = bf16[256,2048]{1,0:T(8,128)(2,1)S(1)} collective-permute-done((bf16[256,2048]{1,0:T(8,128)(2,1)S(1)}, bf16[256,2048]{1,0:T(8,128)(2,1)S(1)}, u32[]{:S(2)}, u32[]{:S(2)}) %collective-permute-start.10) | collective-permute-done | bytes 1048608 | tf_op jit(solution)/shard_map/ppermute | solution.py:49
  266.8 11.8 %collective-permute-done.11 = bf16[256,2048]{1,0:T(8,128)(2,1)S(1)} collective-permute-done((bf16[256,2048]{1,0:T(8,128)(2,1)S(1)}, bf16[256,2048]{1,0:T(8,128)(2,1)S(1)}, u32[]{:S(2)}, u32[]{:S(2)}) %collective-permute-start.11) | collective-permute-done | bytes 1048608 | tf_op jit(solution)/shard_map/ppermute | solution.py:49
  316.5 9.8 %collective-permute-done.13 = bf16[256,2048]{1,0:T(8,128)(2,1)S(1)} collective-permute-done((bf16[256,2048]{1,0:T(8,128)(2,1)S(1)}, bf16[256,2048]{1,0:T(8,128)(2,1)S(1)}, u32[]{:S(2)}, u32[]{:S(2)}) %collective-permute-start.13) | collective-permute-done | bytes 1048608 | tf_op jit(solution)/shard_map/ppermute | solution.py:49
  382.4 12.4 %convolution_convert_fusion.1 = bf16[2048,2048]{1,0:T(8,128)(2,1)} fusion(bf16[256,2048]{1,0:T(8,128)(2,1)S(1)} %copy-done.87, bf16[256,2048]{1,0:T(8,128)(2,1)} %collective-permute-done.7, bf16[256,2048]{1,0:T(8,128)(2,1)} %collective-permute-done.3, bf16[256,2048]{1,0:T(8,128)(2,1)S(1)} %bitcast.125, bf16[256,2048]{1,0:T(8,128)(2,1)S(1)} %get-tuple-element.239, ...), kind=kOutput, calls=%fused_computation.16 | convolution fusion | flops 8627683328 | bytes 16777216 | tf_op jit(solution)/shard_map/dot_general | solution.py:25
  429.7 25.7 %convolution_convert_fusion = bf16[2048,4096]{1,0:T(8,128)(2,1)} fusion(bf16[256,2048]{1,0:T(8,128)(2,1)} %get-tuple-element.236, bf16[256,2048]{1,0:T(8,128)(2,1)} %get-tuple-element.235, bf16[256,2048]{1,0:T(8,128)(2,1)} %copy-done.32, bf16[256,2048]{1,0:T(8,128)(2,1)} %copy-done.33, bf16[256,2048]{1,0:T(8,128)(2,1)} %copy-done.30, ...), kind=kOutput, calls=%fused_computation | convolution fusion | flops 17272143872 | bytes 29360128 | tf_op jit(solution)/shard_map/dot_general | solution.py:25
  476.2 13.9 %collective-permute-done.18 = bf16[256,2048]{1,0:T(8,128)(2,1)S(1)} collective-permute-done((bf16[256,2048]{1,0:T(8,128)(2,1)S(1)}, bf16[256,2048]{1,0:T(8,128)(2,1)S(1)}, u32[]{:S(2)}, u32[]{:S(2)}) %collective-permute-start.18) | collective-permute-done | bytes 1048608 | tf_op jit(solution)/shard_map/ppermute | solution.py:49
  500.4 13.3 %collective-permute-done.20 = bf16[256,2048]{1,0:T(8,128)(2,1)S(1)} collective-permute-done((bf16[256,2048]{1,0:T(8,128)(2,1)S(1)}, bf16[256,2048]{1,0:T(8,128)(2,1)S(1)}, u32[]{:S(2)}, u32[]{:S(2)}) %collective-permute-start.20) | collective-permute-done | bytes 1048608 | tf_op jit(solution)/shard_map/ppermute | solution.py:49
  522.5 18.0 %collective-permute-done.21 = bf16[256,2048]{1,0:T(8,128)(2,1)S(1)} collective-permute-done((bf16[256,2048]{1,0:T(8,128)(2,1)S(1)}, bf16[256,2048]{1,0:T(8,128)(2,1)S(1)}, u32[]{:S(2)}, u32[]{:S(2)}) %collective-permute-start.21) | collective-permute-done | bytes 1048608 | tf_op jit(solution)/shard_map/ppermute | solution.py:49
  543.0 29.2 %attend_back.2 = (bf16[256,512]{1,0:T(8,128)(2,1)}, bf16[256,512]{1,0:T(8,128)(2,1)}, bf16[256,512]{1,0:T(8,128)(2,1)}, bf16[256,512]{1,0:T(8,128)(2,1)}, f32[4,...) custom-call(s32[16]{0:T(128)} %stack.124.refs_0_, ...), custom_call_target="tpu_custom_call" | custom-call | flops 10737418240 | bytes 4194304 | tf_op jit(solution)/shard_map/attend_back/pallas_call | solution.py:416
  582.3 29.3 %attend_back.3 = (bf16[256,512]{1,0:T(8,128)(2,1)}, bf16[256,512]{1,0:T(8,128)(2,1)}, bf16[256,512]{1,0:T(8,128)(2,1)}, bf16[256,512]{1,0:T(8,128)(2,1)}, f32[4,...) custom-call(s32[16]{0:T(128)} %stack.124.refs_0_, ...), custom_call_target="tpu_custom_call", output_to_operand_aliasing={{0}: (23, {}), {1}: (24, {}), {2}: (25, {}), {3}: (26, {}),... | custom-call | flops 10737418240 | bytes 4194304 | tf_op jit(solution)/shard_map/attend_back/pallas_call | solution.py:416
  620.7 9.7 %collective-permute-done.26.came_ref = bf16[4,256,256]{2,1,0:T(8,128)(2,1)S(1)} collective-permute-done((bf16[4,256,256]{2,1,0:T(8,128)(2,1)S(1)}, bf16[4,256,256]{2,1,0:T(8,128)(2,1)S(1)}, u32[]{:S(2)}, u32[]{:S(2)}) %collective-permute-start.26) | collective-permute-done | bytes 524320 | tf_op jit(solution)/shard_map/ppermute | solution.py:54
  658.6 16.1 %collective-permute-done.27 = bf16[256,2048]{1,0:T(8,128)(2,1)} collective-permute-done((bf16[256,2048]{1,0:T(8,128)(2,1)}, bf16[256,2048]{1,0:T(8,128)(2,1)}, u32[]{:S(2)}, u32[]{:S(2)}) %collective-permute-start.27) | collective-permute-done | bytes 1048608 | tf_op jit(solution)/shard_map/ppermute | solution.py:49
  696.5 12.9 %collective-permute-done.33 = f32[2,64]{1,0:T(2,128)S(1)} collective-permute-done((f32[2,64]{1,0:T(2,128)S(1)}, f32[2,64]{1,0:T(2,128)S(1)}, u32[]{:S(2)}, u32[]{:S(2)}) %collective-permute-start.33) | collective-permute-done | bytes 544 | tf_op jit(solution)/shard_map/ppermute | solution.py:90
  726.1 16.8 %collective-permute-done.29 = bf16[256,2048]{1,0:T(8,128)(2,1)S(1)} collective-permute-done((bf16[256,2048]{1,0:T(8,128)(2,1)S(1)}, bf16[256,2048]{1,0:T(8,128)(2,1)S(1)}, u32[]{:S(2)}, u32[]{:S(2)}) %collective-permute-start.29) | collective-permute-done | bytes 1048608 | tf_op jit(solution)/shard_map/ppermute | solution.py:49
  (445 shorter events, 362.1 us)
Async XLA Ops:
  7.2 53.3 %all-gather.3.cloned.1.call-start = ((), (), s32[]{:S(2)}) async-start(), calls=%async_computation.3 | async-start | bytes 5898240 | tf_op jit(solution)/shard_map/all_gather | solution.py:76
  12.4 197.0 %all-gather.5.cloned.1.call-start = ((), (), s32[]{:S(2)}) async-start(), calls=%async_computation.4 | async-start | bytes 28311552 | tf_op jit(solution)/shard_map/all_gather | solution.py:76
  16.4 526.5 %reduce-scatter.4.cloned.1.call-start = ((), (), s32[]{:S(2)}) async-start(), calls=%async_computation.5 | async-start | bytes 9437184 | tf_op jit(solution)/shard_map/reduce_scatter | solution.py:697
  28.7 27.4 %collective-permute-start = (bf16[256,2048]{1,0:T(8,128)(2,1)S(1)}, bf16[256,2048]{1,0:T(8,128)(2,1)}, u32[]{:S(2)}, u32[]{:S(2)}) collective-permute-start(bf16[256,2048]{1,0:T(8,128)(2,1)S(1)} %fusion.62), channel_id=1, source_target_pairs={{0,1},{1,2},{2,3},{3,0},{4,5},{5,6},{6,7},{7,4},{8,9},{9,10},{10,1... | collective-permute-start | bytes 3145736 | tf_op jit(solution)/shard_map/ppermute | solution.py:49
  56.2 26.8 %collective-permute-start.1 = (bf16[256,2048]{1,0:T(8,128)(2,1)}, bf16[256,2048]{1,0:T(8,128)(2,1)}, u32[]{:S(2)}, u32[]{:S(2)}) collective-permute-start(bf16[256,2048]{1,0:T(8,128)(2,1)} %collective-permute-done), channel_id=1, source_target_pairs={{0,1},{1,2},{2,3},{3,0},{4,5},{5,6},{6,7},{7,4},{8,9},{9,10},{10,1... | collective-permute-start | bytes 3145736 | tf_op jit(solution)/shard_map/ppermute | solution.py:49
  82.9 26.0 %collective-permute-start.2 = (bf16[256,2048]{1,0:T(8,128)(2,1)}, bf16[256,2048]{1,0:T(8,128)(2,1)S(1)}, u32[]{:S(2)}, u32[]{:S(2)}) collective-permute-start(bf16[256,2048]{1,0:T(8,128)(2,1)} %collective-permute-done.1), channel_id=1, source_target_pairs={{0,1},{1,2},{2,3},{3,0},{4,5},{5,6},{6,7},{7,4},{8,9},{9,10},{10,1... | collective-permute-start | bytes 3145736 | tf_op jit(solution)/shard_map/ppermute | solution.py:49
  117.7 25.1 %collective-permute-start.4 = (bf16[4,256,256]{2,1,0:T(8,128)(2,1)S(1)}, bf16[4,256,256]{2,1,0:T(8,128)(2,1)S(1)}, u32[]{:S(2)}, u32[]{:S(2)}) collective-permute-start(bf16[4,256,256]{2,1,0:T(8,128)(2,1)S(1)} %pad_maximum_fusion.3.refs_7_.refs_19_), channel_id=1, source_target_pairs={{0,8},{4,12},{8,0},{12,4},{1,9},{5,13},{9,1},{13,5},{2,10},{6,14},... | collective-permute-start | bytes 1572872 | tf_op jit(solution)/shard_map/ppermute | solution.py:54
  119.5 24.5 %collective-permute-start.3 = (bf16[256,2048]{1,0:T(8,128)(2,1)S(1)}, bf16[256,2048]{1,0:T(8,128)(2,1)}, u32[]{:S(2)}, u32[]{:S(2)}) collective-permute-start(bf16[256,2048]{1,0:T(8,128)(2,1)S(1)} %bitcast.123), channel_id=1, source_target_pairs={{0,1},{1,2},{2,3},{3,0},{4,5},{5,6},{6,7},{7,4},{8,9},{9,10},{10,1... | collective-permute-start | bytes 3145736 | tf_op jit(solution)/shard_map/ppermute | solution.py:49
  145.5 27.3 %collective-permute-start.7 = (bf16[256,2048]{1,0:T(8,128)(2,1)}, bf16[256,2048]{1,0:T(8,128)(2,1)}, u32[]{:S(2)}, u32[]{:S(2)}) collective-permute-start(bf16[256,2048]{1,0:T(8,128)(2,1)} %collective-permute-done.3), channel_id=1, source_target_pairs={{0,1},{1,2},{2,3},{3,0},{4,5},{5,6},{6,7},{7,4},{8,9},{9,10},{10,1... | collective-permute-start | bytes 3145736 | tf_op jit(solution)/shard_map/ppermute | solution.py:49
  172.8 26.4 %collective-permute-start.8 = (bf16[256,2048]{1,0:T(8,128)(2,1)}, bf16[256,2048]{1,0:T(8,128)(2,1)S(1)}, u32[]{:S(2)}, u32[]{:S(2)}) collective-permute-start(bf16[256,2048]{1,0:T(8,128)(2,1)} %collective-permute-done.7), channel_id=1, source_target_pairs={{0,1},{1,2},{2,3},{3,0},{4,5},{5,6},{6,7},{7,4},{8,9},{9,10},{10,1... | collective-permute-start | bytes 3145736 | tf_op jit(solution)/shard_map/ppermute | solution.py:49
  203.0 26.0 %collective-permute-start.9 = (bf16[256,2048]{1,0:T(8,128)(2,1)}, bf16[256,2048]{1,0:T(8,128)(2,1)}, u32[]{:S(2)}, u32[]{:S(2)}) collective-permute-start(bf16[256,2048]{1,0:T(8,128)(2,1)} %convolution_convert_fusion.2), channel_id=1, source_target_pairs={{0,1},{1,2},{2,3},{3,0},{4,5},{5,6},{6,7},{7,4},{8,9},{9,10},{10,1... | collective-permute-start | bytes 3145736 | tf_op jit(solution)/shard_map/ppermute | solution.py:49
  326.3 27.9 %collective-permute-start.15 = (bf16[256,2048]{1,0:T(8,128)(2,1)S(1)}, bf16[256,2048]{1,0:T(8,128)(2,1)S(1)}, u32[]{:S(2)}, u32[]{:S(2)}) collective-permute-start(bf16[256,2048]{1,0:T(8,128)(2,1)S(1)} %collective-permute-done.13), channel_id=1, source_target_pairs={{0,1},{1,2},{2,3},{3,0},{4,5},{5,6},{6,7},{7,4},{8,9},{9,10},{10,1... | collective-permute-start | bytes 3145736 | tf_op jit(solution)/shard_map/ppermute | solution.py:49
  338.2 42.9 %collective-permute-start.14 = (bf16[256,2048]{1,0:T(8,128)(2,1)S(1)}, bf16[256,2048]{1,0:T(8,128)(2,1)S(1)}, u32[]{:S(2)}, u32[]{:S(2)}) collective-permute-start(bf16[256,2048]{1,0:T(8,128)(2,1)S(1)} %fusion.58), channel_id=1, source_target_pairs={{0,1},{1,2},{2,3},{3,0},{4,5},{5,6},{6,7},{7,4},{8,9},{9,10},{10,1... | collective-permute-start | bytes 3145736 | tf_op jit(solution)/shard_map/ppermute | solution.py:49
  382.4 25.6 %collective-permute-start.16 = (bf16[256,2048]{1,0:T(8,128)(2,1)}, bf16[256,2048]{1,0:T(8,128)(2,1)}, u32[]{:S(2)}, u32[]{:S(2)}) collective-permute-start(bf16[256,2048]{1,0:T(8,128)(2,1)} %add_convert_fusion.6), channel_id=1, source_target_pairs={{0,1},{1,2},{2,3},{3,0},{4,5},{5,6},{6,7},{7,4},{8,9},{9,10},{10,1... | collective-permute-start | bytes 3145736 | tf_op jit(solution)/shard_map/ppermute | solution.py:49
  408.1 203.5 %reduce-scatter.6.cloned.1.call-start = ((), (), s32[]{:S(2)}) async-start(), calls=%async_computation.6 | async-start | bytes 18874368 | tf_op jit(solution)/shard_map/reduce_scatter | solution.py:698
  426.3 29.1 %collective-permute-start.17 = (bf16[256,2048]{1,0:T(8,128)(2,1)}, bf16[256,2048]{1,0:T(8,128)(2,1)S(1)}, u32[]{:S(2)}, u32[]{:S(2)}) collective-permute-start(bf16[256,2048]{1,0:T(8,128)(2,1)} %add_convert_fusion.5), channel_id=1, source_target_pairs={{0,1},{1,2},{2,3},{3,0},{4,5},{5,6},{6,7},{7,4},{8,9},{9,10},{10,1... | collective-permute-start | bytes 3145736 | tf_op jit(solution)/shard_map/ppermute | solution.py:49
  455.4 290.2 %reduce-scatter.8.cloned.1.call-start = ((), (), s32[]{:S(2)}) async-start(), calls=%async_computation.7 | async-start | bytes 5898240 | tf_op jit(solution)/shard_map/reduce_scatter | solution.py:80
  513.8 26.8 %collective-permute-start.21 = (bf16[256,2048]{1,0:T(8,128)(2,1)S(1)}, bf16[256,2048]{1,0:T(8,128)(2,1)S(1)}, u32[]{:S(2)}, u32[]{:S(2)}) collective-permute-start(bf16[256,2048]{1,0:T(8,128)(2,1)S(1)} %collective-permute-done.20), channel_id=1, source_target_pairs={{0,1},{1,2},{2,3},{3,0},{4,5},{5,6},{6,7},{7,4},{8,9},{9,10},{10,1... | collective-permute-start | bytes 3145736 | tf_op jit(solution)/shard_map/ppermute | solution.py:49
  520.8 51.3 %collective-permute-start.19 = (bf16[256,2048]{1,0:T(8,128)(2,1)}, bf16[256,2048]{1,0:T(8,128)(2,1)S(1)}, u32[]{:S(2)}, u32[]{:S(2)}) collective-permute-start(bf16[256,2048]{1,0:T(8,128)(2,1)} %convolution_convert_fusion.4), channel_id=1, source_target_pairs={{0,1},{1,2},{2,3},{3,0},{4,5},{5,6},{6,7},{7,4},{8,9},{9,10},{10,1... | collective-permute-start | bytes 3145736 | tf_op jit(solution)/shard_map/ppermute | solution.py:49
  577.0 34.6 %collective-permute-start.22 = (bf16[256,2048]{1,0:T(8,128)(2,1)}, bf16[256,2048]{1,0:T(8,128)(2,1)}, u32[]{:S(2)}, u32[]{:S(2)}) collective-permute-start(bf16[256,2048]{1,0:T(8,128)(2,1)} %add_convert_fusion.4), channel_id=1, source_target_pairs={{0,1},{1,2},{2,3},{3,0},{4,5},{5,6},{6,7},{7,4},{8,9},{9,10},{10,1... | collective-permute-start | bytes 3145736 | tf_op jit(solution)/shard_map/ppermute | solution.py:49
  614.9 27.7 %collective-permute-start.23 = (bf16[256,2048]{1,0:T(8,128)(2,1)}, bf16[256,2048]{1,0:T(8,128)(2,1)}, u32[]{:S(2)}, u32[]{:S(2)}) collective-permute-start(bf16[256,2048]{1,0:T(8,128)(2,1)} %add_convert_fusion.3), channel_id=1, source_target_pairs={{0,1},{1,2},{2,3},{3,0},{4,5},{5,6},{6,7},{7,4},{8,9},{9,10},{10,1... | collective-permute-start | bytes 3145736 | tf_op jit(solution)/shard_map/ppermute | solution.py:49
  647.5 27.2 %collective-permute-start.27 = (bf16[256,2048]{1,0:T(8,128)(2,1)}, bf16[256,2048]{1,0:T(8,128)(2,1)}, u32[]{:S(2)}, u32[]{:S(2)}) collective-permute-start(bf16[256,2048]{1,0:T(8,128)(2,1)} %convolution_convert_fusion.3), channel_id=1, source_target_pairs={{0,1},{1,2},{2,3},{3,0},{4,5},{5,6},{6,7},{7,4},{8,9},{9,10},{10,1... | collective-permute-start | bytes 3145736 | tf_op jit(solution)/shard_map/ppermute | solution.py:49
  687.6 26.5 %collective-permute-start.28 = (bf16[256,2048]{1,0:T(8,128)(2,1)}, bf16[256,2048]{1,0:T(8,128)(2,1)}, u32[]{:S(2)}, u32[]{:S(2)}) collective-permute-start(bf16[256,2048]{1,0:T(8,128)(2,1)} %add_convert_fusion.1), channel_id=1, source_target_pairs={{0,1},{1,2},{2,3},{3,0},{4,5},{5,6},{6,7},{7,4},{8,9},{9,10},{10,1... | collective-permute-start | bytes 3145736 | tf_op jit(solution)/shard_map/ppermute | solution.py:49
  715.7 27.2 %collective-permute-start.29 = (bf16[256,2048]{1,0:T(8,128)(2,1)S(1)}, bf16[256,2048]{1,0:T(8,128)(2,1)S(1)}, u32[]{:S(2)}, u32[]{:S(2)}) collective-permute-start(bf16[256,2048]{1,0:T(8,128)(2,1)S(1)} %add_convert_fusion), channel_id=1, source_target_pairs={{0,1},{1,2},{2,3},{3,0},{4,5},{5,6},{6,7},{7,4},{8,9},{9,10},{10,1... | collective-permute-start | bytes 3145736 | tf_op jit(solution)/shard_map/ppermute | solution.py:49
  (129 other events, 1307.5 us)
Sparse Core Ops, SparseCore 0:
  12.5 44.7 all-gather.2
  59.2 141.5 all-gather.4
  408.2 71.9 reduce-scatter.3
  484.0 115.9 reduce-scatter.5
  674.8 54.2 reduce-scatter.7

commit v3 on v2

v3 whole, which is shorter than its diff:
```python
import functools
import math

import jax
import jax.numpy as jnp
from jax import lax
from jax.experimental import pallas as pl
from jax.experimental.pallas import tpu as pltpu
from jax.sharding import Mesh
from jax.sharding import PartitionSpec as P

D = 2048
HD = 64


NORM_EPS = 1e-05
ROPE_BASE = 1000000.0
MASKED = -1e30
CTX = ("ctx_pair", "ctx_place")


def matmul(left_mat, right_mat):
    return jnp.dot(left_mat, right_mat, preferred_element_type=jnp.float32)


def matmul_tn(left_mat, right_mat):
    return lax.dot_general(
        left_mat, right_mat, (((0,), (0,)), ((), ())), preferred_element_type=jnp.float32
    )


def matmul_nt(left_mat, right_mat):
    return lax.dot_general(
        left_mat, right_mat, (((1,), (1,)), ((), ())), preferred_element_type=jnp.float32
    )


def ring_hop(values):
    count = lax.axis_size("tp")
    return lax.ppermute(values, "tp", [(i, (i + 1) % count) for i in range(count)])


def ctx_swap(values, mask):
    count = lax.axis_size(CTX)
    return lax.ppermute(values, CTX, [(i, i ^ mask) for i in range(count)])


def ctx_masks():
    masks = [0]
    bit = lax.axis_size(CTX) // 2
    while bit:
        masks = masks + [mask ^ bit for mask in masks]
        bit //= 2
    return masks


def ctx_gather(own):
    blocks = [own]
    bit = lax.axis_size(CTX) // 2
    while bit:
        blocks = blocks + [ctx_swap(block, bit) for block in blocks]
        bit //= 2
    return blocks


def gather_weight(shard):
    return lax.all_gather(shard, ("dp", *CTX), axis=0, tiled=True)


def all_sum(values, axes):
    for axis in axes:
        count = lax.axis_size(axis)
        bit = 1
        while bit < count:
            values = values + lax.ppermute(values, axis, [(i, i ^ bit) for i in range(count)])
            bit *= 2
    return values


def shift(values, places):
    count = lax.axis_size("tp")
    return lax.ppermute(values, "tp", [(i, (i + places) % count) for i in range(count)])


def together(*values):
    return lax.optimization_barrier(values)


def lane_iota(shape):
    return lax.broadcasted_iota(jnp.int32, shape, 1)


def head_means(values):
    width = values.shape[1]
    row = lax.broadcasted_iota(jnp.int32, (width, width), 0) // HD
    col = lax.broadcasted_iota(jnp.int32, (width, width), 1) // HD
    pick = jnp.where(row == col, 1.0 / HD, 0.0).astype(jnp.float32)
    return jnp.dot(
        values, pick, precision=lax.Precision.HIGHEST, preferred_element_type=jnp.float32
    )


def half_swap(values):
    width, half = values.shape[1], HD // 2
    first = lax.rem(lane_iota(values.shape), HD) < half
    return jnp.where(
        first, pltpu.roll(values, width - half, 1), pltpu.roll(values, half, 1)
    )


def other_head(values):
    return pltpu.roll(values, HD, 1)


def twice(values, head):
    wide = values.astype(jnp.float32)
    low = lane_iota(wide.shape) < HD
    other = other_head(wide)
    both = jnp.where(low, wide, other) if head == 0 else jnp.where(low, other, wide)
    return both.astype(values.dtype)


def apart(values):
    wide = values.astype(jnp.float32)
    low = lane_iota(wide.shape) < HD
    zero = jnp.zeros_like(wide)
    return jnp.concatenate(
        [jnp.where(low, wide, zero), jnp.where(low, zero, wide)], axis=0
    ).astype(values.dtype)


def heads_kernel(raw_ref, cos_ref, sin_ref, q_gain_ref, k_gain_ref, q_ref, kv_ref):
    pair = 2 * HD
    q_cols = q_ref.shape[1]
    k_cols = kv_ref.shape[1] // 2
    cos, sin = cos_ref[...], sin_ref[...]
    for first in range(0, q_cols + k_cols, pair):
        values = raw_ref[:, first : first + pair]
        gain = q_gain_ref[...] if first < q_cols else k_gain_ref[...]
        normed = values * lax.rsqrt(head_means(values * values) + NORM_EPS) * gain
        turned = (normed * cos + half_swap(normed) * sin).astype(jnp.bfloat16)
        if first < q_cols:
            q_ref[:, first : first + pair] = turned
        else:
            kv_ref[:, first - q_cols : first - q_cols + pair] = turned
    kv_ref[:, k_cols:] = raw_ref[:, q_cols + k_cols :].astype(jnp.bfloat16)


def make_heads(raw, cos_wide, sin_wide, q_gain, k_gain, q_cols, k_cols):
    rows = raw.shape[0]
    return pl.pallas_call(
        heads_kernel,
        out_shape=(
            jax.ShapeDtypeStruct((rows, q_cols), jnp.bfloat16),
            jax.ShapeDtypeStruct((rows, 2 * k_cols), jnp.bfloat16),
        ),
        cost_estimate=pl.CostEstimate(
            flops=rows * raw.shape[1] * 400, bytes_accessed=rows * raw.shape[1] * 7, transcendentals=0
        ),
        name="make_heads",
    )(raw, cos_wide, sin_wide, q_gain, k_gain)


def turn_back(grad, values, gain, cos, sin):
    turned = grad * cos - half_swap(grad) * sin
    scale = lax.rsqrt(head_means(values * values) + NORM_EPS)
    unit = values * scale
    scaled = turned * gain
    return scale * (scaled - unit * head_means(scaled * unit)), turned * unit


def fill_bias(starts_ref, low_ref, high_ref, bias_ref, piece):
    low, high = low_ref[0], high_ref[0]
    for i in range(bias_ref.shape[0] // piece):
        place = starts_ref[i] + lax.broadcasted_iota(jnp.int32, (piece, low.shape[1]), 0)
        linked = (place >= low) & (place <= high)
        bias_ref[i * piece : (i + 1) * piece, :] = jnp.where(linked, 0.0, MASKED)


def attend_kernel(places, blocks, block_keys, skip, *refs):
    starts_ref, low_ref, high_ref = refs[:3]
    q_refs = refs[3 : 3 + places]
    kv_refs = refs[3 + places : 3 + places + blocks * places]
    refs = refs[3 + places + blocks * places + skip :]
    out_refs = refs[:places]
    total_ref, bias_ref, key_ref, value_ref = refs[places:]
    pair = 2 * HD
    piece, q_cols = q_refs[0].shape
    rows = places * piece
    k_cols = kv_refs[0].shape[1] // 2
    k_heads = k_cols // HD
    group = q_cols // k_cols
    scale = math.log2(math.e) / math.sqrt(HD)
    fill_bias(starts_ref, low_ref, high_ref, bias_ref, piece)
    for block in range(blocks):
        mine = kv_refs[block * places : (block + 1) * places]
        for head in range(k_heads):
            cols = slice(head // 2 * pair, head // 2 * pair + pair)
            vcols = slice(k_cols + head // 2 * pair, k_cols + head // 2 * pair + pair)
            where = slice(block * block_keys, (block + 1) * block_keys)
            keys = jnp.concatenate([ref[:, cols] for ref in mine], axis=0)
            key_ref[head, where, :] = twice(keys, head % 2)
            if head % 2 == 0:
                values = jnp.concatenate([ref[:, vcols] for ref in mine], axis=0)
                value_ref[head // 2, :, where] = values.astype(jnp.float32).T.astype(jnp.bfloat16)
    for first in range(0, q_cols, pair):
        head = first // HD // group
        queries = apart(jnp.concatenate([q_ref[:, first : first + pair] for q_ref in q_refs], axis=0))

        def step(block, carry):
            mixed, total = carry
            where = pl.ds(pl.multiple_of(block * block_keys, block_keys), block_keys)
            scores = matmul_nt(key_ref[head, where, :], queries)
            bias = bias_ref[where, :]
            weight = jnp.exp2(scores * scale + jnp.concatenate([bias, bias], axis=1))
            total = total + jnp.sum(weight, axis=0, keepdims=True)
            values = value_ref[head // 2, head % 2 * HD : (head % 2 + 1) * HD, where]
            return mixed + matmul(values, weight.astype(jnp.bfloat16)), total

        mixed, total = lax.fori_loop(
            0,
            blocks,
            step,
            (jnp.zeros((HD, 2 * rows), jnp.float32), jnp.zeros((1, 2 * rows), jnp.float32)),
        )
        mixed = mixed / total
        out = jnp.concatenate([mixed[:, :rows], mixed[:, rows:]], axis=0).T.astype(jnp.bfloat16)
        for place in range(places):
            out_refs[place][:, first : first + pair] = out[place * piece : (place + 1) * piece]
        total_ref[0, first // pair, :] = jnp.log2(total)[0]


def attend(starts, low, high, q_chunks, kv_blocks, batch, part, parts, before):
    places, blocks = len(q_chunks), len(kv_blocks)
    kv_flat = [kv for block in kv_blocks for kv in block]
    count = batch // parts
    base = part * count
    rows, q_cols = q_chunks[0].shape
    piece = rows // batch
    kv_cols = kv_flat[0].shape[1]
    k_cols = kv_cols // 2
    keys = blocks * places * piece
    q_rows = places * piece
    pairs = q_cols // (2 * HD)
    q_spec = pl.BlockSpec((piece, q_cols), lambda b: (base + b, 0))
    kv_spec = pl.BlockSpec((piece, kv_cols), lambda b: (base + b, 0))
    line_spec = pl.BlockSpec((1, 1, q_rows), lambda b: (base + b, 0, 0))
    work = count * q_cols // HD * q_rows * keys
    results = pl.pallas_call(
        functools.partial(attend_kernel, places, blocks, places * piece, len(before)),
        grid=(count,),
        out_shape=tuple(
            [jax.ShapeDtypeStruct((rows, q_cols), jnp.bfloat16)] * places
            + [jax.ShapeDtypeStruct((batch, pairs, 2 * q_rows), jnp.float32)]
        ),
        in_specs=[
            pl.BlockSpec(memory_space=pltpu.SMEM),
            line_spec,
            pl.BlockSpec((1, 1, q_rows), lambda b: (0, 0, 0)),
        ]
        + [q_spec] * places
        + [kv_spec] * len(kv_flat)
        + [pl.BlockSpec(memory_space=pl.ANY)] * len(before),
        out_specs=tuple(
            [q_spec] * places + [pl.BlockSpec((1, pairs, 2 * q_rows), lambda b: (base + b, 0, 0))]
        ),
        input_output_aliases={3 + places + len(kv_flat) + i: i for i in range(len(before))},
        scratch_shapes=[
            pltpu.VMEM((keys, q_rows), jnp.float32),
            pltpu.VMEM((k_cols // HD, keys, 2 * HD), jnp.bfloat16),
            pltpu.VMEM((k_cols // HD // 2, 2 * HD, keys), jnp.bfloat16),
        ],
        cost_estimate=pl.CostEstimate(
            flops=work * 4 * HD * 4, bytes_accessed=count * q_rows * q_cols * 8, transcendentals=work
        ),
        name="attend",
    )(starts, low, high, *q_chunks, *kv_flat, *before)
    return list(results)


def attend_back_kernel(places, blocks, block_keys, *refs):
    starts_ref, low_ref, high_ref, total_ref, cos_ref, sin_ref, gain_ref = refs[:7]
    refs = refs[7:]
    q_refs, refs = refs[:places], refs[places:]
    raw_refs, refs = refs[:places], refs[places:]
    grad_refs, refs = refs[:places], refs[places:]
    kv_refs, refs = refs[: blocks * places], refs[blocks * places :]
    dq_ref, refs = refs[0], refs[1:]
    dkv_refs, refs = refs[:blocks], refs[blocks:]
    gain_sum_ref, bias_ref, key_ref, turned_ref, value_ref, prob_ref, dprob_ref, dkey_ref, dvalue_ref = refs
    pair = 2 * HD
    piece, q_cols = q_refs[0].shape
    rows = places * piece
    k_cols = kv_refs[0].shape[1] // 2
    k_heads = k_cols // HD
    group = q_cols // k_cols
    inv_root = 1.0 / math.sqrt(HD)
    scale = math.log2(math.e) * inv_root
    fill_bias(starts_ref, low_ref, high_ref, bias_ref, piece)

    @pl.when(pl.program_id(0) == 0)
    def _():
        gain_sum_ref[...] = jnp.zeros_like(gain_sum_ref)

    for block in range(blocks):
        mine = kv_refs[block * places : (block + 1) * places]
        for head in range(k_heads):
            cols = slice(head // 2 * pair, head // 2 * pair + pair)
            vcols = slice(k_cols + head // 2 * pair, k_cols + head // 2 * pair + pair)
            where = slice(block * block_keys, (block + 1) * block_keys)
            keys = jnp.concatenate([ref[:, cols] for ref in mine], axis=0)
            values = jnp.concatenate([ref[:, vcols] for ref in mine], axis=0)
            key_ref[head, where, :] = twice(keys, head % 2)
            value_ref[head, where, :] = twice(values, head % 2)
            if head % 2 == 0:
                turned_ref[head // 2, :, where] = keys.astype(jnp.float32).T.astype(jnp.bfloat16)
    for first in range(0, q_cols, pair):
        head = first // HD // group
        fresh = first % (group * HD) == 0
        queries = apart(jnp.concatenate([q_ref[:, first : first + pair] for q_ref in q_refs], axis=0))
        grads = apart(jnp.concatenate([g_ref[:, first : first + pair] for g_ref in grad_refs], axis=0))
        total = total_ref[0, first // pair : first // pair + 1, :]

        def look(block, delta):
            where = pl.ds(pl.multiple_of(block * block_keys, block_keys), block_keys)
            scores = matmul_nt(key_ref[head, where, :], queries)
            bias = bias_ref[where, :]
            prob = jnp.exp2(scores * scale + jnp.concatenate([bias, bias], axis=1) - total)
            dprob = matmul_nt(value_ref[head, where, :], grads)
            prob_ref[where, :] = prob
            dprob_ref[where, :] = dprob
            return delta + jnp.sum(prob * dprob, axis=0, keepdims=True)

        delta = lax.fori_loop(0, blocks, look, jnp.zeros((1, 2 * rows), jnp.float32))

        def step(block, dquery):
            where = pl.ds(pl.multiple_of(block * block_keys, block_keys), block_keys)
            prob = prob_ref[where, :]
            dscore = (prob * (dprob_ref[where, :] - delta)).astype(jnp.bfloat16)
            dvalue = matmul(prob.astype(jnp.bfloat16), grads)
            dkey = matmul(dscore, queries)
            if fresh:
                dvalue_ref[head, where, :] = dvalue
                dkey_ref[head, where, :] = dkey
            else:
                dvalue_ref[head, where, :] += dvalue
                dkey_ref[head, where, :] += dkey
            keys = turned_ref[head // 2, head % 2 * HD : (head % 2 + 1) * HD, where]
            return dquery + matmul(keys, dscore)

        dquery = lax.fori_loop(0, blocks, step, jnp.zeros((HD, 2 * rows), jnp.float32)) * inv_root
        dquery = jnp.concatenate([dquery[:, :rows], dquery[:, rows:]], axis=0).T
        raw = jnp.concatenate([raw_ref[:, first : first + pair] for raw_ref in raw_refs], axis=0)
        dq, addend = turn_back(
            dquery, raw, gain_ref[...], cos_ref[...].reshape(rows, pair), sin_ref[...].reshape(rows, pair)
        )
        gain_sum_ref[...] += jnp.sum(addend.reshape(-1, 8, pair), axis=0)
        dq_ref[:, :, first : first + pair] = dq.reshape(places, piece, pair).astype(jnp.bfloat16)
    low = lane_iota((block_keys, pair)) < HD
    for block in range(blocks):
        where = slice(block * block_keys, (block + 1) * block_keys)
        for first in range(0, k_heads, 2):
            for shift, ref, factor in ((0, dkey_ref, inv_root), (k_cols, dvalue_ref, 1.0)):
                one, two = ref[first, where, :], ref[first + 1, where, :]
                sums = jnp.where(low, one + other_head(one), two + other_head(two)) * factor
                cols = slice(shift + first // 2 * pair, shift + first // 2 * pair + pair)
                dkv_refs[block][:, :, cols] = sums.reshape(places, piece, pair).astype(
                    dkv_refs[block].dtype
                )


def attend_back(
    starts,
    low,
    high,
    totals,
    cos_wide,
    sin_wide,
    q_gain,
    q_chunks,
    raw_chunks,
    grad_chunks,
    kv_blocks,
    kinds,
    batch,
    part,
    parts,
):
    places, blocks = len(q_chunks), len(kv_blocks)
    kv_flat = [kv for block in kv_blocks for kv in block]
    count = batch // parts
    base = part * count
    rows, q_cols = q_chunks[0].shape
    piece = rows // batch
    kv_cols = kv_flat[0].shape[1]
    k_cols = kv_cols // 2
    keys = blocks * places * piece
    q_rows = places * piece
    pairs = q_cols // (2 * HD)
    k_heads = k_cols // HD
    q_spec = pl.BlockSpec((piece, q_cols), lambda b: (base + b, 0))
    kv_spec = pl.BlockSpec((piece, kv_cols), lambda b: (base + b, 0))
    line_spec = pl.BlockSpec((1, 1, q_rows), lambda b: (base + b, 0, 0))
    turn_spec = pl.BlockSpec((places, piece, 2 * HD), lambda b: (0, base + b, 0))
    work = count * q_cols // HD * q_rows * keys
    results = pl.pallas_call(
        functools.partial(attend_back_kernel, places, blocks, places * piece),
        grid=(count,),
        out_shape=tuple(
            [jax.ShapeDtypeStruct((places, rows // parts, q_cols), jnp.bfloat16)]
            + [jax.ShapeDtypeStruct((places, rows // parts, kv_cols), kind) for kind in kinds]
            + [jax.ShapeDtypeStruct((8, 2 * HD), jnp.float32)]
        ),
        in_specs=[
            pl.BlockSpec(memory_space=pltpu.SMEM),
            line_spec,
            pl.BlockSpec((1, 1, q_rows), lambda b: (0, 0, 0)),
            pl.BlockSpec((1, pairs, 2 * q_rows), lambda b: (base + b, 0, 0)),
            turn_spec,
            turn_spec,
            pl.BlockSpec((1, 2 * HD), lambda b: (0, 0)),
        ]
        + [q_spec] * (3 * places)
        + [kv_spec] * len(kv_flat),
        out_specs=tuple(
            [pl.BlockSpec((places, piece, q_cols), lambda b: (0, b, 0))]
            + [pl.BlockSpec((places, piece, kv_cols), lambda b: (0, b, 0))] * blocks
            + [pl.BlockSpec((8, 2 * HD), lambda b: (0, 0))]
        ),
        scratch_shapes=[
            pltpu.VMEM((keys, q_rows), jnp.float32),
            pltpu.VMEM((k_heads, keys, 2 * HD), jnp.bfloat16),
            pltpu.VMEM((k_heads // 2, 2 * HD, keys), jnp.bfloat16),
            pltpu.VMEM((k_heads, keys, 2 * HD), jnp.bfloat16),
            pltpu.VMEM((keys, 2 * q_rows), jnp.float32),
            pltpu.VMEM((keys, 2 * q_rows), jnp.float32),
            pltpu.VMEM((k_heads, keys, 2 * HD), jnp.float32),
            pltpu.VMEM((k_heads, keys, 2 * HD), jnp.float32),
        ],
        cost_estimate=pl.CostEstimate(
            flops=work * 10 * HD * 4, bytes_accessed=count * q_rows * q_cols * 16, transcendentals=work
        ),
        name="attend_back",
    )(
        starts,
        low,
        high,
        totals,
        cos_wide,
        sin_wide,
        q_gain,
        *q_chunks,
        *raw_chunks,
        *grad_chunks,
        *kv_flat,
    )
    return results[0], list(results[1:-1]), results[-1]


def heads_back_kernel(places, parts, q_cols, *refs):
    dq_refs, refs = refs[:parts], refs[parts:]
    own_refs, refs = refs[:parts], refs[parts:]
    came_refs, refs = refs[:parts], refs[parts:]
    raw_refs, refs = refs[:places], refs[places:]
    cos_ref, sin_ref, gain_ref, out_ref, gain_sum_ref = refs
    rows = raw_refs[0].shape[0]
    part_rows = rows // parts
    k_cols = own_refs[0].shape[2] // 2
    pair = 2 * HD
    addends = jnp.zeros((8, pair), jnp.float32)
    for place in range(places):
        for part in range(parts):
            mine = slice(part * part_rows, (part + 1) * part_rows)
            out = slice(place * rows + part * part_rows, place * rows + (part + 1) * part_rows)
            out_ref[out, :q_cols] = dq_refs[part][place]
            grads = own_refs[part][place] + came_refs[part][place].astype(jnp.float32)
            for first in range(0, k_cols, pair):
                cols = slice(first, first + pair)
                dk, addend = turn_back(
                    grads[:, cols],
                    raw_refs[place][mine, cols],
                    gain_ref[...],
                    cos_ref[place, mine],
                    sin_ref[place, mine],
                )
                out_ref[out, q_cols + first : q_cols + first + pair] = dk.astype(jnp.bfloat16)
                addends = addends + jnp.sum(addend.reshape(-1, 8, pair), axis=0)
            out_ref[out, q_cols + k_cols :] = grads[:, k_cols:].astype(jnp.bfloat16)
    gain_sum_ref[...] = addends


def heads_back(dq_parts, own_parts, came_parts, raw_chunks, cos_wide, sin_wide, k_gain):
    parts, places = len(dq_parts), len(raw_chunks)
    rows = raw_chunks[0].shape[0]
    q_cols, kv_cols = dq_parts[0].shape[2], own_parts[0].shape[2]
    k_cols = kv_cols // 2

    def whole(array):
        return pl.BlockSpec(array.shape, lambda i: (0,) * array.ndim)

    inputs = [*dq_parts, *own_parts, *came_parts]
    turns = [cos_wide, sin_wide, k_gain]
    return pl.pallas_call(
        functools.partial(heads_back_kernel, places, parts, q_cols),
        grid=(1,),
        out_shape=(
            jax.ShapeDtypeStruct((places * rows, q_cols + kv_cols), jnp.bfloat16),
            jax.ShapeDtypeStruct((8, 2 * HD), jnp.float32),
        ),
        in_specs=[whole(array) for array in inputs]
        + [pl.BlockSpec((rows, k_cols), lambda i: (0, q_cols // k_cols))] * places
        + [whole(array) for array in turns],
        out_specs=(
            pl.BlockSpec((places * rows, q_cols + kv_cols), lambda i: (0, 0)),
            pl.BlockSpec((8, 2 * HD), lambda i: (0, 0)),
        ),
        cost_estimate=pl.CostEstimate(
            flops=places * rows * kv_cols * 400, bytes_accessed=places * rows * 4096, transcendentals=0
        ),
        name="heads_back",
    )(*inputs, *raw_chunks, *turns)


def feed_kernel(count, *refs):
    hidden_refs, grad_refs = refs[:count], refs[count : 2 * count]
    gate_ref, up_ref, down_ref, act_ref, dgate_ref, dup_ref, hidden, grads = refs[2 * count :]

    @pl.when(pl.program_id(0) == 0)
    def _():
        rows = hidden_refs[0].shape[0]
        for i in range(count):
            hidden[i * rows : (i + 1) * rows, :] = hidden_refs[i][...]
            grads[i * rows : (i + 1) * rows, :] = grad_refs[i][...]

    gate = matmul(hidden[...], gate_ref[...])
    up = matmul(hidden[...], up_ref[...])
    grad = matmul(grads[...], down_ref[...])
    sigmoid = 1.0 / (1.0 + jnp.exp(-gate))
    silu = gate * sigmoid
    act_ref[...] = (silu * up).astype(jnp.bfloat16)
    dgate_ref[...] = (grad * up * sigmoid * (1.0 + gate * (1.0 - sigmoid))).astype(jnp.bfloat16)
    dup_ref[...] = (grad * silu).astype(jnp.bfloat16)


def feed_rows(hidden_rows, grad_rows, gate, up, down_t, cols):
    count = len(hidden_rows)
    rows, width = hidden_rows[0].shape
    total = count * rows
    tile = min(cols, 512 if count == 1 else 256)
    steps = cols // tile
    row_spec = pl.BlockSpec((rows, width), lambda j: (0, 0))
    out_spec = pl.BlockSpec((total, tile), lambda j: (0, j))

    def weight_spec(weight):
        return pl.BlockSpec((width, tile), lambda j: (0, weight[1] * steps + j))

    return pl.pallas_call(
        functools.partial(feed_kernel, count),
        grid=(steps,),
        out_shape=tuple([jax.ShapeDtypeStruct((total, cols), jnp.bfloat16)] * 3),
        in_specs=[row_spec] * (2 * count)
        + [
            weight_spec(gate),
            weight_spec(up),
            weight_spec(down_t),
        ],
        out_specs=tuple([out_spec] * 3),
        scratch_shapes=[pltpu.VMEM((total, width), jnp.bfloat16)] * 2,
        cost_estimate=pl.CostEstimate(
            flops=6 * total * width * cols,
            bytes_accessed=6 * width * cols + 4 * total * width + 6 * total * cols,
            transcendentals=total * cols,
        ),
        name="feed_rows",
    )(*hidden_rows, *grad_rows, gate[0], up[0], down_t[0])


def fill_rows(parts, whole):
    row = 0
    for line in parts:
        col = 0
        for ref in line:
            rows, cols = ref.shape
            whole[row : row + rows, col : col + cols] = ref[...]
            col += cols
        row += rows


def rows_nt_kernel(layouts, *refs):
    count = len(layouts)
    parts = []
    for lines, cols in layouts:
        parts.append([refs[i * cols : (i + 1) * cols] for i in range(lines)])
        refs = refs[lines * cols :]
    weight_refs, out_refs, wholes = refs[:count], refs[count:-count], refs[-count:]

    @pl.when(pl.program_id(0) == 0)
    def _():
        for part, whole in zip(parts, wholes):
            fill_rows(part, whole)

    result = matmul_nt(wholes[0][...], weight_refs[0][...])
    for weight_ref, whole in zip(weight_refs[1:], wholes[1:]):
        result = result + matmul_nt(whole[...], weight_ref[...])
    rows = out_refs[0].shape[0]
    for i, out_ref in enumerate(out_refs):
        out_ref[...] = result[i * rows : (i + 1) * rows].astype(out_ref.dtype)


def rows_nt(addends, kind, outs=1, tile=512):
    layouts, parts, depths = [], [], []
    for lines, _ in addends:
        layouts.append((len(lines), len(lines[0])))
        parts.extend(part for line in lines for part in line)
        depths.append(sum(part.shape[1] for part in lines[0]))
    rows = sum(line[0].shape[0] for line in addends[0][0])
    weights = [weight for _, weight in addends]
    width = weights[0][0].shape[0]

    def weight_spec(weight, depth):
        return pl.BlockSpec((tile, depth), lambda j: (j, weight[1]))

    results = pl.pallas_call(
        functools.partial(rows_nt_kernel, layouts),
        grid=(width // tile,),
        out_shape=tuple([jax.ShapeDtypeStruct((rows // outs, width), kind)] * outs),
        in_specs=[pl.BlockSpec(part.shape, lambda j: (0, 0)) for part in parts]
        + [weight_spec(weight, depth) for weight, depth in zip(weights, depths)],
        out_specs=tuple([pl.BlockSpec((rows // outs, tile), lambda j: (0, j))] * outs),
        scratch_shapes=[pltpu.VMEM((rows, depth), jnp.bfloat16) for depth in depths],
        cost_estimate=pl.CostEstimate(
            flops=2 * rows * sum(depths) * width,
            bytes_accessed=2 * sum(depths) * (rows + width) + 2 * rows * width,
            transcendentals=0,
        ),
        name="rows_nt",
    )(*parts, *[weight[0] for weight in weights])
    return list(results)


def add_kernel(one_ref, two_ref, out_ref):
    out_ref[...] = (one_ref[...].astype(jnp.float32) + two_ref[...].astype(jnp.float32)).astype(
        out_ref.dtype
    )


def add_rows(one, two, tile=1024):
    rows, cols = one.shape
    spec = pl.BlockSpec((rows, tile), lambda j: (0, j))
    return pl.pallas_call(
        add_kernel,
        grid=(cols // tile,),
        out_shape=jax.ShapeDtypeStruct(one.shape, one.dtype),
        in_specs=[spec, spec],
        out_specs=spec,
        cost_estimate=pl.CostEstimate(flops=rows * cols, bytes_accessed=6 * rows * cols, transcendentals=0),
        name="add_rows",
    )(one, two)


def split_kernel(rows_ref, weight_ref, *out_refs):
    result = matmul(rows_ref[...], weight_ref[...]).astype(jnp.bfloat16)
    for i, out_ref in enumerate(out_refs):

        @pl.when(pl.program_id(0) == i)
        def _():
            out_ref[...] = result


def split_columns(rows, weight, first, count, cols):
    total, depth = rows.shape
    return pl.pallas_call(
        split_kernel,
        grid=(count,),
        out_shape=tuple([jax.ShapeDtypeStruct((total, cols), jnp.bfloat16)] * count),
        in_specs=[
            pl.BlockSpec((total, depth), lambda j: (0, 0)),
            pl.BlockSpec((depth, cols), lambda j: (0, first + j)),
        ],
        out_specs=tuple([pl.BlockSpec((total, cols), lambda j: (0, 0))] * count),
        cost_estimate=pl.CostEstimate(
            flops=2 * total * depth * cols * count,
            bytes_accessed=2 * (total * depth + depth * cols * count + total * cols * count),
            transcendentals=0,
        ),
        name="split_columns",
    )(rows, weight)


def product_kernel(left_count, right_counts, blocks, first_ref, *refs):
    left_refs, refs = refs[:left_count], refs[left_count:]
    rights = []
    for count in right_counts:
        rights.append(refs[:count])
        refs = refs[count:]
    out_ref, left, right = refs
    steps = pl.num_programs(0) // len(rights)

    @pl.when(pl.program_id(0) == 0)
    def _():
        if blocks:
            cols = left.shape[1] // blocks
            row = 0
            for ref in left_refs:
                rows = ref.shape[0]
                for i in range(blocks):
                    start = pl.multiple_of((2 * i + first_ref[0]) * cols, cols)
                    left[row : row + rows, i * cols : (i + 1) * cols] = ref[:, pl.ds(start, cols)]
                row += rows
        else:
            fill_rows([[ref] for ref in left_refs], left)

    for i, refs in enumerate(rights):

        @pl.when(pl.program_id(0) // steps == i)
        def _():
            fill_rows([[ref] for ref in refs], right)

    out_ref[...] = matmul_tn(left[...], right[...]).astype(jnp.bfloat16)


def product(left, rights, tile=512, first=None, blocks=0):
    width, cols = left[0].shape[1], rights[0][0].shape[1]
    depth = sum(part.shape[0] for part in left)
    tile = min(tile, cols)
    steps = cols // tile
    out_rows = width // 2 if blocks else width
    first = jnp.zeros((1,), jnp.int32) if first is None else first

    def right_spec(part, index):
        return pl.BlockSpec(
            (part.shape[0], tile), lambda j: (0, jnp.clip(j - index * steps, 0, steps - 1))
        )

    return pl.pallas_call(
        functools.partial(product_kernel, len(left), [len(parts) for parts in rights], blocks),
        grid=(steps * len(rights),),
        out_shape=jax.ShapeDtypeStruct((out_rows, cols * len(rights)), jnp.bfloat16),
        in_specs=[pl.BlockSpec(memory_space=pltpu.SMEM)]
        + [pl.BlockSpec(part.shape, lambda j: (0, 0)) for part in left]
        + [right_spec(part, index) for index, parts in enumerate(rights) for part in parts],
        out_specs=pl.BlockSpec((out_rows, tile), lambda j: (0, j)),
        scratch_shapes=[
            pltpu.VMEM((depth, out_rows), jnp.bfloat16),
            pltpu.VMEM((depth, tile), jnp.bfloat16),
        ],
        cost_estimate=pl.CostEstimate(
            flops=2 * depth * out_rows * cols * len(rights),
            bytes_accessed=2 * (depth * width + (depth + out_rows) * cols * len(rights)),
            transcendentals=0,
        ),
        name="product",
    )(first, *left, *[part for parts in rights for part in parts])


def unit_of(values):
    scale = lax.rsqrt(jnp.mean(values * values, axis=-1, keepdims=True) + NORM_EPS)
    return values * scale, scale


def norm_kernel(rows_ref, more_ref, sum_ref, unit_ref):
    values = rows_ref[...].astype(jnp.float32) + more_ref[...]
    sum_ref[...] = values
    unit_ref[...] = unit_of(values)[0].astype(jnp.bfloat16)


def add_and_norm(rows, more, tile=64):
    count, width = rows.shape
    spec = pl.BlockSpec((tile, width), lambda i: (i, 0))
    return pl.pallas_call(
        norm_kernel,
        grid=(count // tile,),
        out_shape=(
            jax.ShapeDtypeStruct(rows.shape, jnp.float32),
            jax.ShapeDtypeStruct(rows.shape, jnp.bfloat16),
        ),
        in_specs=[spec, spec],
        out_specs=(spec, spec),
        cost_estimate=pl.CostEstimate(
            flops=5 * count * width, bytes_accessed=12 * count * width, transcendentals=0
        ),
        name="add_and_norm",
    )(rows, more)


def norm_back_kernel(one_ref, two_ref, rows_ref, base_ref, *out_refs):
    scaled = one_ref[...].astype(jnp.float32) + two_ref[...].astype(jnp.float32)
    unit, scale = unit_of(rows_ref[...].astype(jnp.float32))
    result = base_ref[...].astype(jnp.float32) + scale * (
        scaled - unit * jnp.mean(scaled * unit, axis=-1, keepdims=True)
    )
    for out_ref in out_refs:
        out_ref[...] = result.astype(out_ref.dtype)


def norm_back(one, two, rows, base, kinds, tile=64):
    count, width = rows.shape
    spec = pl.BlockSpec((tile, width), lambda i: (i, 0))
    return pl.pallas_call(
        norm_back_kernel,
        grid=(count // tile,),
        out_shape=tuple(jax.ShapeDtypeStruct(rows.shape, kind) for kind in kinds),
        in_specs=[spec] * 4,
        out_specs=tuple([spec] * len(kinds)),
        cost_estimate=pl.CostEstimate(
            flops=10 * count * width, bytes_accessed=14 * count * width, transcendentals=0
        ),
        name="norm_back",
    )(one, two, rows, base)


def per_device(
    block_in,
    segments,
    positions,
    attention_gain,
    query_weight,
    key_weight,
    value_weight,
    query_gain,
    key_gain,
    output_weight,
    hidden_gain,
    gate_weight,
    up_weight,
    down_weight,
    cotangent,
):
    tp_count = lax.axis_size("tp")
    tp_index = lax.axis_index("tp")
    ctx_index = lax.axis_index(CTX)
    batch, own_rows, width = block_in.shape
    rows = batch * own_rows
    ctx_rows = own_rows * tp_count
    places = range(tp_count)
    order = [*range(1, tp_count), 0]
    masks = ctx_masks()
    q_cols = query_weight.shape[1]
    k_cols = key_weight.shape[1]
    qkv_cols = q_cols + 2 * k_cols
    hidden_cols = gate_weight.shape[1]
    q_gain = jnp.tile(query_gain.astype(jnp.float32), 2)[None]
    k_gain = jnp.tile(key_gain.astype(jnp.float32), 2)[None]

    block = width // (lax.axis_size("dp") * lax.axis_size(CTX))
    paired = block % 128 == 0
    pair_first = lax.rem(ctx_index, 2).astype(jnp.int32)[None]

    def meet(arrays):
        return [*arrays, *[ctx_swap(array, 1) for array in arrays]] if paired else list(arrays)

    def grad_product(left, rights, tile=512):
        return product(left, rights, tile, pair_first, width // block // 2 if paired else 0)

    def scatter_sum(addend):
        axes = ("dp", CTX[0]) if paired else ("dp", *CTX)
        return lax.psum_scatter(addend, axes, scatter_dimension=0, tiled=True)

    back_places = [(tp_count - place) % tp_count for place in places]
    attention_rows = attention_gain.astype(jnp.float32)[:, None]
    hidden_gain_rows = hidden_gain.astype(jnp.float32)[:, None]
    qkv_weight = jnp.concatenate([query_weight, key_weight, value_weight], axis=1).astype(jnp.float32)
    first_weight = jnp.concatenate(
        [
            (gate_weight.astype(jnp.float32) * hidden_gain_rows).astype(jnp.bfloat16),
            (qkv_weight * attention_rows).astype(jnp.bfloat16),
        ],
        axis=1,
    )
    full_first = gather_weight(first_weight)
    full_qkv = full_first[:, hidden_cols:]

    def chunk_start(place):
        owner = lax.rem(tp_index - place + tp_count, tp_count)
        return owner * own_rows

    def own_part(table, start):
        return lax.dynamic_slice_in_dim(table, start, own_rows, 1)

    iota = jnp.arange(own_rows, dtype=jnp.int32)
    row_starts = [ctx_index * ctx_rows + chunk_start(place) for place in places]
    low = jnp.concatenate([own_part(segments, start) for start in row_starts], axis=1)[:, None]
    high = jnp.concatenate([start + iota for start in row_starts])[None, None]
    starts = jnp.stack(
        [
            jnp.bitwise_xor(ctx_index, mask) * ctx_rows + chunk_start(place)
            for mask in masks
            for place in places
        ]
    ).astype(jnp.int32)
    position = jnp.stack([own_part(positions, start).reshape(rows) for start in row_starts])
    half = HD // 2
    frequency = ROPE_BASE ** (-2.0 * jnp.arange(half, dtype=jnp.float32) / HD)
    sign = jnp.where(jnp.arange(2 * HD) % HD < half, -1.0, 1.0).astype(jnp.float32)
    angles = position.astype(jnp.float32)[..., None] * jnp.tile(frequency, 4)
    cos_wide, sin_wide = jnp.cos(angles), jnp.sin(angles) * sign

    def project(place):
        values = matmul(normed_rows[place], full_qkv)
        query_rot, kv = make_heads(
            values, cos_wide[place], sin_wide[place], q_gain, k_gain, q_cols, k_cols
        )
        return values, query_rot, kv

    def project_and_send(place):
        values, query_rot, kv = project(place)
        blocks = ctx_gather(kv)
        return values, query_rot, blocks

    tokens = block_in.reshape(rows, width)
    normed_rows, heads = [unit_of(tokens.astype(jnp.float32))[0].astype(jnp.bfloat16)], []
    for place in range(1, tp_count):
        came = ring_hop(normed_rows[-1])
        ready = range(tp_count - 1) if place == tp_count - 1 else []
        work = [project_and_send(mine) for mine in ready]
        came, work = together(came, work)
        if place == 1:
            came, out_own = together(came, output_weight.T)
            out_pieces = [out_own] + [shift(out_own, -other) for other in range(1, tp_count)]
        if place == 2:
            came, out_pieces = together(came, out_pieces)
            second_weight = jnp.concatenate(
                [*out_pieces, (up_weight.astype(jnp.float32) * hidden_gain_rows).astype(jnp.bfloat16)],
                axis=1,
            )
            full_second = gather_weight(second_weight)
        heads.extend(work)
        normed_rows.append(came)
    last_weight, normed_rows[-1] = together(down_weight.T, normed_rows[-1])
    full_down_t = gather_weight(last_weight)
    full_out, full_gate, full_up, full_down = (full_second, 0), (full_first, 0), (full_second, 1), (full_down_t, 0)

    grad_own, normed_rows[-1] = together(cotangent.reshape(rows, width), normed_rows[-1])
    came = ring_hop(grad_own)
    work = [project_and_send(mine) for mine in range(len(heads), tp_count)]
    came, work = together(came, work)
    heads.extend(work)
    raw, queries, gathered = ([h[i] for h in heads] for i in range(3))
    blocks = [[gathered[place][i] for place in places] for i in range(len(masks))]
    grad_rows = [grad_own, came]
    attended = []
    parts = 2
    late_qkv = full_qkv
    came = ring_hop(grad_rows[-1])
    for part in range(parts):
        attended = attend(starts, low, high, queries, blocks, batch, part, parts, attended)
        if part == 0:
            late_qkv, attended = together(late_qkv, attended)
    came, attended = together(came, attended)
    grad_rows.append(came)
    attended_rows, totals = attended[:tp_count], attended[tp_count]
    mine = [attended_rows[0]] + [shift(attended_rows[place], -place) for place in range(1, tp_count)]
    grad_rows[-1], mine = together(grad_rows[-1], mine)
    for _ in range(len(grad_rows), tp_count):
        grad_rows.append(ring_hop(grad_rows[-1]))
    met_grads = meet(grad_rows)
    (mixed_in,) = rows_nt([([mine], full_out)], jnp.float32)
    met_mine = [meet([piece]) for piece in mine]
    hidden, unit_hidden = add_and_norm(tokens, mixed_in)

    def feed(group):
        return feed_rows(
            [hidden_rows[place] for place in group],
            [grad_rows[place] for place in group],
            full_gate,
            full_up,
            full_down,
            hidden_cols,
        )

    def hidden_terms(fed):
        return rows_nt([([[fed[1]]], full_gate), ([[fed[2]]], full_up)], jnp.bfloat16, 2)

    first, second = list(places)[: tp_count // 2], list(places)[tp_count // 2 :]
    hidden_rows = [unit_hidden]
    fed_first, terms_first = None, None
    for place in range(1, tp_count):
        came = ring_hop(hidden_rows[-1])
        if place == len(first):
            fed_first = feed(first)
            came, fed_first, met_grads, met_mine = together(came, fed_first, met_grads, met_mine)
        if place == len(first) + 1:
            met_first = [meet([fed]) for fed in fed_first]
            terms_first = hidden_terms(fed_first)
            came, terms_first, met_first = together(came, terms_first, met_first)
        hidden_rows.append(came)

    came = ring_hop(terms_first[1])
    met_hidden = meet(hidden_rows)
    fed_second = feed(second)
    came, fed_second, met_hidden = together(came, fed_second, met_hidden)
    met_fed = [old + meet([fed]) for old, fed in zip(met_first, fed_second)]
    if paired:
        met_fed = [[fed[0], fed[2], fed[1], fed[3]] for fed in met_fed]
    terms_second = hidden_terms(fed_second)
    came = ring_hop(add_rows(came, terms_second[0]))
    down_product = grad_product(met_grads, [met_fed[0]])
    came, down_product = together(came, down_product)
    came = ring_hop(add_rows(came, terms_second[1]))
    down_shard = scatter_sum(down_product)
    gate_product = grad_product(met_hidden, [met_fed[1]])
    up_product = grad_product(met_hidden, [met_fed[2]])
    came, gate_product, up_product = together(came, gate_product, up_product)
    gate_shard = scatter_sum(gate_product)

    grad_hidden, branch = norm_back(
        came, terms_first[0], hidden, grad_own, (jnp.float32, jnp.bfloat16)
    )
    pieces = split_columns(branch, full_second, 0, tp_count, q_cols)
    grad_att = [pieces[0]] + [shift(pieces[place], place) for place in range(1, tp_count)]
    met_branch = meet([branch])
    feed_terms = rows_nt(
        [([[fed_first[0]], [fed_second[0]]], full_down)], jnp.bfloat16, tp_count
    )
    out_product = grad_product(met_branch, met_mine)
    grad_att, out_product, feed_terms = together(grad_att, out_product, feed_terms)
    out_shard = scatter_sum(out_product)

    kinds = [jnp.float32] * (len(masks) // 2) + [jnp.bfloat16] * (len(masks) - len(masks) // 2)
    query_gain_sum = jnp.zeros((8, 2 * HD), jnp.float32)
    dq_parts, own_parts, came_parts = [], [], []
    total = feed_terms[1]
    for step, place in enumerate(order[1:]):
        came = ring_hop(total)
        if step < 2:
            dq, back, addend = attend_back(
                starts,
                low,
                high,
                totals,
                cos_wide,
                sin_wide,
                q_gain,
                queries,
                raw,
                grad_att,
                blocks,
                kinds,
                batch,
                step,
                2,
            )
            came, dq, back, addend, grad_att, own_parts, came_parts = together(
                came, dq, back, addend, grad_att, own_parts, came_parts
            )
            if step == 0:
                came, down_shard = together(came, down_shard)
            query_gain_sum = query_gain_sum + addend
            dq_parts.append(dq)
            bit = 1
            while len(back) > 2:
                half_count = len(back) // 2
                back = [
                    back[i] + ctx_swap(back[half_count + i].astype(jnp.bfloat16), bit).astype(jnp.float32)
                    for i in range(half_count)
                ]
                bit *= 2
            own_parts.append(back[0])
            came_parts.append(ctx_swap(back[1].astype(jnp.bfloat16), bit))
        else:
            grad_qkv, key_gain_sum = heads_back(
                dq_parts, own_parts, came_parts, raw, cos_wide, sin_wide, k_gain
            )
            came, grad_qkv, gate_shard, out_shard = together(came, grad_qkv, gate_shard, out_shard)
        if place:
            total = add_rows(came, feed_terms[place])
    feed_out = came.astype(jnp.float32) + feed_terms[0].astype(jnp.float32)
    block_out = (hidden + feed_out).astype(jnp.bfloat16).reshape(block_in.shape)

    row_terms = rows_nt([([[grad_qkv]], (late_qkv, 0))], jnp.bfloat16, tp_count)
    up_shard = scatter_sum(up_product)
    head_sums = jnp.stack([query_gain_sum, key_gain_sum]).sum(axis=1).reshape(2, 2, HD).sum(axis=1)
    total = row_terms[1]
    out_total = out_shard[:, back_places[1] * q_cols : (back_places[1] + 1) * q_cols]
    for step, place in enumerate(order[1:]):
        came = ring_hop(total)
        start = back_places[place] * q_cols
        out_total = ring_hop(out_total).astype(jnp.float32) + out_shard[
            :, start : start + q_cols
        ].astype(jnp.float32)
        if place:
            out_total = out_total.astype(jnp.bfloat16)
        if step == 0:
            head_sums = all_sum(head_sums, (CTX, "dp"))
            qkv_product = product(normed_rows, [[grad_qkv]], grad_qkv.shape[1])
            came, qkv_product, head_sums, out_total = together(
                came, qkv_product, head_sums, out_total
            )
            qkv_shard = lax.psum_scatter(qkv_product, ("dp", *CTX), scatter_dimension=0, tiled=True)
        if step == 1:
            came, up_shard, out_total = together(came, up_shard, out_total)
        if place:
            total = add_rows(came, row_terms[place])
    qkv_sums = qkv_shard.astype(jnp.float32)
    gate_sums, up_sums = gate_shard.astype(jnp.float32), up_shard.astype(jnp.float32)
    attention_sum = jnp.sum(qkv_sums * qkv_weight, axis=1)
    hidden_sums = jnp.sum(
        gate_sums * gate_weight.astype(jnp.float32) + up_sums * up_weight.astype(jnp.float32), axis=1
    )
    small_sums = jnp.concatenate([jnp.stack([attention_sum, hidden_sums]), head_sums], axis=1)
    small_sums = all_sum(small_sums, ("tp",))
    attention_gain_grad, hidden_gain_grad = small_sums[0, :block], small_sums[1, :block]
    head_sums = small_sums[:, block:]
    (input_grad,) = norm_back(came, row_terms[0], tokens, grad_hidden, (jnp.float32,))
    output_grad = out_total.T
    down_grad = down_shard.astype(jnp.float32).T
    gate_grad, up_grad = gate_sums * hidden_gain_rows, up_sums * hidden_gain_rows
    qkv_grad = qkv_sums * attention_rows
    return (
        block_out,
        input_grad.reshape(block_in.shape),
        attention_gain_grad,
        qkv_grad[:, :q_cols],
        qkv_grad[:, q_cols : q_cols + k_cols],
        qkv_grad[:, q_cols + k_cols :],
        head_sums[0],
        head_sums[1],
        output_grad,
        hidden_gain_grad,
        gate_grad,
        up_grad,
        down_grad,
    )


def solution(mesh):
    in_specs = (
        P(None, ("dp", *CTX, "tp"), None),
        P(None, "dp"),
        P(None, "dp"),
        P(("dp", *CTX)),
        P(("dp", *CTX), "tp"),
        P(("dp", *CTX), "tp"),
        P(("dp", *CTX), "tp"),
        P(),
        P(),
        P("tp", ("dp", *CTX)),
        P(("dp", *CTX)),
        P(("dp", *CTX), "tp"),
        P(("dp", *CTX), "tp"),
        P("tp", ("dp", *CTX)),
        P(None, ("dp", *CTX, "tp"), None),
    )
    out_specs = (
        P(None, ("dp", *CTX, "tp"), None),
        P(None, ("dp", *CTX, "tp"), None),
        P(("dp", *CTX)),
        P(("dp", *CTX), "tp"),
        P(("dp", *CTX), "tp"),
        P(("dp", *CTX), "tp"),
        P(),
        P(),
        P("tp", ("dp", *CTX)),
        P(("dp", *CTX)),
        P(("dp", *CTX), "tp"),
        P(("dp", *CTX), "tp"),
        P("tp", ("dp", *CTX)),
    )
    shape = (mesh.shape["dp"], mesh.shape["ctx"] // 2, 2, mesh.shape["tp"])
    split = Mesh(mesh.devices.reshape(shape), ("dp", *CTX, "tp"))
    return jax.shard_map(
        per_device, mesh=split, in_specs=in_specs, out_specs=out_specs, check_vma=False
    )
```

time: 769 us -> 713 us (0.927)
  matrix products: 246 us -> 16.3 us
  Pallas kernels: 112 us -> 305 us
  other arithmetic: 57.4 us -> 24.4 us
  starting transfers between devices: 26.6 us -> 41.9 us
  blocking collectives: 10.4 us -> 0 us
    pallas_call x4 -> x23, Pallas kernels: 9.89 us -> 203 us  [the longest x5 63.6 us: product(): pl.pallas_call(functools.partial(product_kernel, len(left), [len(parts) f...]
    dot_general x24 -> x0, matrix products: 153 us -> none  [the longest x20 105 us: matmul_nt(): lax.dot_general(left_mat, right_mat, (((1,), (1,)), ((), ())), preferred_...]
    dot_general x20 -> x4, matrix products: 92.4 us -> 16.3 us  [matmul(): return jnp.dot(left_mat, right_mat, preferred_element_type=jnp.float32)]
    ppermute x24 -> x21, waiting for transfers between devices: 214 us -> 172 us  [ring_hop(): lax.ppermute(values, 'tp', [(i, (i + 1) % count) for i in range(count)])]
    ppermute x6 -> x46, waiting for transfers between devices: 33.7 us -> 74.3 us  [the longest x9 39.1 us: shift(): lax.ppermute(values, 'tp', [(i, (i + places) % count) for i in range(coun...]
    convert_element_type x17 -> x9, other arithmetic: 30.9 us -> 6.2 us  [the longest x2 1.8 us: per_device(): out_total = out_total.astype(jnp.bfloat16)]
    ppermute x6 -> x46, starting transfers between devices: 4.04 us -> 25.9 us  [the longest x37 13.2 us: ctx_swap(): return lax.ppermute(values, CTX, [(i, i ^ mask) for i in range(count)])]
    reduce_scatter x3 -> x5, waiting for transfers between devices: 0.02 us -> 15.5 us  [the longest x1 15.5 us: per_device(): lax.psum_scatter(qkv_product, ('dp', *CTX), scatter_dimension=0, tiled=True)]
  transfers between devices with their start and end apart: 44 -> 80, of which waited for: 26 -> 33; matrix products, arithmetic and copies ran while one was open for 40% -> 8% of each run, Pallas kernels for 15% -> 43%
where the time goes in v3:
time: 713 us; the launch traced here: 704 us
  Pallas kernels  305 us (43%)
  waiting for transfers between devices  273 us (38%)
  starting transfers between devices  41.9 us (6%)
  local copies, waits for them, and re-layouts  27.8 us (4%)
  other arithmetic  24.4 us (3%)
  matrix products  16.3 us (2%)
  between operations  15.6 us (2%)
    ppermute x21, waiting for transfers between devices, ring_hop(): lax.ppermute(values, 'tp', [(i, (i + 1) % count) for i in range(count)])  172 us
    pallas_call x5, Pallas kernels, product(): pl.pallas_call(functools.partial(product_kernel, len(left), [len(parts) f...  63.6 us
    pallas_call x2, Pallas kernels, attend_back(): pl.pallas_call(functools.partial(attend_back_kernel, places, blocks, plac...  58.1 us
    pallas_call x5, Pallas kernels, rows_nt(): pl.pallas_call(functools.partial(rows_nt_kernel, layouts), grid=(width //...  57 us
    pallas_call x2, Pallas kernels, feed_rows(): pl.pallas_call(functools.partial(feed_kernel, count), grid=(steps,), out_...  41.1 us
    ppermute x9, waiting for transfers between devices, shift(): lax.ppermute(values, 'tp', [(i, (i + places) % count) for i in range(coun...  39.1 us
    ppermute x37, waiting for transfers between devices, ctx_swap(): return lax.ppermute(values, CTX, [(i, i ^ mask) for i in range(count)])  35.2 us
    pallas_call x2, Pallas kernels, attend(): pl.pallas_call(functools.partial(attend_kernel, places, blocks, places *...  32.3 us
  transfers between devices with their start and end apart: 80, of which 33 were waited for; matrix products, arithmetic and copies ran while one was open for 8% of the time, Pallas kernels for 43%

profile of v3, /device:TPU:0, one launch (start us, length us, event | category | flops | bytes accessed | tf_op | source)
XLA Modules:
  0.0 703.7 jit_solution(6468392723181412470)
XLA Ops:
  15.9 25.1 %collective-permute-done.refs_1_ = bf16[256,2048]{1,0:T(8,128)(2,1)} collective-permute-done((bf16[256,2048]{1,0:T(8,128)(2,1)S(1)}, bf16[256,2048]{1,0:T(8,128)(2,1)}, u32[]{:S(2)}, u32[]{:S(2)}) %collective-permute-start) | collective-permute-done | bytes 1048608 | tf_op jit(solution)/shard_map/ppermute | solution.py:40
  45.4 23.7 %collective-permute-done.1.refs_2_ = bf16[256,2048]{1,0:T(8,128)(2,1)S(1)} collective-permute-done((bf16[256,2048]{1,0:T(8,128)(2,1)}, bf16[256,2048]{1,0:T(8,128)(2,1)S(1)}, u32[]{:S(2)}, u32[]{:S(2)}) %collective-permute-start.1) | collective-permute-done | bytes 1048608 | tf_op jit(solution)/shard_map/ppermute | solution.py:40
  72.4 15.6 %collective-permute-done.3 = bf16[256,512]{1,0:T(8,128)(2,1)S(1)} collective-permute-done((bf16[256,512]{1,0:T(8,128)(2,1)S(1)}, bf16[256,512]{1,0:T(8,128)(2,1)S(1)}, u32[]{:S(2)}, u32[]{:S(2)}) %collective-permute-start.3) | collective-permute-done | bytes 262176 | tf_op jit(solution)/shard_map/ppermute | solution.py:82
  165.0 16.1 %attend.2 = (bf16[256,512]{1,0:T(8,128)(2,1)}, bf16[256,512]{1,0:T(8,128)(2,1)}, bf16[256,512]{1,0:T(8,128)(2,1)}, bf16[256,512]{1,0:T(8,128)(2,1)}, f32[4,4,512]{2,1,0:T(4,128)}) custom-call(s32[16]{0:T(128)} %stack.101.refs_0_, s32[4,1,256]{2,1,0:T(1,128)} %broadcast_in_dim.24.refs_1_, s32[1,1,256]{2,1,0:T(1,128)} %bitcast.79, ...), custom_call_target="tpu_custom_call" | custom-call | flops 4294967296 | bytes 2097152 | tf_op jit(solution)/shard_map/attend/pallas_call | solution.py:249
  181.1 16.1 %attend.3 = (bf16[256,512]{1,0:T(8,128)(2,1)}, bf16[256,512]{1,0:T(8,128)(2,1)}, bf16[256,512]{1,0:T(8,128)(2,1)}, bf16[256,512]{1,0:T(8,128)(2,1)}, f32[4,4,512]{2,1,0:T(4,128)}) custom-call(s32[16]{0:T(128)} %stack.101.refs_0_, ...), custom_call_target="tpu_custom_call", output_to_operand_aliasing={{0}: (23, {}), {1}: (24, {}), {2}: (25, {}), {3}: (26, {}),... | custom-call | flops 4294967296 | bytes 2097152 | tf_op jit(solution)/shard_map/attend/pallas_call | solution.py:249
  208.2 14.3 %collective-permute-done.21.refs_2_.refs_6_ = bf16[256,512]{1,0:T(8,128)(2,1)S(1)} collective-permute-done((bf16[256,512]{1,0:T(8,128)(2,1)}, bf16[256,512]{1,0:T(8,128)(2,1)S(1)}, u32[]{:S(2)}, u32[]{:S(2)}) %collective-permute-start.21) | collective-permute-done | bytes 262176 | tf_op jit(solution)/shard_map/ppermute | solution.py:82
  240.1 10.7 %collective-permute-done.25.refs_3_ = bf16[256,2048]{1,0:T(8,128)(2,1)} collective-permute-done((bf16[256,2048]{1,0:T(8,128)(2,1)}, bf16[256,2048]{1,0:T(8,128)(2,1)}, u32[]{:S(2)}, u32[]{:S(2)}) %collective-permute-start.25) | collective-permute-done | bytes 1048608 | tf_op jit(solution)/shard_map/ppermute | solution.py:40
  250.8 20.2 %collective-permute-done.23.refs_1_ = bf16[256,2048]{1,0:T(8,128)(2,1)} collective-permute-done((bf16[256,2048]{1,0:T(8,128)(2,1)}, bf16[256,2048]{1,0:T(8,128)(2,1)}, u32[]{:S(2)}, u32[]{:S(2)}) %collective-permute-start.23) | collective-permute-done | bytes 1048608 | tf_op jit(solution)/shard_map/ppermute | solution.py:40
  271.3 20.5 %feed_rows.2 = (bf16[512,2048]{1,0:T(8,128)(2,1)}, bf16[512,2048]{1,0:T(8,128)(2,1)}, bf16[512,2048]{1,0:T(8,128)(2,1)}) custom-call(bf16[256,2048]{1,0:T(8,128)(2,1)} %get-tuple-element.312.refs_0_, bf16[256,2048]{1,0:T(8,128)(2,1)} %collective-permute-done.23.refs_1_, bf16[256,2048]{1,0:T(8,128)(2,1)} %bitcast.64, ...), custom_call_target="tpu_custom_call" | custom-call | flops 12884901888 | bytes 35651584 | tf_op jit(solution)/shard_map/feed_rows/pallas_call | solution.py:557
  297.6 14.1 %rows_nt.6 = (bf16[256,2048]{1,0:T(8,128)(2,1)}, bf16[256,2048]{1,0:T(8,128)(2,1)}) custom-call(bf16[512,2048]{1,0:T(8,128)(2,1)} %get-tuple-element.320.refs_0_.refs_8_, bf16[512,2048]{1,0:T(8,128)(2,1)} %get-tuple-element.322.refs_1_.refs_8_, bf16[2048,2816]{1,0:T(8,128)(2,1)} %all-gather.4.cloned.1.call-done.refs_4_.refs_2_, ...), custom_call_target="tpu_custom_call" | custom-call | flops 8589934592 | bytes 23068672 | tf_op jit(solution)/shard_map/rows_nt/pallas_call | solution.py:623
  311.7 12.9 %collective-permute-done.34.refs_1_.refs_3_ = bf16[256,2048]{1,0:T(8,128)(2,1)S(1)} collective-permute-done((bf16[256,2048]{1,0:T(8,128)(2,1)}, bf16[256,2048]{1,0:T(8,128)(2,1)S(1)}, u32[]{:S(2)}, u32[]{:S(2)}) %collective-permute-start.34) | collective-permute-done | bytes 1048608 | tf_op jit(solution)/shard_map/ppermute | solution.py:40
  325.6 20.6 %feed_rows.3 = (bf16[512,2048]{1,0:T(8,128)(2,1)}, bf16[512,2048]{1,0:T(8,128)(2,1)}, bf16[512,2048]{1,0:T(8,128)(2,1)}) custom-call(bf16[256,2048]{1,0:T(8,128)(2,1)} %collective-permute-done.24.refs_0_.refs_2_, bf16[256,2048]{1,0:T(8,128)(2,1)} %copy-done.58, bf16[256,2048]{1,0:T(8,128)(2,1)} %collective-permute-done.19.refs_2_, ...), custom_call_target="tpu_custom_call" | custom-call | flops 12884901888 | bytes 35651584 | tf_op jit(solution)/shard_map/feed_rows/pallas_call | solution.py:557
  352.3 14.4 %rows_nt.7 = (bf16[256,2048]{1,0:T(8,128)(2,1)}, bf16[256,2048]{1,0:T(8,128)(2,1)}) custom-call(bf16[512,2048]{1,0:T(8,128)(2,1)} %get-tuple-element.296.refs_0_.refs_9_, bf16[512,2048]{1,0:T(8,128)(2,1)} %get-tuple-element.297.refs_1_.refs_9_, bf16[2048,2816]{1,0:T(8,128)(2,1)} %all-gather.4.cloned.1.call-done.refs_4_.refs_2_, ...), custom_call_target="tpu_custom_call" | custom-call | flops 8589934592 | bytes 23068672 | tf_op jit(solution)/shard_map/rows_nt/pallas_call | solution.py:623
  369.2 16.0 %product.5 = bf16[1024,2048]{1,0:T(8,128)(2,1)} custom-call(s32[1]{0:T(128)} %bitcast.29.first_ref, bf16[256,2048]{1,0:T(8,128)(2,1)} %bitcast.65, bf16[256,2048]{1,0:T(8,128)(2,1)} %collective-permute-done.15.refs_3_.refs_1_, bf16[256,2048]{1,0:T(8,128)(2,1)} %collective-permute-done.19.refs_2_, bf16[256,2048]{1,0:T(8,128)(2,1)} %collective-permute-done.25.refs_3_, ...), custom_call_target="tpu_custom_call" | custom-call | flops 8589934592 | bytes 20971520 | tf_op jit(solution)/shard_map/product/pallas_call | solution.py:735
  385.2 11.2 %collective-permute-done.43.one_ref = bf16[256,2048]{1,0:T(8,128)(2,1)S(1)} collective-permute-done((bf16[256,2048]{1,0:T(8,128)(2,1)}, bf16[256,2048]{1,0:T(8,128)(2,1)S(1)}, u32[]{:S(2)}, u32[]{:S(2)}) %collective-permute-start.43) | collective-permute-done | bytes 1048608 | tf_op jit(solution)/shard_map/ppermute | solution.py:40
  404.2 16.2 %product.6 = bf16[1024,2048]{1,0:T(8,128)(2,1)} custom-call(s32[1]{0:T(128)} %bitcast.29.first_ref, bf16[256,2048]{1,0:T(8,128)(2,1)} %get-tuple-element.312.refs_0_, bf16[256,2048]{1,0:T(8,128)(2,1)} %collective-permute-done.23.refs_1_, bf16[256,2048]{1,0:T(8,128)(2,1)} %collective-permute-done.24.refs_0_.refs_2_, bf16[256,2048]{1,0:T(8,128)(2,1)} %copy-done.58, ...), custom_call_target="tpu_custom_call" | custom-call | flops 8589934592 | bytes 20971520 | tf_op jit(solution)/shard_map/product/pallas_call | solution.py:735
  420.4 16.1 %product.7 = bf16[1024,2048]{1,0:T(8,128)(2,1)} custom-call(s32[1]{0:T(128)} %bitcast.29.first_ref, bf16[256,2048]{1,0:T(8,128)(2,1)} %get-tuple-element.312.refs_0_, bf16[256,2048]{1,0:T(8,128)(2,1)} %collective-permute-done.23.refs_1_, bf16[256,2048]{1,0:T(8,128)(2,1)} %collective-permute-done.24.refs_0_.refs_2_, bf16[256,2048]{1,0:T(8,128)(2,1)} %copy-done.58, ...), custom_call_target="tpu_custom_call" | custom-call | flops 8589934592 | bytes 20971520 | tf_op jit(solution)/shard_map/product/pallas_call | solution.py:735
  453.6 13.6 %rows_nt.8 = (bf16[256,2048]{1,0:T(8,128)(2,1)}, bf16[256,2048]{1,0:T(8,128)(2,1)}, bf16[256,2048]{1,0:T(8,128)(2,1)}, bf16[256,2048]{1,0:T(8,128)(2,1)}) custom-call(bf16[512,2048]{1,0:T(8,128)(2,1)} %get-tuple-element.307.refs_8_.refs_0_, bf16[512,2048]{1,0:T(8,128)(2,1)} %get-tuple-element.308.refs_9_.refs_1_, ...), custom_call_target="tpu_custom_call" | custom-call | flops 8589934592 | bytes 16777216 | tf_op jit(solution)/shard_map/rows_nt/pallas_call | solution.py:623
  479.0 29.0 %attend_back.2 = (bf16[4,128,512]{2,1,0:T(8,128)(2,1)}, f32[4,128,256]{2,1,0:T(8,128)}, f32[4,128,256]{2,1,0:T(8,128)}, bf16[4,128,256]{2,1,0:T(8,128)(2,1)}, bf...) custom-call(s32[16]{0:T(128)} %stack.101.refs_0_, s32[4,1,256]{2,1,0:T(1,128)} %broadcast_in_dim.24.refs_1_, ...), custom_call_target="tpu_custom_call" | custom-call | flops 10737418240 | bytes 4194304 | tf_op jit(solution)/shard_map/attend_back/pallas_call | solution.py:406
  516.9 29.1 %attend_back.3 = (bf16[4,128,512]{2,1,0:T(8,128)(2,1)}, f32[4,128,256]{2,1,0:T(8,128)}, f32[4,128,256]{2,1,0:T(8,128)}, bf16[4,128,256]{2,1,0:T(8,128)(2,1)}, bf...) custom-call(s32[16]{0:T(128)} %stack.101.refs_0_, s32[4,1,256]{2,1,0:T(1,128)} %broadcast_in_dim.24.refs_1_, ...), custom_call_target="tpu_custom_call" | custom-call | flops 10737418240 | bytes 4194304 | tf_op jit(solution)/shard_map/attend_back/pallas_call | solution.py:406
  554.0 13.3 %collective-permute-done.60.refs_5_ = bf16[4,128,256]{2,1,0:T(8,128)(2,1)S(1)} collective-permute-done((bf16[4,128,256]{2,1,0:T(8,128)(2,1)S(1)}, bf16[4,128,256]{2,1,0:T(8,128)(2,1)S(1)}, u32[]{:S(2)}, u32[]{:S(2)}) %collective-permute-start.60) | collective-permute-done | bytes 262176 | tf_op jit(solution)/shard_map/ppermute | solution.py:45
  602.4 14.2 %collective-permute-done.65 = bf16[256,512]{1,0:T(8,128)(2,1)S(1)} collective-permute-done((bf16[256,512]{1,0:T(8,128)(2,1)S(1)}, bf16[256,512]{1,0:T(8,128)(2,1)S(1)}, u32[]{:S(2)}, u32[]{:S(2)}) %collective-permute-start.65) | collective-permute-done | bytes 262176 | tf_op jit(solution)/shard_map/ppermute | solution.py:40
  627.5 22.7 %collective-permute-done.67 = bf16[256,512]{1,0:T(8,128)(2,1)S(1)} collective-permute-done((bf16[256,512]{1,0:T(8,128)(2,1)S(1)}, bf16[256,512]{1,0:T(8,128)(2,1)S(1)}, u32[]{:S(2)}, u32[]{:S(2)}) %collective-permute-start.67) | collective-permute-done | bytes 262176 | tf_op jit(solution)/shard_map/ppermute | solution.py:40
  659.1 15.5 %reduce-scatter.14.cloned.1.call-done = bf16[256,768]{1,0:T(8,128)(2,1)} async-done(((bf16[2048,768]{1,0:T(8,128)(2,1)}), bf16[256,768]{1,0:T(8,128)(2,1)}) %reduce-scatter.14.cloned.1.call-update) | async-done | bytes 393232 | tf_op jit(solution)/shard_map/reduce_scatter | solution.py:1089
  (405 shorter events, 266.7 us)
Async XLA Ops:
  7.2 90.4 %all-gather.4.cloned.1.call-start = ((), (), s32[]{:S(2)}) async-start(), calls=%async_computation.5 | async-start | bytes 12976128 | tf_op jit(solution)/shard_map/all_gather | solution.py:67
  11.5 212.8 %all-gather.6.cloned.1.call-start = ((), (), s32[]{:S(2)}) async-start(), calls=%async_computation.6 | async-start | bytes 18874368 | tf_op jit(solution)/shard_map/all_gather | solution.py:67
  44.8 43.1 %collective-permute-start.3 = (bf16[256,512]{1,0:T(8,128)(2,1)S(1)}, bf16[256,512]{1,0:T(8,128)(2,1)S(1)}, u32[]{:S(2)}, u32[]{:S(2)}) collective-permute-start(bf16[256,512]{1,0:T(8,128)(2,1)S(1)} %bitcast.71), channel_id=1, source_target_pairs={{0,2},{1,3},{2,0},{3,1},{4,6},{5,7},{6,4},{7,5},{8,10},{9,11},{10,... | collective-permute-start | bytes 786440 | tf_op jit(solution)/shard_map/ppermute | solution.py:82
  44.8 43.1 %collective-permute-start.4 = (bf16[256,512]{1,0:T(8,128)(2,1)S(1)}, bf16[256,512]{1,0:T(8,128)(2,1)S(1)}, u32[]{:S(2)}, u32[]{:S(2)}) collective-permute-start(bf16[256,512]{1,0:T(8,128)(2,1)S(1)} %bitcast.72), channel_id=1, source_target_pairs={{0,1},{1,2},{2,3},{3,0},{4,5},{5,6},{6,7},{7,4},{8,9},{9,10},{10,1... | collective-permute-start | bytes 786440 | tf_op jit(solution)/shard_map/ppermute | solution.py:82
  92.1 179.2 %all-gather.8.cloned.1.call-start = ((), (), s32[]{:S(2)}) async-start(), calls=%async_computation.7 | async-start | bytes 9437184 | tf_op jit(solution)/shard_map/all_gather | solution.py:67
  131.2 381.6 %reduce-scatter.6.cloned.1.call-start = ((), (), s32[]{:S(2)}) async-start(), calls=%async_computation.8 | async-start | bytes 5242880 | tf_op jit(solution)/shard_map/reduce_scatter | solution.py:857
  159.2 38.0 %collective-permute-start.19 = (bf16[256,2048]{1,0:T(8,128)(2,1)}, bf16[256,2048]{1,0:T(8,128)(2,1)}, u32[]{:S(2)}, u32[]{:S(2)}) collective-permute-start(bf16[256,2048]{1,0:T(8,128)(2,1)} %collective-permute-done.15.refs_3_.refs_1_), channel_id=1, source_target_pairs={{0,1},{1,2},{2,3},{3,0},{4,5},{5,6},{6,7},{7,4},{8,9},{9,10},{10,1... | collective-permute-start | bytes 3145736 | tf_op jit(solution)/shard_map/ppermute | solution.py:40
  201.8 36.2 %collective-permute-start.26 = (bf16[256,2048]{1,0:T(8,128)(2,1)S(1)}, bf16[256,2048]{1,0:T(8,128)(2,1)}, u32[]{:S(2)}, u32[]{:S(2)}) collective-permute-start(bf16[256,2048]{1,0:T(8,128)(2,1)S(1)} %bitcast.68), channel_id=1, source_target_pairs={{0,4},{4,0},{8,12},{12,8},{1,5},{5,1},{9,13},{13,9},{2,6},{6,2},{1... | collective-permute-start | bytes 3145736 | tf_op jit(solution)/shard_map/ppermute | solution.py:45
  201.8 36.7 %collective-permute-start.27 = (bf16[256,2048]{1,0:T(8,128)(2,1)}, bf16[256,2048]{1,0:T(8,128)(2,1)}, u32[]{:S(2)}, u32[]{:S(2)}) collective-permute-start(bf16[256,2048]{1,0:T(8,128)(2,1)} %collective-permute-done.15.refs_3_.refs_1_), channel_id=1, source_target_pairs={{0,4},{4,0},{8,12},{12,8},{1,5},{5,1},{9,13},{13,9},{2,6},{6,2},{1... | collective-permute-start | bytes 3145736 | tf_op jit(solution)/shard_map/ppermute | solution.py:45
  235.7 35.4 %collective-permute-start.23 = (bf16[256,2048]{1,0:T(8,128)(2,1)}, bf16[256,2048]{1,0:T(8,128)(2,1)}, u32[]{:S(2)}, u32[]{:S(2)}) collective-permute-start(bf16[256,2048]{1,0:T(8,128)(2,1)} %get-tuple-element.312.refs_0_), channel_id=1, source_target_pairs={{0,1},{1,2},{2,3},{3,0},{4,5},{5,6},{6,7},{7,4},{8,9},{9,10},{10,1... | collective-permute-start | bytes 3145736 | tf_op jit(solution)/shard_map/ppermute | solution.py:40
  238.5 53.4 %collective-permute-start.28 = (bf16[256,2048]{1,0:T(8,128)(2,1)}, bf16[256,2048]{1,0:T(8,128)(2,1)S(1)}, u32[]{:S(2)}, u32[]{:S(2)}) collective-permute-start(bf16[256,2048]{1,0:T(8,128)(2,1)} %collective-permute-done.19.refs_2_), channel_id=1, source_target_pairs={{0,4},{4,0},{8,12},{12,8},{1,5},{5,1},{9,13},{13,9},{2,6},{6,2},{1... | collective-permute-start | bytes 3145736 | tf_op jit(solution)/shard_map/ppermute | solution.py:45
  239.6 52.3 %collective-permute-start.32 = (bf16[256,512]{1,0:T(8,128)(2,1)S(1)}, bf16[256,512]{1,0:T(8,128)(2,1)S(1)}, u32[]{:S(2)}, u32[]{:S(2)}) collective-permute-start(bf16[256,512]{1,0:T(8,128)(2,1)S(1)} %copy-done.11), channel_id=1, source_target_pairs={{0,4},{4,0},{8,12},{12,8},{1,5},{5,1},{9,13},{13,9},{2,6},{6,2},{1... | collective-permute-start | bytes 786440 | tf_op jit(solution)/shard_map/ppermute | solution.py:45
  239.9 51.9 %collective-permute-start.33 = (bf16[256,512]{1,0:T(8,128)(2,1)S(1)}, bf16[256,512]{1,0:T(8,128)(2,1)S(1)}, u32[]{:S(2)}, u32[]{:S(2)}) collective-permute-start(bf16[256,512]{1,0:T(8,128)(2,1)S(1)} %copy-done.13), channel_id=1, source_target_pairs={{0,4},{4,0},{8,12},{12,8},{1,5},{5,1},{9,13},{13,9},{2,6},{6,2},{1... | collective-permute-start | bytes 786440 | tf_op jit(solution)/shard_map/ppermute | solution.py:45
  250.8 41.1 %collective-permute-start.29 = (bf16[256,2048]{1,0:T(8,128)(2,1)}, bf16[256,2048]{1,0:T(8,128)(2,1)}, u32[]{:S(2)}, u32[]{:S(2)}) collective-permute-start(bf16[256,2048]{1,0:T(8,128)(2,1)} %collective-permute-done.25.refs_3_), channel_id=1, source_target_pairs={{0,4},{4,0},{8,12},{12,8},{1,5},{5,1},{9,13},{13,9},{2,6},{6,2},{1... | collective-permute-start | bytes 3145736 | tf_op jit(solution)/shard_map/ppermute | solution.py:45
  297.0 49.2 %collective-permute-start.39 = (bf16[256,2048]{1,0:T(8,128)(2,1)}, bf16[256,2048]{1,0:T(8,128)(2,1)}, u32[]{:S(2)}, u32[]{:S(2)}) collective-permute-start(bf16[256,2048]{1,0:T(8,128)(2,1)} %get-tuple-element.312.refs_0_), channel_id=1, source_target_pairs={{0,4},{4,0},{8,12},{12,8},{1,5},{5,1},{9,13},{13,9},{2,6},{6,2},{1... | collective-permute-start | bytes 3145736 | tf_op jit(solution)/shard_map/ppermute | solution.py:45
  397.4 175.3 %reduce-scatter.8.cloned.1.call-start = ((), (), s32[]{:S(2)}) async-start(), calls=%async_computation.9 | async-start | bytes 5242880 | tf_op jit(solution)/shard_map/reduce_scatter | solution.py:857
  400.4 36.1 %collective-permute-start.45 = (bf16[256,2048]{1,0:T(8,128)(2,1)}, bf16[256,2048]{1,0:T(8,128)(2,1)S(1)}, u32[]{:S(2)}, u32[]{:S(2)}) collective-permute-start(bf16[256,2048]{1,0:T(8,128)(2,1)} %add_rows.7), channel_id=1, source_target_pairs={{0,1},{1,2},{2,3},{3,0},{4,5},{5,6},{6,7},{7,4},{8,9},{9,10},{10,1... | collective-permute-start | bytes 3145736 | tf_op jit(solution)/shard_map/ppermute | solution.py:40
  437.5 140.3 %reduce-scatter.10.cloned.1.call-start = ((), (), s32[]{:S(2)}) async-start(), calls=%async_computation.10 | async-start | bytes 5242880 | tf_op jit(solution)/shard_map/reduce_scatter | solution.py:857
  476.2 175.7 %reduce-scatter.12.cloned.1.call-start = ((), (), s32[]{:S(2)}) async-start(), calls=%async_computation.11 | async-start | bytes 5242880 | tf_op jit(solution)/shard_map/reduce_scatter | solution.py:857
  476.9 197.6 %reduce-scatter.14.cloned.1.call-start = ((), (), s32[]{:S(2)}) async-start(), calls=%async_computation.12 | async-start | bytes 3538944 | tf_op jit(solution)/shard_map/reduce_scatter | solution.py:1089
  508.1 37.9 %collective-permute-start.54 = (bf16[4,128,256]{2,1,0:T(8,128)(2,1)}, bf16[4,128,256]{2,1,0:T(8,128)(2,1)S(1)}, u32[]{:S(2)}, u32[]{:S(2)}) collective-permute-start(bf16[4,128,256]{2,1,0:T(8,128)(2,1)} %get-tuple-element.374), channel_id=1, source_target_pairs={{0,4},{4,0},{8,12},{12,8},{1,5},{5,1},{9,13},{13,9},{2,6},{6,2},{1... | collective-permute-start | bytes 786440 | tf_op jit(solution)/shard_map/ppermute | solution.py:45
  511.0 36.0 %collective-permute-start.56 = (bf16[4,128,256]{2,1,0:T(8,128)(2,1)S(1)}, bf16[4,128,256]{2,1,0:T(8,128)(2,1)S(1)}, u32[]{:S(2)}, u32[]{:S(2)}) collective-permute-start(bf16[4,128,256]{2,1,0:T(8,128)(2,1)S(1)} %add_convert_fusion.4), channel_id=1, source_target_pairs={{0,8},{4,12},{8,0},{12,4},{1,9},{5,13},{9,1},{13,5},{2,10},{6,14},... | collective-permute-start | bytes 786440 | tf_op jit(solution)/shard_map/ppermute | solution.py:45
  515.3 31.7 %collective-permute-start.53 = (bf16[256,2048]{1,0:T(8,128)(2,1)}, bf16[256,2048]{1,0:T(8,128)(2,1)S(1)}, u32[]{:S(2)}, u32[]{:S(2)}) collective-permute-start(bf16[256,2048]{1,0:T(8,128)(2,1)} %add_rows.8), channel_id=1, source_target_pairs={{0,1},{1,2},{2,3},{3,0},{4,5},{5,6},{6,7},{7,4},{8,9},{9,10},{10,1... | collective-permute-start | bytes 3145736 | tf_op jit(solution)/shard_map/ppermute | solution.py:40
  620.2 31.8 %collective-permute-start.66 = (bf16[256,2048]{1,0:T(8,128)(2,1)}, bf16[256,2048]{1,0:T(8,128)(2,1)}, u32[]{:S(2)}, u32[]{:S(2)}) collective-permute-start(bf16[256,2048]{1,0:T(8,128)(2,1)} %add_rows.10), channel_id=1, source_target_pairs={{0,1},{1,2},{2,3},{3,0},{4,5},{5,6},{6,7},{7,4},{8,9},{9,10},{10,1... | collective-permute-start | bytes 3145736 | tf_op jit(solution)/shard_map/ppermute | solution.py:40
  (135 other events, 2035.4 us)
Sparse Core Ops, SparseCore 0:
  11.6 70.3 all-gather.3
  92.2 99.2 all-gather.5
  194.1 54.4 all-gather.7
  396.5 50.9 reduce-scatter.5
  450.6 52.6 reduce-scatter.7
  506.2 62.6 reduce-scatter.9
  572.2 52.7 reduce-scatter.11
  628.3 46.2 reduce-scatter.13

commit v4 on v3

--- a/solution.py
+++ b/solution.py
@@ -174,7 +174,9 @@
     for i in range(bias_ref.shape[0] // piece):
         place = starts_ref[i] + lax.broadcasted_iota(jnp.int32, (piece, low.shape[1]), 0)
         linked = (place >= low) & (place <= high)
-        bias_ref[i * piece : (i + 1) * piece, :] = jnp.where(linked, 0.0, MASKED)
+        bias = jnp.where(linked, 0.0, MASKED)
+        bias_ref[i * piece : (i + 1) * piece, : low.shape[1]] = bias
+        bias_ref[i * piece : (i + 1) * piece, low.shape[1] :] = bias
 
 
 def attend_kernel(places, blocks, block_keys, skip, *refs):
@@ -207,22 +209,15 @@
         head = first // HD // group
         queries = apart(jnp.concatenate([q_ref[:, first : first + pair] for q_ref in q_refs], axis=0))
 
-        def step(block, carry):
-            mixed, total = carry
-            where = pl.ds(pl.multiple_of(block * block_keys, block_keys), block_keys)
+        mixed = jnp.zeros((HD, 2 * rows), jnp.float32)
+        total = jnp.zeros((1, 2 * rows), jnp.float32)
+        for block in range(blocks):
+            where = slice(block * block_keys, (block + 1) * block_keys)
             scores = matmul_nt(key_ref[head, where, :], queries)
-            bias = bias_ref[where, :]
-            weight = jnp.exp2(scores * scale + jnp.concatenate([bias, bias], axis=1))
+            weight = jnp.exp2(scores * scale + bias_ref[where, :])
             total = total + jnp.sum(weight, axis=0, keepdims=True)
             values = value_ref[head // 2, head % 2 * HD : (head % 2 + 1) * HD, where]
-            return mixed + matmul(values, weight.astype(jnp.bfloat16)), total
-
-        mixed, total = lax.fori_loop(
-            0,
-            blocks,
-            step,
-            (jnp.zeros((HD, 2 * rows), jnp.float32), jnp.zeros((1, 2 * rows), jnp.float32)),
-        )
+            mixed = mixed + matmul(values, weight.astype(jnp.bfloat16))
         mixed = mixed / total
         out = jnp.concatenate([mixed[:, :rows], mixed[:, rows:]], axis=0).T.astype(jnp.bfloat16)
         for place in range(places):
@@ -266,7 +261,7 @@
         ),
         input_output_aliases={3 + places + len(kv_flat) + i: i for i in range(len(before))},
         scratch_shapes=[
-            pltpu.VMEM((keys, q_rows), jnp.float32),
+            pltpu.VMEM((keys, 2 * q_rows), jnp.float32),
             pltpu.VMEM((k_cols // HD, keys, 2 * HD), jnp.bfloat16),
             pltpu.VMEM((k_cols // HD // 2, 2 * HD, keys), jnp.bfloat16),
         ],
@@ -284,10 +279,11 @@
     q_refs, refs = refs[:places], refs[places:]
     raw_refs, refs = refs[:places], refs[places:]
     grad_refs, refs = refs[:places], refs[places:]
+    mixed_refs, refs = refs[:places], refs[places:]
     kv_refs, refs = refs[: blocks * places], refs[blocks * places :]
     dq_ref, refs = refs[0], refs[1:]
     dkv_refs, refs = refs[:blocks], refs[blocks:]
-    gain_sum_ref, bias_ref, key_ref, turned_ref, value_ref, prob_ref, dprob_ref, dkey_ref, dvalue_ref = refs
+    gain_sum_ref, bias_ref, key_ref, turned_ref, value_ref, dkey_ref, dvalue_ref = refs
     pair = 2 * HD
     piece, q_cols = q_refs[0].shape
     rows = places * piece
@@ -321,22 +317,15 @@
         grads = apart(jnp.concatenate([g_ref[:, first : first + pair] for g_ref in grad_refs], axis=0))
         total = total_ref[0, first // pair : first // pair + 1, :]
 
-        def look(block, delta):
-            where = pl.ds(pl.multiple_of(block * block_keys, block_keys), block_keys)
+        mixed = apart(jnp.concatenate([m_ref[:, first : first + pair] for m_ref in mixed_refs], axis=0))
+        delta = jnp.sum((grads.astype(jnp.float32) * mixed.astype(jnp.float32)).T, axis=0, keepdims=True)
+        dquery = jnp.zeros((HD, 2 * rows), jnp.float32)
+        for block in range(blocks):
+            where = slice(block * block_keys, (block + 1) * block_keys)
             scores = matmul_nt(key_ref[head, where, :], queries)
-            bias = bias_ref[where, :]
-            prob = jnp.exp2(scores * scale + jnp.concatenate([bias, bias], axis=1) - total)
             dprob = matmul_nt(value_ref[head, where, :], grads)
-            prob_ref[where, :] = prob
-            dprob_ref[where, :] = dprob
-            return delta + jnp.sum(prob * dprob, axis=0, keepdims=True)
-
-        delta = lax.fori_loop(0, blocks, look, jnp.zeros((1, 2 * rows), jnp.float32))
-
-        def step(block, dquery):
-            where = pl.ds(pl.multiple_of(block * block_keys, block_keys), block_keys)
-            prob = prob_ref[where, :]
-            dscore = (prob * (dprob_ref[where, :] - delta)).astype(jnp.bfloat16)
+            prob = jnp.exp2(scores * scale + bias_ref[where, :] - total)
+            dscore = (prob * (dprob - delta)).astype(jnp.bfloat16)
             dvalue = matmul(prob.astype(jnp.bfloat16), grads)
             dkey = matmul(dscore, queries)
             if fresh:
@@ -346,9 +335,8 @@
                 dvalue_ref[head, where, :] += dvalue
                 dkey_ref[head, where, :] += dkey
             keys = turned_ref[head // 2, head % 2 * HD : (head % 2 + 1) * HD, where]
-            return dquery + matmul(keys, dscore)
-
-        dquery = lax.fori_loop(0, blocks, step, jnp.zeros((HD, 2 * rows), jnp.float32)) * inv_root
+            dquery = dquery + matmul(keys, dscore)
+        dquery = dquery * inv_root
         dquery = jnp.concatenate([dquery[:, :rows], dquery[:, rows:]], axis=0).T
         raw = jnp.concatenate([raw_ref[:, first : first + pair] for raw_ref in raw_refs], axis=0)
         dq, addend = turn_back(
@@ -380,6 +368,7 @@
     q_chunks,
     raw_chunks,
     grad_chunks,
+    mixed_chunks,
     kv_blocks,
     kinds,
     batch,
@@ -420,7 +409,7 @@
             turn_spec,
             pl.BlockSpec((1, 2 * HD), lambda b: (0, 0)),
         ]
-        + [q_spec] * (3 * places)
+        + [q_spec] * (4 * places)
         + [kv_spec] * len(kv_flat),
         out_specs=tuple(
             [pl.BlockSpec((places, piece, q_cols), lambda b: (0, b, 0))]
@@ -428,12 +417,10 @@
             + [pl.BlockSpec((8, 2 * HD), lambda b: (0, 0))]
         ),
         scratch_shapes=[
-            pltpu.VMEM((keys, q_rows), jnp.float32),
+            pltpu.VMEM((keys, 2 * q_rows), jnp.float32),
             pltpu.VMEM((k_heads, keys, 2 * HD), jnp.bfloat16),
             pltpu.VMEM((k_heads // 2, 2 * HD, keys), jnp.bfloat16),
             pltpu.VMEM((k_heads, keys, 2 * HD), jnp.bfloat16),
-            pltpu.VMEM((keys, 2 * q_rows), jnp.float32),
-            pltpu.VMEM((keys, 2 * q_rows), jnp.float32),
             pltpu.VMEM((k_heads, keys, 2 * HD), jnp.float32),
             pltpu.VMEM((k_heads, keys, 2 * HD), jnp.float32),
         ],
@@ -452,6 +439,7 @@
         *q_chunks,
         *raw_chunks,
         *grad_chunks,
+        *mixed_chunks,
         *kv_flat,
     )
     return results[0], list(results[1:-1]), results[-1]
@@ -607,15 +595,18 @@
         out_ref[...] = result[i * rows : (i + 1) * rows].astype(out_ref.dtype)
 
 
-def rows_nt(addends, kind, outs=1, tile=512):
+def rows_nt(addends, kind, outs, rows_each, tile=512):
     layouts, parts, depths = [], [], []
     for lines, _ in addends:
         layouts.append((len(lines), len(lines[0])))
         parts.extend(part for line in lines for part in line)
-        depths.append(sum(part.shape[1] for part in lines[0]))
-    rows = sum(line[0].shape[0] for line in addends[0][0])
+        depths.append(sum(part[0].shape[1] for part in lines[0]))
+    rows = rows_each * len(addends[0][0])
     weights = [weight for _, weight in addends]
     width = weights[0][0].shape[0]
+
+    def part_spec(part):
+        return pl.BlockSpec((rows_each, part[0].shape[1]), lambda j: (part[1], 0))
 
     def weight_spec(weight, depth):
         return pl.BlockSpec((tile, depth), lambda j: (j, weight[1]))
@@ -624,7 +615,7 @@
         functools.partial(rows_nt_kernel, layouts),
         grid=(width // tile,),
         out_shape=tuple([jax.ShapeDtypeStruct((rows // outs, width), kind)] * outs),
-        in_specs=[pl.BlockSpec(part.shape, lambda j: (0, 0)) for part in parts]
+        in_specs=[part_spec(part) for part in parts]
         + [weight_spec(weight, depth) for weight, depth in zip(weights, depths)],
         out_specs=tuple([pl.BlockSpec((rows // outs, tile), lambda j: (0, j))] * outs),
         scratch_shapes=[pltpu.VMEM((rows, depth), jnp.bfloat16) for depth in depths],
@@ -634,7 +625,7 @@
             transcendentals=0,
         ),
         name="rows_nt",
-    )(*parts, *[weight[0] for weight in weights])
+    )(*[part[0] for part in parts], *[weight[0] for weight in weights])
     return list(results)
 
 
@@ -908,16 +899,18 @@
         return values, query_rot, blocks
 
     tokens = block_in.reshape(rows, width)
-    normed_rows, heads = [unit_of(tokens.astype(jnp.float32))[0].astype(jnp.bfloat16)], []
+    normed = unit_of(tokens.astype(jnp.float32))[0].astype(jnp.bfloat16)
+    normed, out_own = together(normed, output_weight.T)
+    normed_rows, heads = [normed], []
+    out_pieces = [out_own]
+    for _ in range(1, tp_count):
+        out_pieces.append(shift(out_pieces[-1], -1))
     for place in range(1, tp_count):
         came = ring_hop(normed_rows[-1])
-        ready = range(tp_count - 1) if place == tp_count - 1 else []
+        ready = range(tp_count - 2) if place == tp_count - 1 else []
         work = [project_and_send(mine) for mine in ready]
         came, work = together(came, work)
         if place == 1:
-            came, out_own = together(came, output_weight.T)
-            out_pieces = [out_own] + [shift(out_own, -other) for other in range(1, tp_count)]
-        if place == 2:
             came, out_pieces = together(came, out_pieces)
             second_weight = jnp.concatenate(
                 [*out_pieces, (up_weight.astype(jnp.float32) * hidden_gain_rows).astype(jnp.bfloat16)],
@@ -954,7 +947,7 @@
     for _ in range(len(grad_rows), tp_count):
         grad_rows.append(ring_hop(grad_rows[-1]))
     met_grads = meet(grad_rows)
-    (mixed_in,) = rows_nt([([mine], full_out)], jnp.float32)
+    (mixed_in,) = rows_nt([([[(piece, 0) for piece in mine]], full_out)], jnp.float32, 1, rows)
     met_mine = [meet([piece]) for piece in mine]
     hidden, unit_hidden = add_and_norm(tokens, mixed_in)
 
@@ -969,7 +962,9 @@
         )
 
     def hidden_terms(fed):
-        return rows_nt([([[fed[1]]], full_gate), ([[fed[2]]], full_up)], jnp.bfloat16, 2)
+        halves = range(tp_count // 2)
+        gates, ups = ([[(fed[part], half)] for half in halves] for part in (1, 2))
+        return rows_nt([(gates, full_gate), (ups, full_up)], jnp.bfloat16, len(halves), rows)
 
     first, second = list(places)[: tp_count // 2], list(places)[tp_count // 2 :]
     hidden_rows = [unit_hidden]
@@ -988,19 +983,23 @@
     came = ring_hop(terms_first[1])
     met_hidden = meet(hidden_rows)
     fed_second = feed(second)
-    came, fed_second, met_hidden = together(came, fed_second, met_hidden)
+    feed_terms = rows_nt([([[(fed_first[0], 1)]], full_down)], jnp.bfloat16, 1, rows)
+    came, fed_second, met_hidden, feed_terms = together(came, fed_second, met_hidden, feed_terms)
+    feed_came = ring_hop(feed_terms[0])
     met_fed = [old + meet([fed]) for old, fed in zip(met_first, fed_second)]
     if paired:
         met_fed = [[fed[0], fed[2], fed[1], fed[3]] for fed in met_fed]
-    terms_second = hidden_terms(fed_second)
+    terms_second, feed_came = together(hidden_terms(fed_second), feed_came)
     came = ring_hop(add_rows(came, terms_second[0]))
     down_product = grad_product(met_grads, [met_fed[0]])
     came, down_product = together(came, down_product)
     came = ring_hop(add_rows(came, terms_second[1]))
     down_shard = scatter_sum(down_product)
     gate_product = grad_product(met_hidden, [met_fed[1]])
-    up_product = grad_product(met_hidden, [met_fed[2]])
-    came, gate_product, up_product = together(came, gate_product, up_product)
+    lines = [[(fed_second[0], 0)], [(fed_second[0], 1)], [(fed_first[0], 0)]]
+    feed_rest = rows_nt([(lines, full_down)], jnp.bfloat16, len(lines), rows)
+    came, gate_product, feed_rest = together(came, gate_product, feed_rest)
+    feed_terms = dict(zip(order, feed_terms + feed_rest))
     gate_shard = scatter_sum(gate_product)
 
     grad_hidden, branch = norm_back(
@@ -1009,19 +1008,18 @@
     pieces = split_columns(branch, full_second, 0, tp_count, q_cols)
     grad_att = [pieces[0]] + [shift(pieces[place], place) for place in range(1, tp_count)]
     met_branch = meet([branch])
-    feed_terms = rows_nt(
-        [([[fed_first[0]], [fed_second[0]]], full_down)], jnp.bfloat16, tp_count
-    )
+    up_product = grad_product(met_hidden, [met_fed[2]])
     out_product = grad_product(met_branch, met_mine)
-    grad_att, out_product, feed_terms = together(grad_att, out_product, feed_terms)
+    grad_att, out_product, up_product = together(grad_att, out_product, up_product)
     out_shard = scatter_sum(out_product)
 
     kinds = [jnp.float32] * (len(masks) // 2) + [jnp.bfloat16] * (len(masks) - len(masks) // 2)
     query_gain_sum = jnp.zeros((8, 2 * HD), jnp.float32)
     dq_parts, own_parts, came_parts = [], [], []
-    total = feed_terms[1]
+    came = feed_came
     for step, place in enumerate(order[1:]):
-        came = ring_hop(total)
+        if place:
+            came = ring_hop(add_rows(came, feed_terms[place]))
         if step < 2:
             dq, back, addend = attend_back(
                 starts,
@@ -1034,17 +1032,21 @@
                 queries,
                 raw,
                 grad_att,
+                attended_rows,
                 blocks,
                 kinds,
                 batch,
                 step,
                 2,
             )
-            came, dq, back, addend, grad_att, own_parts, came_parts = together(
-                came, dq, back, addend, grad_att, own_parts, came_parts
-            )
             if step == 0:
-                came, down_shard = together(came, down_shard)
+                came, dq, back, addend, grad_att, down_shard = together(
+                    came, dq, back, addend, grad_att, down_shard
+                )
+            else:
+                dq, back, addend, own_parts, came_parts = together(
+                    dq, back, addend, own_parts, came_parts
+                )
             query_gain_sum = query_gain_sum + addend
             dq_parts.append(dq)
             bit = 1
@@ -1061,36 +1063,39 @@
             grad_qkv, key_gain_sum = heads_back(
                 dq_parts, own_parts, came_parts, raw, cos_wide, sin_wide, k_gain
             )
-            came, grad_qkv, gate_shard, out_shard = together(came, grad_qkv, gate_shard, out_shard)
-        if place:
-            total = add_rows(came, feed_terms[place])
+            came, grad_qkv, gate_shard = together(came, grad_qkv, gate_shard)
     feed_out = came.astype(jnp.float32) + feed_terms[0].astype(jnp.float32)
     block_out = (hidden + feed_out).astype(jnp.bfloat16).reshape(block_in.shape)
 
-    row_terms = rows_nt([([[grad_qkv]], (late_qkv, 0))], jnp.bfloat16, tp_count)
+    def out_hop(total, place):
+        start = back_places[place] * q_cols
+        total = ring_hop(total).astype(jnp.float32) + out_shard[:, start : start + q_cols].astype(
+            jnp.float32
+        )
+        return total.astype(jnp.bfloat16) if place else total
+
+    row_terms = rows_nt(
+        [([[(grad_qkv, place)] for place in places], (late_qkv, 0))], jnp.bfloat16, tp_count, rows
+    )
     up_shard = scatter_sum(up_product)
     head_sums = jnp.stack([query_gain_sum, key_gain_sum]).sum(axis=1).reshape(2, 2, HD).sum(axis=1)
     total = row_terms[1]
-    out_total = out_shard[:, back_places[1] * q_cols : (back_places[1] + 1) * q_cols]
     for step, place in enumerate(order[1:]):
         came = ring_hop(total)
-        start = back_places[place] * q_cols
-        out_total = ring_hop(out_total).astype(jnp.float32) + out_shard[
-            :, start : start + q_cols
-        ].astype(jnp.float32)
-        if place:
-            out_total = out_total.astype(jnp.bfloat16)
         if step == 0:
             head_sums = all_sum(head_sums, (CTX, "dp"))
             qkv_product = product(normed_rows, [[grad_qkv]], grad_qkv.shape[1])
-            came, qkv_product, head_sums, out_total = together(
-                came, qkv_product, head_sums, out_total
-            )
+            came, head_sums, out_shard, qkv_product = together(came, head_sums, out_shard, qkv_product)
             qkv_shard = lax.psum_scatter(qkv_product, ("dp", *CTX), scatter_dimension=0, tiled=True)
+            out_total = out_shard[:, back_places[1] * q_cols : (back_places[1] + 1) * q_cols]
+        else:
+            out_total = out_hop(out_total, order[step])
+            came, out_total = together(came, out_total)
         if step == 1:
-            came, up_shard, out_total = together(came, up_shard, out_total)
+            came, up_shard = together(came, up_shard)
         if place:
             total = add_rows(came, row_terms[place])
+    out_total = out_hop(out_total, 0)
     qkv_sums = qkv_shard.astype(jnp.float32)
     gate_sums, up_sums = gate_shard.astype(jnp.float32), up_shard.astype(jnp.float32)
     attention_sum = jnp.sum(qkv_sums * qkv_weight, axis=1)

time: 713 us -> 685 us (0.961)
  Pallas kernels: 305 us -> 274 us
    pallas_call x2, Pallas kernels: 58.1 us -> 35.7 us  [attend_back(): pl.pallas_call(functools.partial(attend_back_kernel, places, blocks, plac...]
    ppermute x9, waiting for transfers between devices: 39.1 us -> 59.1 us  [shift(): lax.ppermute(values, 'tp', [(i, (i + places) % count) for i in range(coun...]
    pallas_call x2, Pallas kernels: 32.3 us -> 19.8 us  [attend(): pl.pallas_call(functools.partial(attend_kernel, places, blocks, places *...]
    pallas_call x5 -> x6, Pallas kernels: 57 us -> 61.2 us  [rows_nt(): pl.pallas_call(functools.partial(rows_nt_kernel, layouts), grid=(width //...]
    unnamed x166 -> x160, local copies, waits for them, and re-layouts: 16.3 us -> 14.4 us
  transfers between devices with their start and end apart: 80 -> 80, of which waited for: 33 -> 33; matrix products, arithmetic and copies ran while one was open for 8% -> 7% of each run, Pallas kernels for 43% -> 41%
where the time goes in v4:
time: 685 us; the launch traced here: 676 us
  waiting for transfers between devices  276 us (40%)
  Pallas kernels  274 us (40%)
  starting transfers between devices  48.1 us (7%)
  local copies, waits for them, and re-layouts  26.8 us (4%)
  other arithmetic  19.6 us (3%)
  matrix products  16.3 us (2%)
  between operations  15.6 us (2%)
    ppermute x21, waiting for transfers between devices, ring_hop(): lax.ppermute(values, 'tp', [(i, (i + 1) % count) for i in range(count)])  168 us
    pallas_call x5, Pallas kernels, product(): pl.pallas_call(functools.partial(product_kernel, len(left), [len(parts) f...  63.5 us
    pallas_call x6, Pallas kernels, rows_nt(): pl.pallas_call(functools.partial(rows_nt_kernel, layouts), grid=(width //...  61.2 us
    ppermute x9, waiting for transfers between devices, shift(): lax.ppermute(values, 'tp', [(i, (i + places) % count) for i in range(coun...  59.1 us
    pallas_call x2, Pallas kernels, feed_rows(): pl.pallas_call(functools.partial(feed_kernel, count), grid=(steps,), out_...  41.2 us
    pallas_call x2, Pallas kernels, attend_back(): pl.pallas_call(functools.partial(attend_back_kernel, places, blocks, plac...  35.7 us
    ppermute x37, waiting for transfers between devices, ctx_swap(): return lax.ppermute(values, CTX, [(i, i ^ mask) for i in range(count)])  30.5 us
    pallas_call x2, Pallas kernels, attend(): pl.pallas_call(functools.partial(attend_kernel, places, blocks, places *...  19.8 us
  transfers between devices with their start and end apart: 80, of which 33 were waited for; matrix products, arithmetic and copies ran while one was open for 7% of the time, Pallas kernels for 41%

profile of v4, /device:TPU:0, one launch (start us, length us, event | category | flops | bytes accessed | tf_op | source)
XLA Modules:
  0.0 676.3 jit_solution(8843624839287147645)
XLA Ops:
  17.9 28.1 %collective-permute-done.1 = bf16[256,512]{1,0:T(8,128)(2,1)S(1)} collective-permute-done((bf16[256,512]{1,0:T(8,128)(2,1)S(1)}, bf16[256,512]{1,0:T(8,128)(2,1)S(1)}, u32[]{:S(2)}, u32[]{:S(2)}) %collective-permute-start.1) | collective-permute-done | bytes 262176 | tf_op jit(solution)/shard_map/ppermute | solution.py:82
  68.2 20.6 %collective-permute-done.4.refs_2_ = bf16[256,2048]{1,0:T(8,128)(2,1)} collective-permute-done((bf16[256,2048]{1,0:T(8,128)(2,1)}, bf16[256,2048]{1,0:T(8,128)(2,1)}, u32[]{:S(2)}, u32[]{:S(2)}) %collective-permute-start.4) | collective-permute-done | bytes 1048608 | tf_op jit(solution)/shard_map/ppermute | solution.py:40
  150.1 9.9 %attend.2 = (bf16[256,512]{1,0:T(8,128)(2,1)}, bf16[256,512]{1,0:T(8,128)(2,1)}, bf16[256,512]{1,0:T(8,128)(2,1)}, bf16[256,512]{1,0:T(8,128)(2,1)}, f32[4,4,512]{2,1,0:T(4,128)}) custom-call(s32[16]{0:T(128)} %stack.101.refs_0_, s32[4,1,256]{2,1,0:T(1,128)} %broadcast_in_dim.24.refs_1_, s32[1,1,256]{2,1,0:T(1,128)} %bitcast.77, ...), custom_call_target="tpu_custom_call" | custom-call | flops 4294967296 | bytes 2097152 | tf_op jit(solution)/shard_map/attend/pallas_call | solution.py:244
  160.0 9.9 %attend.3 = (bf16[256,512]{1,0:T(8,128)(2,1)}, bf16[256,512]{1,0:T(8,128)(2,1)}, bf16[256,512]{1,0:T(8,128)(2,1)}, bf16[256,512]{1,0:T(8,128)(2,1)}, f32[4,4,512]{2,1,0:T(4,128)}) custom-call(s32[16]{0:T(128)} %stack.101.refs_0_, ...), custom_call_target="tpu_custom_call", output_to_operand_aliasing={{0}: (23, {}), {1}: (24, {}), {2}: (25, {}), {3}: (26, {}),... | custom-call | flops 4294967296 | bytes 2097152 | tf_op jit(solution)/shard_map/attend/pallas_call | solution.py:244
  181.1 15.6 %collective-permute-done.21.refs_2_.refs_6_ = bf16[256,512]{1,0:T(8,128)(2,1)S(1)} collective-permute-done((bf16[256,512]{1,0:T(8,128)(2,1)}, bf16[256,512]{1,0:T(8,128)(2,1)S(1)}, u32[]{:S(2)}, u32[]{:S(2)}) %collective-permute-start.21) | collective-permute-done | bytes 262176 | tf_op jit(solution)/shard_map/ppermute | solution.py:82
  213.1 11.8 %collective-permute-done.25.refs_3_ = bf16[256,2048]{1,0:T(8,128)(2,1)} collective-permute-done((bf16[256,2048]{1,0:T(8,128)(2,1)S(1)}, bf16[256,2048]{1,0:T(8,128)(2,1)}, u32[]{:S(2)}, u32[]{:S(2)}) %collective-permute-start.25) | collective-permute-done | bytes 1048608 | tf_op jit(solution)/shard_map/ppermute | solution.py:40
  224.8 20.4 %collective-permute-done.23.refs_1_ = bf16[256,2048]{1,0:T(8,128)(2,1)} collective-permute-done((bf16[256,2048]{1,0:T(8,128)(2,1)}, bf16[256,2048]{1,0:T(8,128)(2,1)}, u32[]{:S(2)}, u32[]{:S(2)}) %collective-permute-start.23) | collective-permute-done | bytes 1048608 | tf_op jit(solution)/shard_map/ppermute | solution.py:40
  245.2 20.6 %feed_rows.2 = (bf16[512,2048]{1,0:T(8,128)(2,1)}, bf16[512,2048]{1,0:T(8,128)(2,1)}, bf16[512,2048]{1,0:T(8,128)(2,1)}) custom-call(bf16[256,2048]{1,0:T(8,128)(2,1)} %get-tuple-element.318.refs_0_, bf16[256,2048]{1,0:T(8,128)(2,1)} %collective-permute-done.23.refs_1_, bf16[256,2048]{1,0:T(8,128)(2,1)} %bitcast.64, ...), custom_call_target="tpu_custom_call" | custom-call | flops 12884901888 | bytes 35651584 | tf_op jit(solution)/shard_map/feed_rows/pallas_call | solution.py:545
  278.2 14.0 %rows_nt.7 = (bf16[256,2048]{1,0:T(8,128)(2,1)}, bf16[256,2048]{1,0:T(8,128)(2,1)}) custom-call(bf16[512,2048]{1,0:T(8,128)(2,1)} %get-tuple-element.326.refs_0_.refs_1_.refs_8_, bf16[512,2048]{1,0:T(8,128)(2,1)} %get-tuple-element.326.refs_0_.refs_1_.refs_8_, bf16[512,2048]{1,0:T(8,128)(2,1)} %get-tuple-element.352.refs_2_.refs_3_.refs_8_, ...), custom_call_target="tpu_custom_call" | custom-call | flops 8589934592 | bytes 23068672 | tf_op jit(solution)/shard_map/rows_nt/pallas_call | solution.py:614
  300.5 20.6 %feed_rows.3 = (bf16[512,2048]{1,0:T(8,128)(2,1)}, bf16[512,2048]{1,0:T(8,128)(2,1)}, bf16[512,2048]{1,0:T(8,128)(2,1)}) custom-call(bf16[256,2048]{1,0:T(8,128)(2,1)} %collective-permute-done.24.refs_0_.refs_2_, bf16[256,2048]{1,0:T(8,128)(2,1)} %collective-permute-done.34.refs_1_.refs_3_, bf16[256,2048]{1,0:T(8,128)(2,1)} %copy-done.61, ...), custom_call_target="tpu_custom_call" | custom-call | flops 12884901888 | bytes 35651584 | tf_op jit(solution)/shard_map/feed_rows/pallas_call | solution.py:545
  327.8 14.2 %rows_nt.9 = (bf16[256,2048]{1,0:T(8,128)(2,1)}, bf16[256,2048]{1,0:T(8,128)(2,1)}) custom-call(bf16[512,2048]{1,0:T(8,128)(2,1)} %get-tuple-element.297.refs_0_.refs_1_.refs_9_, bf16[512,2048]{1,0:T(8,128)(2,1)} %get-tuple-element.297.refs_0_.refs_1_.refs_9_, bf16[512,2048]{1,0:T(8,128)(2,1)} %get-tuple-element.298.refs_2_.refs_3_.refs_9_, ...), custom_call_target="tpu_custom_call" | custom-call | flops 8589934592 | bytes 23068672 | tf_op jit(solution)/shard_map/rows_nt/pallas_call | solution.py:614
  342.0 13.1 %collective-permute-done.43.one_ref = bf16[256,2048]{1,0:T(8,128)(2,1)S(1)} collective-permute-done((bf16[256,2048]{1,0:T(8,128)(2,1)S(1)}, bf16[256,2048]{1,0:T(8,128)(2,1)S(1)}, u32[]{:S(2)}, u32[]{:S(2)}) %collective-permute-start.43) | collective-permute-done | bytes 1048608 | tf_op jit(solution)/shard_map/ppermute | solution.py:40
  358.3 16.0 %product.5 = bf16[1024,2048]{1,0:T(8,128)(2,1)} custom-call(s32[1]{0:T(128)} %bitcast.29.first_ref, bf16[256,2048]{1,0:T(8,128)(2,1)} %bitcast.65, bf16[256,2048]{1,0:T(8,128)(2,1)} %collective-permute-done.12.refs_3_.refs_1_, bf16[256,2048]{1,0:T(8,128)(2,1)} %copy-done.61, bf16[256,2048]{1,0:T(8,128)(2,1)} %collective-permute-done.25.refs_3_, ...), custom_call_target="tpu_custom_call" | custom-call | flops 8589934592 | bytes 20971520 | tf_op jit(solution)/shard_map/product/pallas_call | solution.py:726
  374.4 10.7 %collective-permute-done.44.one_ref = bf16[256,2048]{1,0:T(8,128)(2,1)} collective-permute-done((bf16[256,2048]{1,0:T(8,128)(2,1)}, bf16[256,2048]{1,0:T(8,128)(2,1)}, u32[]{:S(2)}, u32[]{:S(2)}) %collective-permute-start.44) | collective-permute-done | bytes 1048608 | tf_op jit(solution)/shard_map/ppermute | solution.py:40
  387.7 11.5 %rows_nt.10 = (bf16[256,2048]{1,0:T(8,128)(2,1)}, bf16[256,2048]{1,0:T(8,128)(2,1)}, bf16[256,2048]{1,0:T(8,128)(2,1)}) custom-call(bf16[512,2048]{1,0:T(8,128)(2,1)} %get-tuple-element.314.refs_9_.refs_0_.refs_1_, bf16[512,2048]{1,0:T(8,128)(2,1)} %get-tuple-element.314.refs_9_.refs_0_.refs_1_, ...), custom_call_target="tpu_custom_call" | custom-call | flops 6442450944 | bytes 14680064 | tf_op jit(solution)/shard_map/rows_nt/pallas_call | solution.py:614
  399.3 16.3 %product.6 = bf16[1024,2048]{1,0:T(8,128)(2,1)} custom-call(s32[1]{0:T(128)} %bitcast.29.first_ref, bf16[256,2048]{1,0:T(8,128)(2,1)} %get-tuple-element.318.refs_0_, bf16[256,2048]{1,0:T(8,128)(2,1)} %collective-permute-done.23.refs_1_, bf16[256,2048]{1,0:T(8,128)(2,1)} %collective-permute-done.24.refs_0_.refs_2_, ...), custom_call_target="tpu_custom_call" | custom-call | flops 8589934592 | bytes 20971520 | tf_op jit(solution)/shard_map/product/pallas_call | solution.py:726
  435.0 16.1 %product.8 = bf16[1024,2048]{1,0:T(8,128)(2,1)} custom-call(s32[1]{0:T(128)} %bitcast.29.first_ref, bf16[256,2048]{1,0:T(8,128)(2,1)} %get-tuple-element.318.refs_0_, bf16[256,2048]{1,0:T(8,128)(2,1)} %collective-permute-done.23.refs_1_, bf16[256,2048]{1,0:T(8,128)(2,1)} %collective-permute-done.24.refs_0_.refs_2_, ...), custom_call_target="tpu_custom_call" | custom-call | flops 8589934592 | bytes 20971520 | tf_op jit(solution)/shard_map/product/pallas_call | solution.py:726
  465.1 17.9 %attend_back.2 = (bf16[4,128,512]{2,1,0:T(8,128)(2,1)}, f32[4,128,256]{2,1,0:T(8,128)}, f32[4,128,256]{2,1,0:T(8,128)}, bf16[4,128,256]{2,1,0:T(8,128)(2,1)}, bf...) custom-call(s32[16]{0:T(128)} %stack.101.refs_0_, s32[4,1,256]{2,1,0:T(1,128)} %broadcast_in_dim.24.refs_1_, ...), custom_call_target="tpu_custom_call" | custom-call | flops 10737418240 | bytes 4194304 | tf_op jit(solution)/shard_map/attend_back/pallas_call | solution.py:395
  494.9 17.8 %attend_back.3 = (bf16[4,128,512]{2,1,0:T(8,128)(2,1)}, f32[4,128,256]{2,1,0:T(8,128)}, f32[4,128,256]{2,1,0:T(8,128)}, bf16[4,128,256]{2,1,0:T(8,128)(2,1)}, bf...) custom-call(s32[16]{0:T(128)} %stack.101.refs_0_, s32[4,1,256]{2,1,0:T(1,128)} %broadcast_in_dim.24.refs_1_, ...), custom_call_target="tpu_custom_call" | custom-call | flops 10737418240 | bytes 4194304 | tf_op jit(solution)/shard_map/attend_back/pallas_call | solution.py:395
  518.4 12.7 %collective-permute-done.60.refs_5_ = bf16[4,128,256]{2,1,0:T(8,128)(2,1)S(1)} collective-permute-done((bf16[4,128,256]{2,1,0:T(8,128)(2,1)S(1)}, bf16[4,128,256]{2,1,0:T(8,128)(2,1)S(1)}, u32[]{:S(2)}, u32[]{:S(2)}) %collective-permute-start.60) | collective-permute-done | bytes 262176 | tf_op jit(solution)/shard_map/ppermute | solution.py:45
  558.9 11.9 %collective-permute-done.61.one_ref = bf16[256,2048]{1,0:T(8,128)(2,1)S(1)} collective-permute-done((bf16[256,2048]{1,0:T(8,128)(2,1)}, bf16[256,2048]{1,0:T(8,128)(2,1)S(1)}, u32[]{:S(2)}, u32[]{:S(2)}) %collective-permute-start.61) | collective-permute-done | bytes 1048608 | tf_op jit(solution)/shard_map/ppermute | solution.py:40
  577.8 27.4 %collective-permute-done.66 = bf16[256,512]{1,0:T(8,128)(2,1)} collective-permute-done((bf16[256,512]{1,0:T(8,128)(2,1)S(1)}, bf16[256,512]{1,0:T(8,128)(2,1)}, u32[]{:S(2)}, u32[]{:S(2)}) %collective-permute-start.66) | collective-permute-done | bytes 262176 | tf_op jit(solution)/shard_map/ppermute | solution.py:40
  620.6 23.3 %collective-permute-done.68 = bf16[256,512]{1,0:T(8,128)(2,1)S(1)} collective-permute-done((bf16[256,512]{1,0:T(8,128)(2,1)S(1)}, bf16[256,512]{1,0:T(8,128)(2,1)S(1)}, u32[]{:S(2)}, u32[]{:S(2)}) %collective-permute-start.68) | collective-permute-done | bytes 262176 | tf_op jit(solution)/shard_map/ppermute | solution.py:40
  648.9 9.6 %reduce-scatter.14.cloned.1.call-done = bf16[256,768]{1,0:T(8,128)(2,1)} async-done(((bf16[2048,768]{1,0:T(8,128)(2,1)}), bf16[256,768]{1,0:T(8,128)(2,1)}) %reduce-scatter.14.cloned.1.call-update) | async-done | bytes 393232 | tf_op jit(solution)/shard_map/reduce_scatter | solution.py:1089
  (400 shorter events, 270.7 us)
Async XLA Ops:
  7.2 83.7 %all-gather.4.cloned.1.call-start = ((), (), s32[]{:S(2)}) async-start(), calls=%async_computation.5 | async-start | bytes 12976128 | tf_op jit(solution)/shard_map/all_gather | solution.py:67
  11.5 185.6 %all-gather.6.cloned.1.call-start = ((), (), s32[]{:S(2)}) async-start(), calls=%async_computation.6 | async-start | bytes 18874368 | tf_op jit(solution)/shard_map/all_gather | solution.py:67
  12.8 44.4 %collective-permute-start = (bf16[256,2048]{1,0:T(8,128)(2,1)S(1)}, bf16[256,2048]{1,0:T(8,128)(2,1)}, u32[]{:S(2)}, u32[]{:S(2)}) collective-permute-start(bf16[256,2048]{1,0:T(8,128)(2,1)S(1)} %multiply_convert_fusion.refs_0_), channel_id=1, source_target_pairs={{0,1},{1,2},{2,3},{3,0},{4,5},{5,6},{6,7},{7,4},{8,9},{9,10},{10,1... | collective-permute-start | bytes 3145736 | tf_op jit(solution)/shard_map/ppermute | solution.py:40
  15.9 30.2 %collective-permute-start.1 = (bf16[256,512]{1,0:T(8,128)(2,1)S(1)}, bf16[256,512]{1,0:T(8,128)(2,1)S(1)}, u32[]{:S(2)}, u32[]{:S(2)}) collective-permute-start(bf16[256,512]{1,0:T(8,128)(2,1)S(1)} %bitcast.70), channel_id=1, source_target_pairs={{0,3},{1,0},{2,1},{3,2},{4,7},{5,4},{6,5},{7,6},{8,11},{9,8},{10,9... | collective-permute-start | bytes 786440 | tf_op jit(solution)/shard_map/ppermute | solution.py:82
  63.0 182.2 %all-gather.8.cloned.1.call-start = ((), (), s32[]{:S(2)}) async-start(), calls=%async_computation.7 | async-start | bytes 9437184 | tf_op jit(solution)/shard_map/all_gather | solution.py:67
  116.5 373.3 %reduce-scatter.6.cloned.1.call-start = ((), (), s32[]{:S(2)}) async-start(), calls=%async_computation.8 | async-start | bytes 5242880 | tf_op jit(solution)/shard_map/reduce_scatter | solution.py:848
  174.7 36.3 %collective-permute-start.26 = (bf16[256,2048]{1,0:T(8,128)(2,1)S(1)}, bf16[256,2048]{1,0:T(8,128)(2,1)}, u32[]{:S(2)}, u32[]{:S(2)}) collective-permute-start(bf16[256,2048]{1,0:T(8,128)(2,1)S(1)} %bitcast.68), channel_id=1, source_target_pairs={{0,4},{4,0},{8,12},{12,8},{1,5},{5,1},{9,13},{13,9},{2,6},{6,2},{1... | collective-permute-start | bytes 3145736 | tf_op jit(solution)/shard_map/ppermute | solution.py:45
  174.7 36.8 %collective-permute-start.27 = (bf16[256,2048]{1,0:T(8,128)(2,1)}, bf16[256,2048]{1,0:T(8,128)(2,1)}, u32[]{:S(2)}, u32[]{:S(2)}) collective-permute-start(bf16[256,2048]{1,0:T(8,128)(2,1)} %collective-permute-done.12.refs_3_.refs_1_), channel_id=1, source_target_pairs={{0,4},{4,0},{8,12},{12,8},{1,5},{5,1},{9,13},{13,9},{2,6},{6,2},{1... | collective-permute-start | bytes 3145736 | tf_op jit(solution)/shard_map/ppermute | solution.py:45
  208.8 36.4 %collective-permute-start.23 = (bf16[256,2048]{1,0:T(8,128)(2,1)}, bf16[256,2048]{1,0:T(8,128)(2,1)}, u32[]{:S(2)}, u32[]{:S(2)}) collective-permute-start(bf16[256,2048]{1,0:T(8,128)(2,1)} %get-tuple-element.318.refs_0_), channel_id=1, source_target_pairs={{0,1},{1,2},{2,3},{3,0},{4,5},{5,6},{6,7},{7,4},{8,9},{9,10},{10,1... | collective-permute-start | bytes 3145736 | tf_op jit(solution)/shard_map/ppermute | solution.py:40
  211.5 54.4 %collective-permute-start.28 = (bf16[256,2048]{1,0:T(8,128)(2,1)S(1)}, bf16[256,2048]{1,0:T(8,128)(2,1)}, u32[]{:S(2)}, u32[]{:S(2)}) collective-permute-start(bf16[256,2048]{1,0:T(8,128)(2,1)S(1)} %collective-permute-done.19.refs_2_), channel_id=1, source_target_pairs={{0,4},{4,0},{8,12},{12,8},{1,5},{5,1},{9,13},{13,9},{2,6},{6,2},{1... | collective-permute-start | bytes 3145736 | tf_op jit(solution)/shard_map/ppermute | solution.py:45
  212.5 53.4 %collective-permute-start.32 = (bf16[256,512]{1,0:T(8,128)(2,1)S(1)}, bf16[256,512]{1,0:T(8,128)(2,1)S(1)}, u32[]{:S(2)}, u32[]{:S(2)}) collective-permute-start(bf16[256,512]{1,0:T(8,128)(2,1)S(1)} %copy-done.13), channel_id=1, source_target_pairs={{0,4},{4,0},{8,12},{12,8},{1,5},{5,1},{9,13},{13,9},{2,6},{6,2},{1... | collective-permute-start | bytes 786440 | tf_op jit(solution)/shard_map/ppermute | solution.py:45
  212.8 53.0 %collective-permute-start.33 = (bf16[256,512]{1,0:T(8,128)(2,1)S(1)}, bf16[256,512]{1,0:T(8,128)(2,1)S(1)}, u32[]{:S(2)}, u32[]{:S(2)}) collective-permute-start(bf16[256,512]{1,0:T(8,128)(2,1)S(1)} %copy-done.15), channel_id=1, source_target_pairs={{0,4},{4,0},{8,12},{12,8},{1,5},{5,1},{9,13},{13,9},{2,6},{6,2},{1... | collective-permute-start | bytes 786440 | tf_op jit(solution)/shard_map/ppermute | solution.py:45
  224.8 41.1 %collective-permute-start.29 = (bf16[256,2048]{1,0:T(8,128)(2,1)}, bf16[256,2048]{1,0:T(8,128)(2,1)}, u32[]{:S(2)}, u32[]{:S(2)}) collective-permute-start(bf16[256,2048]{1,0:T(8,128)(2,1)} %collective-permute-done.25.refs_3_), channel_id=1, source_target_pairs={{0,4},{4,0},{8,12},{12,8},{1,5},{5,1},{9,13},{13,9},{2,6},{6,2},{1... | collective-permute-start | bytes 3145736 | tf_op jit(solution)/shard_map/ppermute | solution.py:45
  270.5 28.7 %collective-permute-start.36 = (bf16[512,2048]{1,0:T(8,128)(2,1)}, bf16[512,2048]{1,0:T(8,128)(2,1)}, u32[]{:S(2)}, u32[]{:S(2)}) collective-permute-start(bf16[512,2048]{1,0:T(8,128)(2,1)} %get-tuple-element.326.refs_0_.refs_1_.refs_8_), channel_id=1, source_target_pairs={{0,4},{4,0},{8,12},{12,8},{1,5},{5,1},{9,13},{13,9},{2,6},{6,2},{1... | collective-permute-start | bytes 6291464 | tf_op jit(solution)/shard_map/ppermute | solution.py:45
  271.0 50.2 %collective-permute-start.39 = (bf16[256,2048]{1,0:T(8,128)(2,1)}, bf16[256,2048]{1,0:T(8,128)(2,1)}, u32[]{:S(2)}, u32[]{:S(2)}) collective-permute-start(bf16[256,2048]{1,0:T(8,128)(2,1)} %get-tuple-element.318.refs_0_), channel_id=1, source_target_pairs={{0,4},{4,0},{8,12},{12,8},{1,5},{5,1},{9,13},{13,9},{2,6},{6,2},{1... | collective-permute-start | bytes 3145736 | tf_op jit(solution)/shard_map/ppermute | solution.py:45
  327.6 30.7 %collective-permute-start.45 = (bf16[512,2048]{1,0:T(8,128)(2,1)}, bf16[512,2048]{1,0:T(8,128)(2,1)}, u32[]{:S(2)}, u32[]{:S(2)}) collective-permute-start(bf16[512,2048]{1,0:T(8,128)(2,1)} %get-tuple-element.314.refs_9_.refs_0_.refs_1_), channel_id=1, source_target_pairs={{0,4},{4,0},{8,12},{12,8},{1,5},{5,1},{9,13},{13,9},{2,6},{6,2},{1... | collective-permute-start | bytes 6291464 | tf_op jit(solution)/shard_map/ppermute | solution.py:45
  385.1 151.3 %reduce-scatter.8.cloned.1.call-start = ((), (), s32[]{:S(2)}) async-start(), calls=%async_computation.9 | async-start | bytes 5242880 | tf_op jit(solution)/shard_map/reduce_scatter | solution.py:848
  416.6 154.2 %reduce-scatter.10.cloned.1.call-start = ((), (), s32[]{:S(2)}) async-start(), calls=%async_computation.10 | async-start | bytes 5242880 | tf_op jit(solution)/shard_map/reduce_scatter | solution.py:848
  459.7 149.1 %reduce-scatter.12.cloned.1.call-start = ((), (), s32[]{:S(2)}) async-start(), calls=%async_computation.11 | async-start | bytes 5242880 | tf_op jit(solution)/shard_map/reduce_scatter | solution.py:848
  460.4 198.1 %reduce-scatter.14.cloned.1.call-start = ((), (), s32[]{:S(2)}) async-start(), calls=%async_computation.12 | async-start | bytes 3538944 | tf_op jit(solution)/shard_map/reduce_scatter | solution.py:1089
  493.4 43.1 %collective-permute-start.54 = (bf16[256,2048]{1,0:T(8,128)(2,1)}, bf16[256,2048]{1,0:T(8,128)(2,1)S(1)}, u32[]{:S(2)}, u32[]{:S(2)}) collective-permute-start(bf16[256,2048]{1,0:T(8,128)(2,1)} %add_rows.9), channel_id=1, source_target_pairs={{0,1},{1,2},{2,3},{3,0},{4,5},{5,6},{6,7},{7,4},{8,9},{9,10},{10,1... | collective-permute-start | bytes 3145736 | tf_op jit(solution)/shard_map/ppermute | solution.py:40
  574.3 32.0 %collective-permute-start.65 = (bf16[256,2048]{1,0:T(8,128)(2,1)}, bf16[256,2048]{1,0:T(8,128)(2,1)}, u32[]{:S(2)}, u32[]{:S(2)}) collective-permute-start(bf16[256,2048]{1,0:T(8,128)(2,1)} %add_rows.10), channel_id=1, source_target_pairs={{0,1},{1,2},{2,3},{3,0},{4,5},{5,6},{6,7},{7,4},{8,9},{9,10},{10,1... | collective-permute-start | bytes 3145736 | tf_op jit(solution)/shard_map/ppermute | solution.py:40
  575.3 29.9 %collective-permute-start.66 = (bf16[256,512]{1,0:T(8,128)(2,1)S(1)}, bf16[256,512]{1,0:T(8,128)(2,1)}, u32[]{:S(2)}, u32[]{:S(2)}) collective-permute-start(bf16[256,512]{1,0:T(8,128)(2,1)S(1)} %slice.72), channel_id=1, source_target_pairs={{0,1},{1,2},{2,3},{3,0},{4,5},{5,6},{6,7},{7,4},{8,9},{9,10},{10,1... | collective-permute-start | bytes 786440 | tf_op jit(solution)/shard_map/ppermute | solution.py:40
  611.3 32.7 %collective-permute-start.67 = (bf16[256,2048]{1,0:T(8,128)(2,1)}, bf16[256,2048]{1,0:T(8,128)(2,1)}, u32[]{:S(2)}, u32[]{:S(2)}) collective-permute-start(bf16[256,2048]{1,0:T(8,128)(2,1)} %add_rows.11), channel_id=1, source_target_pairs={{0,1},{1,2},{2,3},{3,0},{4,5},{5,6},{6,7},{7,4},{8,9},{9,10},{10,1... | collective-permute-start | bytes 3145736 | tf_op jit(solution)/shard_map/ppermute | solution.py:40
  (132 other events, 1946.8 us)
Sparse Core Ops, SparseCore 0:
  11.7 70.3 all-gather.3
  84.5 98.2 all-gather.5
  185.3 54.3 all-gather.7
  385.3 50.5 reduce-scatter.5
  439.0 52.6 reduce-scatter.7
  494.5 58.2 reduce-scatter.9
  556.1 52.6 reduce-scatter.11
  612.2 46.2 reduce-scatter.13

commit v5 on v4

--- a/solution.py
+++ b/solution.py
@@ -179,11 +179,11 @@
         bias_ref[i * piece : (i + 1) * piece, low.shape[1] :] = bias
 
 
-def attend_kernel(places, blocks, block_keys, skip, *refs):
+def attend_kernel(places, blocks, block_keys, *refs):
     starts_ref, low_ref, high_ref = refs[:3]
     q_refs = refs[3 : 3 + places]
     kv_refs = refs[3 + places : 3 + places + blocks * places]
-    refs = refs[3 + places + blocks * places + skip :]
+    refs = refs[3 + places + blocks * places :]
     out_refs = refs[:places]
     total_ref, bias_ref, key_ref, value_ref = refs[places:]
     pair = 2 * HD
@@ -225,11 +225,9 @@
         total_ref[0, first // pair, :] = jnp.log2(total)[0]
 
 
-def attend(starts, low, high, q_chunks, kv_blocks, batch, part, parts, before):
+def attend(starts, low, high, q_chunks, kv_blocks, batch):
     places, blocks = len(q_chunks), len(kv_blocks)
     kv_flat = [kv for block in kv_blocks for kv in block]
-    count = batch // parts
-    base = part * count
     rows, q_cols = q_chunks[0].shape
     piece = rows // batch
     kv_cols = kv_flat[0].shape[1]
@@ -237,13 +235,13 @@
     keys = blocks * places * piece
     q_rows = places * piece
     pairs = q_cols // (2 * HD)
-    q_spec = pl.BlockSpec((piece, q_cols), lambda b: (base + b, 0))
-    kv_spec = pl.BlockSpec((piece, kv_cols), lambda b: (base + b, 0))
-    line_spec = pl.BlockSpec((1, 1, q_rows), lambda b: (base + b, 0, 0))
-    work = count * q_cols // HD * q_rows * keys
+    q_spec = pl.BlockSpec((piece, q_cols), lambda b: (b, 0))
+    kv_spec = pl.BlockSpec((piece, kv_cols), lambda b: (b, 0))
+    line_spec = pl.BlockSpec((1, 1, q_rows), lambda b: (b, 0, 0))
+    work = batch * q_cols // HD * q_rows * keys
     results = pl.pallas_call(
-        functools.partial(attend_kernel, places, blocks, places * piece, len(before)),
-        grid=(count,),
+        functools.partial(attend_kernel, places, blocks, places * piece),
+        grid=(batch,),
         out_shape=tuple(
             [jax.ShapeDtypeStruct((rows, q_cols), jnp.bfloat16)] * places
             + [jax.ShapeDtypeStruct((batch, pairs, 2 * q_rows), jnp.float32)]
@@ -254,22 +252,20 @@
             pl.BlockSpec((1, 1, q_rows), lambda b: (0, 0, 0)),
         ]
         + [q_spec] * places
-        + [kv_spec] * len(kv_flat)
-        + [pl.BlockSpec(memory_space=pl.ANY)] * len(before),
+        + [kv_spec] * len(kv_flat),
         out_specs=tuple(
-            [q_spec] * places + [pl.BlockSpec((1, pairs, 2 * q_rows), lambda b: (base + b, 0, 0))]
-        ),
-        input_output_aliases={3 + places + len(kv_flat) + i: i for i in range(len(before))},
+            [q_spec] * places + [pl.BlockSpec((1, pairs, 2 * q_rows), lambda b: (b, 0, 0))]
+        ),
         scratch_shapes=[
             pltpu.VMEM((keys, 2 * q_rows), jnp.float32),
             pltpu.VMEM((k_cols // HD, keys, 2 * HD), jnp.bfloat16),
             pltpu.VMEM((k_cols // HD // 2, 2 * HD, keys), jnp.bfloat16),
         ],
         cost_estimate=pl.CostEstimate(
-            flops=work * 4 * HD * 4, bytes_accessed=count * q_rows * q_cols * 8, transcendentals=work
+            flops=work * 4 * HD * 4, bytes_accessed=batch * q_rows * q_cols * 8, transcendentals=work
         ),
         name="attend",
-    )(starts, low, high, *q_chunks, *kv_flat, *before)
+    )(starts, low, high, *q_chunks, *kv_flat)
     return list(results)
 
 
@@ -372,13 +368,11 @@
     kv_blocks,
     kinds,
     batch,
-    part,
-    parts,
+    base,
+    count,
 ):
     places, blocks = len(q_chunks), len(kv_blocks)
     kv_flat = [kv for block in kv_blocks for kv in block]
-    count = batch // parts
-    base = part * count
     rows, q_cols = q_chunks[0].shape
     piece = rows // batch
     kv_cols = kv_flat[0].shape[1]
@@ -396,8 +390,8 @@
         functools.partial(attend_back_kernel, places, blocks, places * piece),
         grid=(count,),
         out_shape=tuple(
-            [jax.ShapeDtypeStruct((places, rows // parts, q_cols), jnp.bfloat16)]
-            + [jax.ShapeDtypeStruct((places, rows // parts, kv_cols), kind) for kind in kinds]
+            [jax.ShapeDtypeStruct((places, count * piece, q_cols), jnp.bfloat16)]
+            + [jax.ShapeDtypeStruct((places, count * piece, kv_cols), kind) for kind in kinds]
             + [jax.ShapeDtypeStruct((8, 2 * HD), jnp.float32)]
         ),
         in_specs=[
@@ -445,23 +439,31 @@
     return results[0], list(results[1:-1]), results[-1]
 
 
-def heads_back_kernel(places, parts, q_cols, *refs):
+def heads_back_kernel(places, came_counts, q_cols, *refs):
+    parts = len(came_counts)
     dq_refs, refs = refs[:parts], refs[parts:]
     own_refs, refs = refs[:parts], refs[parts:]
-    came_refs, refs = refs[:parts], refs[parts:]
+    came_refs = []
+    for count in came_counts:
+        came_refs.append(refs[:count])
+        refs = refs[count:]
     raw_refs, refs = refs[:places], refs[places:]
     cos_ref, sin_ref, gain_ref, out_ref, gain_sum_ref = refs
     rows = raw_refs[0].shape[0]
-    part_rows = rows // parts
     k_cols = own_refs[0].shape[2] // 2
     pair = 2 * HD
     addends = jnp.zeros((8, pair), jnp.float32)
     for place in range(places):
+        start = 0
         for part in range(parts):
-            mine = slice(part * part_rows, (part + 1) * part_rows)
-            out = slice(place * rows + part * part_rows, place * rows + (part + 1) * part_rows)
+            stop = start + own_refs[part].shape[1]
+            mine = slice(start, stop)
+            out = slice(place * rows + start, place * rows + stop)
+            start = stop
             out_ref[out, :q_cols] = dq_refs[part][place]
-            grads = own_refs[part][place] + came_refs[part][place].astype(jnp.float32)
+            grads = own_refs[part][place]
+            for came_ref in came_refs[part]:
+                grads = grads + came_ref[place].astype(jnp.float32)
             for first in range(0, k_cols, pair):
                 cols = slice(first, first + pair)
                 dk, addend = turn_back(
@@ -486,10 +488,10 @@
     def whole(array):
         return pl.BlockSpec(array.shape, lambda i: (0,) * array.ndim)
 
-    inputs = [*dq_parts, *own_parts, *came_parts]
+    inputs = [*dq_parts, *own_parts, *[came for part in came_parts for came in part]]
     turns = [cos_wide, sin_wide, k_gain]
     return pl.pallas_call(
-        functools.partial(heads_back_kernel, places, parts, q_cols),
+        functools.partial(heads_back_kernel, places, [len(part) for part in came_parts], q_cols),
         grid=(1,),
         out_shape=(
             jax.ShapeDtypeStruct((places * rows, q_cols + kv_cols), jnp.bfloat16),
@@ -678,13 +680,13 @@
     )(rows, weight)
 
 
-def product_kernel(left_count, right_counts, blocks, first_ref, *refs):
+def product_kernel(left_count, right_counts, blocks, skip, first_ref, *refs):
     left_refs, refs = refs[:left_count], refs[left_count:]
     rights = []
     for count in right_counts:
         rights.append(refs[:count])
         refs = refs[count:]
-    out_ref, left, right = refs
+    out_ref, left, right = refs[skip:]
     steps = pl.num_programs(0) // len(rights)
 
     @pl.when(pl.program_id(0) == 0)
@@ -710,13 +712,17 @@
     out_ref[...] = matmul_tn(left[...], right[...]).astype(jnp.bfloat16)
 
 
-def product(left, rights, tile=512, first=None, blocks=0):
+def product(left, rights, tile=512, first=None, blocks=0, more=0, into=None, share=1.0):
     width, cols = left[0].shape[1], rights[0][0].shape[1]
     depth = sum(part.shape[0] for part in left)
     tile = min(tile, cols)
     steps = cols // tile
     out_rows = width // 2 if blocks else width
     first = jnp.zeros((1,), jnp.int32) if first is None else first
+    taken = [] if into is None else [into]
+    out_cols = into.shape[1] if taken else cols * (len(rights) + more)
+    skipped = out_cols // tile - steps * len(rights) if taken else 0
+    operands = 1 + len(left) + sum(len(parts) for parts in rights)
 
     def right_spec(part, index):
         return pl.BlockSpec(
@@ -724,24 +730,28 @@
         )
 
     return pl.pallas_call(
-        functools.partial(product_kernel, len(left), [len(parts) for parts in rights], blocks),
+        functools.partial(
+            product_kernel, len(left), [len(parts) for parts in rights], blocks, len(taken)
+        ),
         grid=(steps * len(rights),),
-        out_shape=jax.ShapeDtypeStruct((out_rows, cols * len(rights)), jnp.bfloat16),
+        out_shape=jax.ShapeDtypeStruct((out_rows, out_cols), jnp.bfloat16),
         in_specs=[pl.BlockSpec(memory_space=pltpu.SMEM)]
         + [pl.BlockSpec(part.shape, lambda j: (0, 0)) for part in left]
-        + [right_spec(part, index) for index, parts in enumerate(rights) for part in parts],
-        out_specs=pl.BlockSpec((out_rows, tile), lambda j: (0, j)),
+        + [right_spec(part, index) for index, parts in enumerate(rights) for part in parts]
+        + [pl.BlockSpec(memory_space=pl.ANY)] * len(taken),
+        out_specs=pl.BlockSpec((out_rows, tile), lambda j: (0, skipped + j)),
+        input_output_aliases={operands: 0} if taken else {},
         scratch_shapes=[
             pltpu.VMEM((depth, out_rows), jnp.bfloat16),
             pltpu.VMEM((depth, tile), jnp.bfloat16),
         ],
         cost_estimate=pl.CostEstimate(
-            flops=2 * depth * out_rows * cols * len(rights),
-            bytes_accessed=2 * (depth * width + (depth + out_rows) * cols * len(rights)),
+            flops=int(share * 2 * depth * out_rows * cols * len(rights)),
+            bytes_accessed=int(share * 2 * (depth * width + (depth + out_rows) * cols * len(rights))),
             transcendentals=0,
         ),
         name="product",
-    )(first, *left, *[part for parts in rights for part in parts])
+    )(first, *left, *[part for parts in rights for part in parts], *taken)
 
 
 def unit_of(values):
@@ -840,8 +850,9 @@
     def meet(arrays):
         return [*arrays, *[ctx_swap(array, 1) for array in arrays]] if paired else list(arrays)
 
-    def grad_product(left, rights, tile=512):
-        return product(left, rights, tile, pair_first, width // block // 2 if paired else 0)
+    def grad_product(left, rights, more=0, into=None, tile=512, share=1.0):
+        blocks = width // block // 2 if paired else 0
+        return product(left, rights, tile, pair_first, blocks, more, into, share)
 
     def scatter_sum(addend):
         axes = ("dp", CTX[0]) if paired else ("dp", *CTX)
@@ -931,15 +942,16 @@
     raw, queries, gathered = ([h[i] for h in heads] for i in range(3))
     blocks = [[gathered[place][i] for place in places] for i in range(len(masks))]
     grad_rows = [grad_own, came]
-    attended = []
-    parts = 2
-    late_qkv = full_qkv
     came = ring_hop(grad_rows[-1])
-    for part in range(parts):
-        attended = attend(starts, low, high, queries, blocks, batch, part, parts, attended)
-        if part == 0:
-            late_qkv, attended = together(late_qkv, attended)
-    came, attended = together(came, attended)
+    attended = attend(starts, low, high, queries, blocks, batch)
+    met_normed, mine_qkv = meet(normed_rows), full_qkv
+    if paired:
+        mine_qkv = lax.dynamic_index_in_dim(
+            full_qkv.reshape(width // block // 2, 2, block, qkv_cols), pair_first[0], 1, False
+        ).reshape(width // 2, qkv_cols)
+    late_qkv, came, attended, met_normed, mine_qkv = together(
+        full_qkv, came, attended, met_normed, mine_qkv
+    )
     grad_rows.append(came)
     attended_rows, totals = attended[:tp_count], attended[tp_count]
     mine = [attended_rows[0]] + [shift(attended_rows[place], -place) for place in range(1, tp_count)]
@@ -992,28 +1004,36 @@
     terms_second, feed_came = together(hidden_terms(fed_second), feed_came)
     came = ring_hop(add_rows(came, terms_second[0]))
     down_product = grad_product(met_grads, [met_fed[0]])
-    came, down_product = together(came, down_product)
+    feed_terms += rows_nt([([[(fed_second[0], 0)]], full_down)], jnp.bfloat16, 1, rows)
+    came, down_product, feed_terms = together(came, down_product, feed_terms)
     came = ring_hop(add_rows(came, terms_second[1]))
     down_shard = scatter_sum(down_product)
-    gate_product = grad_product(met_hidden, [met_fed[1]])
-    lines = [[(fed_second[0], 0)], [(fed_second[0], 1)], [(fed_first[0], 0)]]
-    feed_rest = rows_nt([(lines, full_down)], jnp.bfloat16, len(lines), rows)
-    came, gate_product, feed_rest = together(came, gate_product, feed_rest)
+    pair_product = grad_product(met_hidden, [met_fed[1]], more=1)
+    feed_rest = rows_nt(
+        [([[(fed_second[0], 1)], [(fed_first[0], 0)]], full_down)], jnp.bfloat16, 2, rows
+    )
+    came, pair_product, feed_rest = together(came, pair_product, feed_rest)
     feed_terms = dict(zip(order, feed_terms + feed_rest))
-    gate_shard = scatter_sum(gate_product)
 
     grad_hidden, branch = norm_back(
         came, terms_first[0], hidden, grad_own, (jnp.float32, jnp.bfloat16)
     )
     pieces = split_columns(branch, full_second, 0, tp_count, q_cols)
+    pieces, branch = together(pieces, branch)
     grad_att = [pieces[0]] + [shift(pieces[place], place) for place in range(1, tp_count)]
     met_branch = meet([branch])
-    up_product = grad_product(met_hidden, [met_fed[2]])
-    out_product = grad_product(met_branch, met_mine)
-    grad_att, out_product, up_product = together(grad_att, out_product, up_product)
+    out_product = grad_product(met_branch, met_mine, share=0.1)
+    out_product, pair_product = together(out_product, pair_product)
+    pair_product = grad_product(met_hidden, [met_fed[2]], into=pair_product, share=0.1)
+    grad_att, pair_product, out_product = together(grad_att, pair_product, out_product)
     out_shard = scatter_sum(out_product)
-
-    kinds = [jnp.float32] * (len(masks) // 2) + [jnp.bfloat16] * (len(masks) - len(masks) // 2)
+    pair_shard = scatter_sum(pair_product)
+
+    half_count = len(masks) // 2
+    kinds = [
+        [jnp.float32] * half_count + [jnp.bfloat16] * half_count,
+        [jnp.float32] + [jnp.bfloat16] * (len(masks) - 1),
+    ]
     query_gain_sum = jnp.zeros((8, 2 * HD), jnp.float32)
     dq_parts, own_parts, came_parts = [], [], []
     came = feed_came
@@ -1034,10 +1054,10 @@
                 grad_att,
                 attended_rows,
                 blocks,
-                kinds,
+                kinds[step],
                 batch,
-                step,
-                2,
+                [0, batch - batch // 4][step],
+                [batch - batch // 4, batch // 4][step],
             )
             if step == 0:
                 came, dq, back, addend, grad_att, down_shard = together(
@@ -1049,6 +1069,10 @@
                 )
             query_gain_sum = query_gain_sum + addend
             dq_parts.append(dq)
+            own_parts.append(back[0])
+            if step:
+                came_parts.append([ctx_swap(part, mask) for part, mask in zip(back[1:], masks[1:])])
+                continue
             bit = 1
             while len(back) > 2:
                 half_count = len(back) // 2
@@ -1057,13 +1081,13 @@
                     for i in range(half_count)
                 ]
                 bit *= 2
-            own_parts.append(back[0])
-            came_parts.append(ctx_swap(back[1].astype(jnp.bfloat16), bit))
+            own_parts[0] = back[0]
+            came_parts.append([ctx_swap(back[1].astype(jnp.bfloat16), bit)])
         else:
             grad_qkv, key_gain_sum = heads_back(
                 dq_parts, own_parts, came_parts, raw, cos_wide, sin_wide, k_gain
             )
-            came, grad_qkv, gate_shard = together(came, grad_qkv, gate_shard)
+            came, grad_qkv, out_shard = together(came, grad_qkv, out_shard)
     feed_out = came.astype(jnp.float32) + feed_terms[0].astype(jnp.float32)
     block_out = (hidden + feed_out).astype(jnp.bfloat16).reshape(block_in.shape)
 
@@ -1074,38 +1098,45 @@
         )
         return total.astype(jnp.bfloat16) if place else total
 
+    met_qkv = meet([grad_qkv])
     row_terms = rows_nt(
         [([[(grad_qkv, place)] for place in places], (late_qkv, 0))], jnp.bfloat16, tp_count, rows
     )
-    up_shard = scatter_sum(up_product)
     head_sums = jnp.stack([query_gain_sum, key_gain_sum]).sum(axis=1).reshape(2, 2, HD).sum(axis=1)
-    total = row_terms[1]
+    total, met_qkv = together(row_terms[1], met_qkv)
+    out_total = out_shard[:, back_places[1] * q_cols : (back_places[1] + 1) * q_cols]
     for step, place in enumerate(order[1:]):
         came = ring_hop(total)
+        if step == 2:
+            out_total, pair_shard, qkv_product = together(out_total, pair_shard, qkv_product)
+            qkv_shard = scatter_sum(qkv_product)
+        out_total = out_hop(out_total, place)
+        if step < 2:
+            came, out_total = together(came, out_total)
         if step == 0:
             head_sums = all_sum(head_sums, (CTX, "dp"))
-            qkv_product = product(normed_rows, [[grad_qkv]], grad_qkv.shape[1])
-            came, head_sums, out_shard, qkv_product = together(came, head_sums, out_shard, qkv_product)
-            qkv_shard = lax.psum_scatter(qkv_product, ("dp", *CTX), scatter_dimension=0, tiled=True)
-            out_total = out_shard[:, back_places[1] * q_cols : (back_places[1] + 1) * q_cols]
-        else:
-            out_total = out_hop(out_total, order[step])
-            came, out_total = together(came, out_total)
+            qkv_product = grad_product(met_normed, [met_qkv], tile=qkv_cols)
+            attention_sum = jnp.sum(qkv_product.astype(jnp.float32) * mine_qkv.astype(jnp.float32), axis=1)
+            came, head_sums, qkv_product, attention_sum = together(
+                came, head_sums, qkv_product, attention_sum
+            )
+            small_sums = jnp.concatenate([attention_sum, head_sums.reshape(-1)])
         if step == 1:
-            came, up_shard = together(came, up_shard)
+            small_sums = all_sum(small_sums, ("tp",))
+            came, small_sums = together(came, small_sums)
+            head_sums = small_sums[-2 * HD :].reshape(2, HD)
+            column = jnp.pad(small_sums[: -2 * HD].astype(jnp.bfloat16)[:, None], ((0, 0), (0, 127)))
+            qkv_product = jnp.concatenate([qkv_product, column], axis=1)
         if place:
             total = add_rows(came, row_terms[place])
-    out_total = out_hop(out_total, 0)
-    qkv_sums = qkv_shard.astype(jnp.float32)
-    gate_sums, up_sums = gate_shard.astype(jnp.float32), up_shard.astype(jnp.float32)
-    attention_sum = jnp.sum(qkv_sums * qkv_weight, axis=1)
+    pair_sums = pair_shard.astype(jnp.float32)
+    gate_sums, up_sums = pair_sums[:, :hidden_cols], pair_sums[:, hidden_cols:]
     hidden_sums = jnp.sum(
         gate_sums * gate_weight.astype(jnp.float32) + up_sums * up_weight.astype(jnp.float32), axis=1
     )
-    small_sums = jnp.concatenate([jnp.stack([attention_sum, hidden_sums]), head_sums], axis=1)
-    small_sums = all_sum(small_sums, ("tp",))
-    attention_gain_grad, hidden_gain_grad = small_sums[0, :block], small_sums[1, :block]
-    head_sums = small_sums[:, block:]
+    hidden_gain_grad = all_sum(hidden_sums, ("tp",))
+    qkv_sums = qkv_shard[:, :qkv_cols].astype(jnp.float32)
+    attention_gain_grad = qkv_shard[:, qkv_cols].astype(jnp.float32) / attention_rows[:, 0]
     (input_grad,) = norm_back(came, row_terms[0], tokens, grad_hidden, (jnp.float32,))
     output_grad = out_total.T
     down_grad = down_shard.astype(jnp.float32).T

time: 685 us -> 674 us (0.984)
  waiting for transfers between devices: 276 us -> 239 us
  starting transfers between devices: 48.1 us -> 63.7 us
    ppermute x21, waiting for transfers between devices: 168 us -> 94.5 us  [ring_hop(): lax.ppermute(values, 'tp', [(i, (i + 1) % count) for i in range(count)])]
    ppermute x5 -> x7, waiting for transfers between devices: 5.19 us -> 52.7 us  [all_sum(): lax.ppermute(values, axis, [(i, i ^ bit) for i in range(count)])]
    reduce_scatter x1 -> x0, waiting for transfers between devices: 9.57 us -> none  [per_device(): lax.psum_scatter(qkv_product, ('dp', *CTX), scatter_dimension=0, tiled=True)]
    ppermute x5 -> x7, starting transfers between devices: 6.32 us -> 13.4 us  [all_sum(): lax.ppermute(values, axis, [(i, i ^ bit) for i in range(count)])]
    pallas_call x6 -> x7, Pallas kernels: 61.2 us -> 65.4 us  [rows_nt(): pl.pallas_call(functools.partial(rows_nt_kernel, layouts), grid=(width //...]
    ppermute x37 -> x42, starting transfers between devices: 11.8 us -> 14.6 us  [ctx_swap(): return lax.ppermute(values, CTX, [(i, i ^ mask) for i in range(count)])]
    ppermute x37 -> x42, waiting for transfers between devices: 30.5 us -> 28.6 us  [ctx_swap(): return lax.ppermute(values, CTX, [(i, i ^ mask) for i in range(count)])]
    pallas_call x2 -> x1, Pallas kernels: 19.8 us -> 18 us  [attend(): pl.pallas_call(functools.partial(attend_kernel, places, blocks, places *...]
  transfers between devices with their start and end apart: 80 -> 86, of which waited for: 33 -> 32; matrix products, arithmetic and copies ran while one was open for 7% -> 8% of each run, Pallas kernels for 41% -> 42%
where the time goes in v5:
time: 674 us; the launch traced here: 666 us
  Pallas kernels  279 us (41%)
  waiting for transfers between devices  239 us (35%)
  starting transfers between devices  63.7 us (9%)
  local copies, waits for them, and re-layouts  27.8 us (4%)
  other arithmetic  24.5 us (4%)
  matrix products  16.1 us (2%)
  between operations  15.5 us (2%)
    ppermute x21, waiting for transfers between devices, ring_hop(): lax.ppermute(values, 'tp', [(i, (i + 1) % count) for i in range(count)])  94.5 us
    pallas_call x7, Pallas kernels, rows_nt(): pl.pallas_call(functools.partial(rows_nt_kernel, layouts), grid=(width //...  65.4 us
    pallas_call x5, Pallas kernels, product(): pl.pallas_call(functools.partial(product_kernel, len(left), [len(parts) f...  64.9 us
    ppermute x9, waiting for transfers between devices, shift(): lax.ppermute(values, 'tp', [(i, (i + places) % count) for i in range(coun...  58.4 us
    ppermute x7, waiting for transfers between devices, all_sum(): lax.ppermute(values, axis, [(i, i ^ bit) for i in range(count)])  52.7 us
    pallas_call x2, Pallas kernels, feed_rows(): pl.pallas_call(functools.partial(feed_kernel, count), grid=(steps,), out_...  41.6 us
    pallas_call x2, Pallas kernels, attend_back(): pl.pallas_call(functools.partial(attend_back_kernel, places, blocks, plac...  36.2 us
    ppermute x42, waiting for transfers between devices, ctx_swap(): return lax.ppermute(values, CTX, [(i, i ^ mask) for i in range(count)])  28.6 us
  transfers between devices with their start and end apart: 86, of which 32 were waited for; matrix products, arithmetic and copies ran while one was open for 8% of the time, Pallas kernels for 42%

profile of v5, /device:TPU:0, one launch (start us, length us, event | category | flops | bytes accessed | tf_op | source)
XLA Modules:
  0.0 666.1 jit_solution(5101766473497699742)
XLA Ops:
  17.9 28.1 %collective-permute-done.1 = bf16[256,512]{1,0:T(8,128)(2,1)S(1)} collective-permute-done((bf16[256,512]{1,0:T(8,128)(2,1)S(1)}, bf16[256,512]{1,0:T(8,128)(2,1)S(1)}, u32[]{:S(2)}, u32[]{:S(2)}) %collective-permute-start.1) | collective-permute-done | bytes 262176 | tf_op jit(solution)/shard_map/ppermute | solution.py:82
  70.5 20.4 %collective-permute-done.4.refs_2_ = bf16[256,2048]{1,0:T(8,128)(2,1)} collective-permute-done((bf16[256,2048]{1,0:T(8,128)(2,1)S(1)}, bf16[256,2048]{1,0:T(8,128)(2,1)}, u32[]{:S(2)}, u32[]{:S(2)}) %collective-permute-start.4) | collective-permute-done | bytes 1048608 | tf_op jit(solution)/shard_map/ppermute | solution.py:40
  109.2 7.1 %collective-permute-done.9.refs_12_.refs_28_ = bf16[256,256]{1,0:T(8,128)(2,1)} collective-permute-done((bf16[256,256]{1,0:T(8,128)(2,1)}, bf16[256,256]{1,0:T(8,128)(2,1)}, u32[]{:S(2)}, u32[]{:S(2)}) %collective-permute-start.9) | collective-permute-done | bytes 131104 | tf_op jit(solution)/shard_map/ppermute | solution.py:45
  135.7 7.0 %collective-permute-done.16.refs_14_.refs_30_ = bf16[256,256]{1,0:T(8,128)(2,1)} collective-permute-done((bf16[256,256]{1,0:T(8,128)(2,1)}, bf16[256,256]{1,0:T(8,128)(2,1)}, u32[]{:S(2)}, u32[]{:S(2)}) %collective-permute-start.16) | collective-permute-done | bytes 131104 | tf_op jit(solution)/shard_map/ppermute | solution.py:45
  152.5 18.0 %attend.1 = (bf16[256,512]{1,0:T(8,128)(2,1)}, bf16[256,512]{1,0:T(8,128)(2,1)}, bf16[256,512]{1,0:T(8,128)(2,1)}, bf16[256,512]{1,0:T(8,128)(2,1)}, f32[4,4,512]{2,1,0:T(4,128)}) custom-call(s32[16]{0:T(128)} %stack.92.refs_0_, s32[4,1,256]{2,1,0:T(1,128)} %broadcast_in_dim.27.refs_1_, s32[1,1,256]{2,1,0:T(1,128)} %bitcast.71, ...), custom_call_target="tpu_custom_call" | custom-call | flops 8589934592 | bytes 4194304 | tf_op jit(solution)/shard_map/attend/pallas_call | solution.py:242
  181.5 16.5 %collective-permute-done.25.refs_2_.refs_6_ = bf16[256,512]{1,0:T(8,128)(2,1)S(1)} collective-permute-done((bf16[256,512]{1,0:T(8,128)(2,1)}, bf16[256,512]{1,0:T(8,128)(2,1)S(1)}, u32[]{:S(2)}, u32[]{:S(2)}) %collective-permute-start.25) | collective-permute-done | bytes 262176 | tf_op jit(solution)/shard_map/ppermute | solution.py:82
  215.0 11.3 %collective-permute-done.29.refs_3_ = bf16[256,2048]{1,0:T(8,128)(2,1)} collective-permute-done((bf16[256,2048]{1,0:T(8,128)(2,1)}, bf16[256,2048]{1,0:T(8,128)(2,1)}, u32[]{:S(2)}, u32[]{:S(2)}) %collective-permute-start.29) | collective-permute-done | bytes 1048608 | tf_op jit(solution)/shard_map/ppermute | solution.py:40
  226.3 20.6 %collective-permute-done.27.refs_1_ = bf16[256,2048]{1,0:T(8,128)(2,1)S(1)} collective-permute-done((bf16[256,2048]{1,0:T(8,128)(2,1)}, bf16[256,2048]{1,0:T(8,128)(2,1)S(1)}, u32[]{:S(2)}, u32[]{:S(2)}) %collective-permute-start.27) | collective-permute-done | bytes 1048608 | tf_op jit(solution)/shard_map/ppermute | solution.py:40
  247.9 20.6 %feed_rows.2 = (bf16[512,2048]{1,0:T(8,128)(2,1)}, bf16[512,2048]{1,0:T(8,128)(2,1)}, bf16[512,2048]{1,0:T(8,128)(2,1)}) custom-call(bf16[256,2048]{1,0:T(8,128)(2,1)} %get-tuple-element.325.refs_0_, bf16[256,2048]{1,0:T(8,128)(2,1)} %copy-done.30, bf16[256,2048]{1,0:T(8,128)(2,1)} %bitcast.62, bf16[256,2048]{1,0:T(8,128)(2,1)} %collective-permute-done.12.refs_3_.refs_1_, ...), custom_call_target="tpu_custom_call" | custom-call | flops 12884901888 | bytes 35651584 | tf_op jit(solution)/shard_map/feed_rows/pallas_call | solution.py:547
  280.2 14.1 %rows_nt.8 = (bf16[256,2048]{1,0:T(8,128)(2,1)}, bf16[256,2048]{1,0:T(8,128)(2,1)}) custom-call(bf16[512,2048]{1,0:T(8,128)(2,1)} %get-tuple-element.333.refs_0_.refs_1_.refs_8_, bf16[512,2048]{1,0:T(8,128)(2,1)} %get-tuple-element.333.refs_0_.refs_1_.refs_8_, bf16[512,2048]{1,0:T(8,128)(2,1)} %get-tuple-element.348.refs_2_.refs_3_.refs_8_, ...), custom_call_target="tpu_custom_call" | custom-call | flops 8589934592 | bytes 23068672 | tf_op jit(solution)/shard_map/rows_nt/pallas_call | solution.py:616
  301.4 21.0 %feed_rows.3 = (bf16[512,2048]{1,0:T(8,128)(2,1)}, bf16[512,2048]{1,0:T(8,128)(2,1)}, bf16[512,2048]{1,0:T(8,128)(2,1)}) custom-call(bf16[256,2048]{1,0:T(8,128)(2,1)} %collective-permute-done.28.refs_0_.refs_2_, bf16[256,2048]{1,0:T(8,128)(2,1)} %collective-permute-done.38.refs_1_.refs_3_, bf16[256,2048]{1,0:T(8,128)(2,1)} %collective-permute-done.19.refs_2_, ...), custom_call_target="tpu_custom_call" | custom-call | flops 12884901888 | bytes 35651584 | tf_op jit(solution)/shard_map/feed_rows/pallas_call | solution.py:547
  328.5 14.0 %rows_nt.10 = (bf16[256,2048]{1,0:T(8,128)(2,1)}, bf16[256,2048]{1,0:T(8,128)(2,1)}) custom-call(bf16[512,2048]{1,0:T(8,128)(2,1)} %get-tuple-element.298.refs_0_.refs_1_.refs_9_, bf16[512,2048]{1,0:T(8,128)(2,1)} %get-tuple-element.298.refs_0_.refs_1_.refs_9_, bf16[512,2048]{1,0:T(8,128)(2,1)} %get-tuple-element.299.refs_2_.refs_3_.refs_9_, ...), custom_call_target="tpu_custom_call" | custom-call | flops 8589934592 | bytes 23068672 | tf_op jit(solution)/shard_map/rows_nt/pallas_call | solution.py:616
  342.6 13.5 %collective-permute-done.47.one_ref = bf16[256,2048]{1,0:T(8,128)(2,1)S(1)} collective-permute-done((bf16[256,2048]{1,0:T(8,128)(2,1)}, bf16[256,2048]{1,0:T(8,128)(2,1)S(1)}, u32[]{:S(2)}, u32[]{:S(2)}) %collective-permute-start.47) | collective-permute-done | bytes 1048608 | tf_op jit(solution)/shard_map/ppermute | solution.py:40
  366.1 16.0 %product.5 = bf16[1024,2048]{1,0:T(8,128)(2,1)} custom-call(s32[1]{0:T(128)} %bitcast.31.first_ref, bf16[256,2048]{1,0:T(8,128)(2,1)} %bitcast.63, bf16[256,2048]{1,0:T(8,128)(2,1)} %collective-permute-done.12.refs_3_.refs_1_, bf16[256,2048]{1,0:T(8,128)(2,1)} %collective-permute-done.19.refs_2_, bf16[256,2048]{1,0:T(8,128)(2,1)} %collective-permute-done.29.refs_3_, ...), custom_call_target="tpu_custom_call" | custom-call | flops 8589934592 | bytes 20971520 | tf_op jit(solution)/shard_map/product/pallas_call | solution.py:732
  390.1 9.4 %rows_nt.12 = (bf16[256,2048]{1,0:T(8,128)(2,1)}, bf16[256,2048]{1,0:T(8,128)(2,1)}) custom-call(bf16[512,2048]{1,0:T(8,128)(2,1)} %get-tuple-element.315.refs_9_.refs_0_, bf16[512,2048]{1,0:T(8,128)(2,1)} %get-tuple-element.314.refs_0_.refs_8_.refs_1_, bf16[2048,2048]{1,0:T(8,128)(2,1)} %all-gather.8.cloned.1.call-done.refs_6_.refs_1_.refs_2_), custom_call_target="tpu_custom_call" | custom-call | flops 4294967296 | bytes 12582912 | tf_op jit(solution)/shard_map/rows_nt/pallas_call | solution.py:616
  399.5 16.5 %product.6.refs_12_ = bf16[1024,4096]{1,0:T(8,128)(2,1)} custom-call(s32[1]{0:T(128)} %bitcast.31.first_ref, bf16[256,2048]{1,0:T(8,128)(2,1)} %get-tuple-element.325.refs_0_, bf16[256,2048]{1,0:T(8,128)(2,1)} %copy-done.30, bf16[256,2048]{1,0:T(8,128)(2,1)} %collective-permute-done.28.refs_0_.refs_2_, ...), custom_call_target="tpu_custom_call" | custom-call | flops 8589934592 | bytes 20971520 | tf_op jit(solution)/shard_map/product/pallas_call | solution.py:732
  423.3 6.9 %split_columns.1 = (bf16[256,512]{1,0:T(8,128)(2,1)}, bf16[256,512]{1,0:T(8,128)(2,1)}, bf16[256,512]{1,0:T(8,128)(2,1)}, bf16[256,512]{1,0:T(8,128)(2,1)}) custom-call(bf16[256,2048]{1,0:T(8,128)(2,1)} %get-tuple-element.350.rows_ref.refs_0_, bf16[2048,4096]{1,0:T(8,128)(2,1)} %all-gather.6.cloned.1.call-done.refs_4_.refs_5_.weight_ref), custom_call_target="tpu_custom_call" | custom-call | flops 2147483648 | bytes 10485760 | tf_op jit(solution)/shard_map/split_columns/pallas_call | solution.py:665
  440.9 16.1 %product.8 = bf16[1024,4096]{1,0:T(8,128)(2,1)} custom-call(s32[1]{0:T(128)} %bitcast.31.first_ref, bf16[256,2048]{1,0:T(8,128)(2,1)} %get-tuple-element.325.refs_0_, bf16[256,2048]{1,0:T(8,128)(2,1)} %copy-done.30, bf16[256,2048]{1,0:T(8,128)(2,1)} %collective-permute-done.28.refs_0_.refs_2_, ...), custom_call_target="tpu_custom_call", output_to_operand_aliasing={{}: (13, {})} | custom-call | flops 858993472 | bytes 2097152 | tf_op jit(solution)/shard_map/product/pallas_call | solution.py:732
  462.5 26.2 %attend_back.2 = (bf16[4,192,512]{2,1,0:T(8,128)(2,1)}, f32[4,192,256]{2,1,0:T(8,128)}, f32[4,192,256]{2,1,0:T(8,128)}, bf16[4,192,256]{2,1,0:T(8,128)(2,1)}, bf...) custom-call(s32[16]{0:T(128)} %stack.92.refs_0_, s32[4,1,256]{2,1,0:T(1,128)} %broadcast_in_dim.27.refs_1_, ...), custom_call_target="tpu_custom_call" | custom-call | flops 16106127360 | bytes 6291456 | tf_op jit(solution)/shard_map/attend_back/pallas_call | solution.py:389
  494.5 9.9 %attend_back.3 = (bf16[4,64,512]{2,1,0:T(8,128)(2,1)}, f32[4,64,256]{2,1,0:T(8,128)}, bf16[4,64,256]{2,1,0:T(8,128)(2,1)}, bf16[4,64,256]{2,1,0:T(8,128)(2,1)}, ...) custom-call(s32[16]{0:T(128)} %stack.92.refs_0_, s32[4,1,256]{2,1,0:T(1,128)} %broadcast_in_dim.27.refs_1_, ...), custom_call_target="tpu_custom_call" | custom-call | flops 5368709120 | bytes 2097152 | tf_op jit(solution)/shard_map/attend_back/pallas_call | solution.py:389
  527.3 7.4 %rows_nt.13 = (bf16[256,2048]{1,0:T(8,128)(2,1)}, bf16[256,2048]{1,0:T(8,128)(2,1)}, bf16[256,2048]{1,0:T(8,128)(2,1)}, bf16[256,2048]{1,0:T(8,128)(2,1)}) custom-call(bf16[1024,768]{1,0:T(8,128)(2,1)} %get-tuple-element.418.refs_0_.refs_1_.refs_2_.refs_3_.refs_8_, bf16[1024,768]{1,0:T(8,128)(2,1)} %get-tuple-element.418.refs_0_.refs_1_.refs_2_.refs_3_.refs_8_, ...), custom_call_target="tpu_custom_call" | custom-call | flops 3221225472 | bytes 8912896 | tf_op jit(solution)/shard_map/rows_nt/pallas_call | solution.py:616
  546.5 9.4 %product.9 = bf16[1024,768]{1,0:T(8,128)(2,1)} custom-call(s32[1]{0:T(128)} %bitcast.31.first_ref, bf16[256,2048]{1,0:T(8,128)(2,1)} %copy-done.9, bf16[256,2048]{1,0:T(8,128)(2,1)} %copy-done.24, bf16[256,2048]{1,0:T(8,128)(2,1)} %collective-permute-done.4.refs_2_, bf16[256,2048]{1,0:T(8,128)(2,1)} %collective-permute-done.5.refs_3_, ...), custom_call_target="tpu_custom_call" | custom-call | flops 3221225472 | bytes 13107200 | tf_op jit(solution)/shard_map/product/pallas_call | solution.py:732
  568.0 25.3 %collective-permute-done.73 = f32[1152]{0:T(1024)S(1)} collective-permute-done((f32[1152]{0:T(1024)S(1)}, f32[1152]{0:T(1024)S(1)}, u32[]{:S(2)}, u32[]{:S(2)}) %collective-permute-start.73) | collective-permute-done | bytes 4640 | tf_op jit(solution)/shard_map/ppermute | solution.py:75
  621.7 20.4 %collective-permute-done.77 = f32[256]{0:T(256)S(1)} collective-permute-done((f32[256]{0:T(256)S(1)}, f32[256]{0:T(256)S(1)}, u32[]{:S(2)}, u32[]{:S(2)}) %collective-permute-start.77) | collective-permute-done | bytes 1056 | tf_op jit(solution)/shard_map/ppermute | solution.py:75
  (408 shorter events, 274.5 us)
Async XLA Ops:
  7.2 85.8 %all-gather.4.cloned.1.call-start = ((), (), s32[]{:S(2)}) async-start(), calls=%async_computation.4 | async-start | bytes 12976128 | tf_op jit(solution)/shard_map/all_gather | solution.py:67
  11.5 187.1 %all-gather.6.cloned.1.call-start = ((), (), s32[]{:S(2)}) async-start(), calls=%async_computation.5 | async-start | bytes 18874368 | tf_op jit(solution)/shard_map/all_gather | solution.py:67
  12.8 44.4 %collective-permute-start = (bf16[256,2048]{1,0:T(8,128)(2,1)S(1)}, bf16[256,2048]{1,0:T(8,128)(2,1)S(1)}, u32[]{:S(2)}, u32[]{:S(2)}) collective-permute-start(bf16[256,2048]{1,0:T(8,128)(2,1)S(1)} %multiply_convert_fusion.refs_0_), channel_id=1, source_target_pairs={{0,1},{1,2},{2,3},{3,0},{4,5},{5,6},{6,7},{7,4},{8,9},{9,10},{10,1... | collective-permute-start | bytes 3145736 | tf_op jit(solution)/shard_map/ppermute | solution.py:40
  15.9 30.2 %collective-permute-start.1 = (bf16[256,512]{1,0:T(8,128)(2,1)S(1)}, bf16[256,512]{1,0:T(8,128)(2,1)S(1)}, u32[]{:S(2)}, u32[]{:S(2)}) collective-permute-start(bf16[256,512]{1,0:T(8,128)(2,1)S(1)} %bitcast.68), channel_id=1, source_target_pairs={{0,3},{1,0},{2,1},{3,2},{4,7},{5,4},{6,5},{7,6},{8,11},{9,8},{10,9... | collective-permute-start | bytes 786440 | tf_op jit(solution)/shard_map/ppermute | solution.py:82
  65.3 181.9 %all-gather.8.cloned.1.call-start = ((), (), s32[]{:S(2)}) async-start(), calls=%async_computation.6 | async-start | bytes 9437184 | tf_op jit(solution)/shard_map/all_gather | solution.py:67
  118.0 370.8 %reduce-scatter.5.cloned.1.call-start = ((), (), s32[]{:S(2)}) async-start(), calls=%async_computation.7 | async-start | bytes 5242880 | tf_op jit(solution)/shard_map/reduce_scatter | solution.py:859
  176.7 35.5 %collective-permute-start.30 = (bf16[256,2048]{1,0:T(8,128)(2,1)S(1)}, bf16[256,2048]{1,0:T(8,128)(2,1)}, u32[]{:S(2)}, u32[]{:S(2)}) collective-permute-start(bf16[256,2048]{1,0:T(8,128)(2,1)S(1)} %bitcast.66), channel_id=1, source_target_pairs={{0,4},{4,0},{8,12},{12,8},{1,5},{5,1},{9,13},{13,9},{2,6},{6,2},{1... | collective-permute-start | bytes 3145736 | tf_op jit(solution)/shard_map/ppermute | solution.py:45
  176.7 36.0 %collective-permute-start.31 = (bf16[256,2048]{1,0:T(8,128)(2,1)}, bf16[256,2048]{1,0:T(8,128)(2,1)}, u32[]{:S(2)}, u32[]{:S(2)}) collective-permute-start(bf16[256,2048]{1,0:T(8,128)(2,1)} %collective-permute-done.12.refs_3_.refs_1_), channel_id=1, source_target_pairs={{0,4},{4,0},{8,12},{12,8},{1,5},{5,1},{9,13},{13,9},{2,6},{6,2},{1... | collective-permute-start | bytes 3145736 | tf_op jit(solution)/shard_map/ppermute | solution.py:45
  210.1 36.8 %collective-permute-start.27 = (bf16[256,2048]{1,0:T(8,128)(2,1)}, bf16[256,2048]{1,0:T(8,128)(2,1)S(1)}, u32[]{:S(2)}, u32[]{:S(2)}) collective-permute-start(bf16[256,2048]{1,0:T(8,128)(2,1)} %get-tuple-element.325.refs_0_), channel_id=1, source_target_pairs={{0,1},{1,2},{2,3},{3,0},{4,5},{5,6},{6,7},{7,4},{8,9},{9,10},{10,1... | collective-permute-start | bytes 3145736 | tf_op jit(solution)/shard_map/ppermute | solution.py:40
  212.7 55.8 %collective-permute-start.36 = (bf16[256,512]{1,0:T(8,128)(2,1)S(1)}, bf16[256,512]{1,0:T(8,128)(2,1)S(1)}, u32[]{:S(2)}, u32[]{:S(2)}) collective-permute-start(bf16[256,512]{1,0:T(8,128)(2,1)S(1)} %copy-done.20), channel_id=1, source_target_pairs={{0,4},{4,0},{8,12},{12,8},{1,5},{5,1},{9,13},{13,9},{2,6},{6,2},{1... | collective-permute-start | bytes 786440 | tf_op jit(solution)/shard_map/ppermute | solution.py:45
  214.1 54.4 %collective-permute-start.37 = (bf16[256,512]{1,0:T(8,128)(2,1)S(1)}, bf16[256,512]{1,0:T(8,128)(2,1)S(1)}, u32[]{:S(2)}, u32[]{:S(2)}) collective-permute-start(bf16[256,512]{1,0:T(8,128)(2,1)S(1)} %copy-done.22), channel_id=1, source_target_pairs={{0,4},{4,0},{8,12},{12,8},{1,5},{5,1},{9,13},{13,9},{2,6},{6,2},{1... | collective-permute-start | bytes 786440 | tf_op jit(solution)/shard_map/ppermute | solution.py:45
  214.9 53.7 %collective-permute-start.32 = (bf16[256,2048]{1,0:T(8,128)(2,1)}, bf16[256,2048]{1,0:T(8,128)(2,1)}, u32[]{:S(2)}, u32[]{:S(2)}) collective-permute-start(bf16[256,2048]{1,0:T(8,128)(2,1)} %collective-permute-done.19.refs_2_), channel_id=1, source_target_pairs={{0,4},{4,0},{8,12},{12,8},{1,5},{5,1},{9,13},{13,9},{2,6},{6,2},{1... | collective-permute-start | bytes 3145736 | tf_op jit(solution)/shard_map/ppermute | solution.py:45
  226.3 42.2 %collective-permute-start.33 = (bf16[256,2048]{1,0:T(8,128)(2,1)}, bf16[256,2048]{1,0:T(8,128)(2,1)}, u32[]{:S(2)}, u32[]{:S(2)}) collective-permute-start(bf16[256,2048]{1,0:T(8,128)(2,1)} %collective-permute-done.29.refs_3_), channel_id=1, source_target_pairs={{0,4},{4,0},{8,12},{12,8},{1,5},{5,1},{9,13},{13,9},{2,6},{6,2},{1... | collective-permute-start | bytes 3145736 | tf_op jit(solution)/shard_map/ppermute | solution.py:45
  273.0 49.5 %collective-permute-start.43 = (bf16[256,2048]{1,0:T(8,128)(2,1)}, bf16[256,2048]{1,0:T(8,128)(2,1)}, u32[]{:S(2)}, u32[]{:S(2)}) collective-permute-start(bf16[256,2048]{1,0:T(8,128)(2,1)} %get-tuple-element.325.refs_0_), channel_id=1, source_target_pairs={{0,4},{4,0},{8,12},{12,8},{1,5},{5,1},{9,13},{13,9},{2,6},{6,2},{1... | collective-permute-start | bytes 3145736 | tf_op jit(solution)/shard_map/ppermute | solution.py:45
  328.5 37.6 %collective-permute-start.49 = (bf16[512,2048]{1,0:T(8,128)(2,1)}, bf16[512,2048]{1,0:T(8,128)(2,1)}, u32[]{:S(2)}, u32[]{:S(2)}) collective-permute-start(bf16[512,2048]{1,0:T(8,128)(2,1)} %get-tuple-element.315.refs_9_.refs_0_), channel_id=1, source_target_pairs={{0,4},{4,0},{8,12},{12,8},{1,5},{5,1},{9,13},{13,9},{2,6},{6,2},{1... | collective-permute-start | bytes 6291464 | tf_op jit(solution)/shard_map/ppermute | solution.py:45
  387.1 138.3 %reduce-scatter.7.cloned.1.call-start = ((), (), s32[]{:S(2)}) async-start(), calls=%async_computation.8 | async-start | bytes 5242880 | tf_op jit(solution)/shard_map/reduce_scatter | solution.py:859
  387.1 53.8 %collective-permute-start.56 = (bf16[512,2048]{1,0:T(8,128)(2,1)S(1)}, bf16[512,2048]{1,0:T(8,128)(2,1)}, u32[]{:S(2)}, u32[]{:S(2)}) collective-permute-start(bf16[512,2048]{1,0:T(8,128)(2,1)S(1)} %copy-done), channel_id=1, source_target_pairs={{0,4},{4,0},{8,12},{12,8},{1,5},{5,1},{9,13},{13,9},{2,6},{6,2},{1... | collective-permute-start | bytes 6291464 | tf_op jit(solution)/shard_map/ppermute | solution.py:45
  457.7 149.9 %reduce-scatter.9.cloned.1.call-start = ((), (), s32[]{:S(2)}) async-start(), calls=%async_computation.9 | async-start | bytes 10485760 | tf_op jit(solution)/shard_map/reduce_scatter | solution.py:859
  458.3 196.3 %reduce-scatter.11.cloned.1.call-start = ((), (), s32[]{:S(2)}) async-start(), calls=%async_computation.10 | async-start | bytes 2293760 | tf_op jit(solution)/shard_map/reduce_scatter | solution.py:859
  492.2 33.2 %collective-permute-start.58 = (bf16[256,2048]{1,0:T(8,128)(2,1)}, bf16[256,2048]{1,0:T(8,128)(2,1)S(1)}, u32[]{:S(2)}, u32[]{:S(2)}) collective-permute-start(bf16[256,2048]{1,0:T(8,128)(2,1)} %add_rows.9), channel_id=1, source_target_pairs={{0,1},{1,2},{2,3},{3,0},{4,5},{5,6},{6,7},{7,4},{8,9},{9,10},{10,1... | collective-permute-start | bytes 3145736 | tf_op jit(solution)/shard_map/ppermute | solution.py:40
  565.0 35.5 %collective-permute-start.71 = (bf16[256,2048]{1,0:T(8,128)(2,1)}, bf16[256,2048]{1,0:T(8,128)(2,1)S(1)}, u32[]{:S(2)}, u32[]{:S(2)}) collective-permute-start(bf16[256,2048]{1,0:T(8,128)(2,1)} %add_rows.10), channel_id=1, source_target_pairs={{0,1},{1,2},{2,3},{3,0},{4,5},{5,6},{6,7},{7,4},{8,9},{9,10},{10,1... | collective-permute-start | bytes 3145736 | tf_op jit(solution)/shard_map/ppermute | solution.py:40
  565.1 34.4 %collective-permute-start.72 = (bf16[256,512]{1,0:T(8,128)(2,1)S(1)}, bf16[256,512]{1,0:T(8,128)(2,1)S(1)}, u32[]{:S(2)}, u32[]{:S(2)}) collective-permute-start(bf16[256,512]{1,0:T(8,128)(2,1)S(1)} %add_convert_fusion.3), channel_id=1, source_target_pairs={{0,1},{1,2},{2,3},{3,0},{4,5},{5,6},{6,7},{7,4},{8,9},{9,10},{10,1... | collective-permute-start | bytes 786440 | tf_op jit(solution)/shard_map/ppermute | solution.py:40
  612.3 33.7 %collective-permute-start.75 = (bf16[256,2048]{1,0:T(8,128)(2,1)}, bf16[256,2048]{1,0:T(8,128)(2,1)S(1)}, u32[]{:S(2)}, u32[]{:S(2)}) collective-permute-start(bf16[256,2048]{1,0:T(8,128)(2,1)} %add_rows.11), channel_id=1, source_target_pairs={{0,1},{1,2},{2,3},{3,0},{4,5},{5,6},{6,7},{7,4},{8,9},{9,10},{10,1... | collective-permute-start | bytes 3145736 | tf_op jit(solution)/shard_map/ppermute | solution.py:40
  613.9 38.6 %collective-permute-start.76 = (bf16[256,512]{1,0:T(8,128)(2,1)S(1)}, bf16[256,512]{1,0:T(8,128)(2,1)}, u32[]{:S(2)}, u32[]{:S(2)}) collective-permute-start(bf16[256,512]{1,0:T(8,128)(2,1)S(1)} %add_convert_fusion.2), channel_id=1, source_target_pairs={{0,1},{1,2},{2,3},{3,0},{4,5},{5,6},{6,7},{7,4},{8,9},{9,10},{10,1... | collective-permute-start | bytes 786440 | tf_op jit(solution)/shard_map/ppermute | solution.py:40
  (132 other events, 1953.1 us)
Sparse Core Ops, SparseCore 0:
  11.7 70.3 all-gather.3
  84.5 98.2 all-gather.5
  185.3 54.3 all-gather.7
  386.3 50.7 reduce-scatter.4
  457.2 60.0 reduce-scatter.6
  520.2 87.3 reduce-scatter.8
  611.0 33.0 reduce-scatter.10

commit v6 on v5

--- a/solution.py
+++ b/solution.py
@@ -914,7 +914,7 @@
     normed, out_own = together(normed, output_weight.T)
     normed_rows, heads = [normed], []
     out_pieces = [out_own]
-    for _ in range(1, tp_count):
+    for _ in range(2, tp_count):
         out_pieces.append(shift(out_pieces[-1], -1))
     for place in range(1, tp_count):
         came = ring_hop(normed_rows[-1])
@@ -923,6 +923,7 @@
         came, work = together(came, work)
         if place == 1:
             came, out_pieces = together(came, out_pieces)
+            out_pieces.append(shift(out_pieces[-1], -1))
             second_weight = jnp.concatenate(
                 [*out_pieces, (up_weight.astype(jnp.float32) * hidden_gain_rows).astype(jnp.bfloat16)],
                 axis=1,
@@ -1134,10 +1135,17 @@
     hidden_sums = jnp.sum(
         gate_sums * gate_weight.astype(jnp.float32) + up_sums * up_weight.astype(jnp.float32), axis=1
     )
-    hidden_gain_grad = all_sum(hidden_sums, ("tp",))
+    hidden_gain_grad = hidden_sums
+    stages = []
+    for stage in range(tp_count.bit_length() - 1):
+        stages.append([(i, i ^ (1 << stage)) for i in range(tp_count)])
+    hidden_gain_grad = hidden_gain_grad + lax.ppermute(hidden_gain_grad, "tp", stages[0])
     qkv_sums = qkv_shard[:, :qkv_cols].astype(jnp.float32)
     attention_gain_grad = qkv_shard[:, qkv_cols].astype(jnp.float32) / attention_rows[:, 0]
     (input_grad,) = norm_back(came, row_terms[0], tokens, grad_hidden, (jnp.float32,))
+    input_grad, hidden_gain_grad = together(input_grad, hidden_gain_grad)
+    for pairs in stages[1:]:
+        hidden_gain_grad = hidden_gain_grad + lax.ppermute(hidden_gain_grad, "tp", pairs)
     output_grad = out_total.T
     down_grad = down_shard.astype(jnp.float32).T
     gate_grad, up_grad = gate_sums * hidden_gain_rows, up_sums * hidden_gain_rows

time: 674 us -> 668 us (level)
    ppermute x7 -> x5, waiting for transfers between devices: 52.7 us -> 33 us  [all_sum(): lax.ppermute(values, axis, [(i, i ^ bit) for i in range(count)])]
    ppermute x21, waiting for transfers between devices: 94.5 us -> 113 us  [ring_hop(): lax.ppermute(values, 'tp', [(i, (i + 1) % count) for i in range(count)])]
    unnamed x149 -> x145, local copies, waits for them, and re-layouts: 16.1 us -> 15 us
where the time goes in v6:
time: 668 us; the launch traced here: 660 us
  Pallas kernels  279 us (42%)
  waiting for transfers between devices  239 us (36%)
  starting transfers between devices  57 us (9%)
  local copies, waits for them, and re-layouts  26.6 us (4%)
  other arithmetic  25.8 us (4%)
  matrix products  16.3 us (2%)
  between operations  15.5 us (2%)
    ppermute x21, waiting for transfers between devices, ring_hop(): lax.ppermute(values, 'tp', [(i, (i + 1) % count) for i in range(count)])  113 us
    pallas_call x5, Pallas kernels, product(): pl.pallas_call(functools.partial(product_kernel, len(left), [len(parts) f...  65.1 us
    pallas_call x7, Pallas kernels, rows_nt(): pl.pallas_call(functools.partial(rows_nt_kernel, layouts), grid=(width //...  64.8 us
    ppermute x9, waiting for transfers between devices, shift(): lax.ppermute(values, 'tp', [(i, (i + places) % count) for i in range(coun...  56.5 us
    pallas_call x2, Pallas kernels, feed_rows(): pl.pallas_call(functools.partial(feed_kernel, count), grid=(steps,), out_...  41.6 us
    pallas_call x2, Pallas kernels, attend_back(): pl.pallas_call(functools.partial(attend_back_kernel, places, blocks, plac...  36.4 us
    ppermute x5, waiting for transfers between devices, all_sum(): lax.ppermute(values, axis, [(i, i ^ bit) for i in range(count)])  33 us
    ppermute x42, waiting for transfers between devices, ctx_swap(): return lax.ppermute(values, CTX, [(i, i ^ mask) for i in range(count)])  28 us
  transfers between devices with their start and end apart: 86, of which 32 were waited for; matrix products, arithmetic and copies ran while one was open for 8% of the time, Pallas kernels for 42%

profile of v6, /device:TPU:0, one launch (start us, length us, event | category | flops | bytes accessed | tf_op | source)
XLA Modules:
  0.0 659.5 jit_solution(5200463004582426375)
XLA Ops:
  17.9 28.1 %collective-permute-done.1 = bf16[256,512]{1,0:T(8,128)(2,1)S(1)} collective-permute-done((bf16[256,512]{1,0:T(8,128)(2,1)S(1)}, bf16[256,512]{1,0:T(8,128)(2,1)S(1)}, u32[]{:S(2)}, u32[]{:S(2)}) %collective-permute-start.1) | collective-permute-done | bytes 262176 | tf_op jit(solution)/shard_map/ppermute | solution.py:82
  68.3 20.4 %collective-permute-done.3.refs_2_ = bf16[256,2048]{1,0:T(8,128)(2,1)} collective-permute-done((bf16[256,2048]{1,0:T(8,128)(2,1)S(1)}, bf16[256,2048]{1,0:T(8,128)(2,1)}, u32[]{:S(2)}, u32[]{:S(2)}) %collective-permute-start.3) | collective-permute-done | bytes 1048608 | tf_op jit(solution)/shard_map/ppermute | solution.py:40
  132.9 7.1 %collective-permute-done.15.refs_14_.refs_30_ = bf16[256,256]{1,0:T(8,128)(2,1)} collective-permute-done((bf16[256,256]{1,0:T(8,128)(2,1)}, bf16[256,256]{1,0:T(8,128)(2,1)}, u32[]{:S(2)}, u32[]{:S(2)}) %collective-permute-start.15) | collective-permute-done | bytes 131104 | tf_op jit(solution)/shard_map/ppermute | solution.py:45
  149.7 18.0 %attend.1 = (bf16[256,512]{1,0:T(8,128)(2,1)}, bf16[256,512]{1,0:T(8,128)(2,1)}, bf16[256,512]{1,0:T(8,128)(2,1)}, bf16[256,512]{1,0:T(8,128)(2,1)}, f32[4,4,512]{2,1,0:T(4,128)}) custom-call(s32[16]{0:T(128)} %stack.92.refs_0_, s32[4,1,256]{2,1,0:T(1,128)} %broadcast_in_dim.27.refs_1_, s32[1,1,256]{2,1,0:T(1,128)} %bitcast.71, ...), custom_call_target="tpu_custom_call" | custom-call | flops 8589934592 | bytes 4194304 | tf_op jit(solution)/shard_map/attend/pallas_call | solution.py:242
  179.6 16.8 %collective-permute-done.24.refs_2_.refs_6_ = bf16[256,512]{1,0:T(8,128)(2,1)S(1)} collective-permute-done((bf16[256,512]{1,0:T(8,128)(2,1)}, bf16[256,512]{1,0:T(8,128)(2,1)S(1)}, u32[]{:S(2)}, u32[]{:S(2)}) %collective-permute-start.24) | collective-permute-done | bytes 262176 | tf_op jit(solution)/shard_map/ppermute | solution.py:82
  212.4 12.3 %collective-permute-done.29.refs_3_ = bf16[256,2048]{1,0:T(8,128)(2,1)} collective-permute-done((bf16[256,2048]{1,0:T(8,128)(2,1)}, bf16[256,2048]{1,0:T(8,128)(2,1)}, u32[]{:S(2)}, u32[]{:S(2)}) %collective-permute-start.29) | collective-permute-done | bytes 1048608 | tf_op jit(solution)/shard_map/ppermute | solution.py:40
  224.7 20.6 %collective-permute-done.27.refs_1_ = bf16[256,2048]{1,0:T(8,128)(2,1)S(1)} collective-permute-done((bf16[256,2048]{1,0:T(8,128)(2,1)}, bf16[256,2048]{1,0:T(8,128)(2,1)S(1)}, u32[]{:S(2)}, u32[]{:S(2)}) %collective-permute-start.27) | collective-permute-done | bytes 1048608 | tf_op jit(solution)/shard_map/ppermute | solution.py:40
  246.3 20.6 %feed_rows.2 = (bf16[512,2048]{1,0:T(8,128)(2,1)}, bf16[512,2048]{1,0:T(8,128)(2,1)}, bf16[512,2048]{1,0:T(8,128)(2,1)}) custom-call(bf16[256,2048]{1,0:T(8,128)(2,1)} %get-tuple-element.325.refs_0_, bf16[256,2048]{1,0:T(8,128)(2,1)} %copy-done.29, bf16[256,2048]{1,0:T(8,128)(2,1)} %bitcast.62, bf16[256,2048]{1,0:T(8,128)(2,1)} %collective-permute-done.11.refs_3_.refs_1_, ...), custom_call_target="tpu_custom_call" | custom-call | flops 12884901888 | bytes 35651584 | tf_op jit(solution)/shard_map/feed_rows/pallas_call | solution.py:547
  278.6 14.1 %rows_nt.8 = (bf16[256,2048]{1,0:T(8,128)(2,1)}, bf16[256,2048]{1,0:T(8,128)(2,1)}) custom-call(bf16[512,2048]{1,0:T(8,128)(2,1)} %get-tuple-element.333.refs_0_.refs_1_.refs_8_, bf16[512,2048]{1,0:T(8,128)(2,1)} %get-tuple-element.333.refs_0_.refs_1_.refs_8_, bf16[512,2048]{1,0:T(8,128)(2,1)} %get-tuple-element.348.refs_2_.refs_3_.refs_8_, ...), custom_call_target="tpu_custom_call" | custom-call | flops 8589934592 | bytes 23068672 | tf_op jit(solution)/shard_map/rows_nt/pallas_call | solution.py:616
  299.8 21.0 %feed_rows.3 = (bf16[512,2048]{1,0:T(8,128)(2,1)}, bf16[512,2048]{1,0:T(8,128)(2,1)}, bf16[512,2048]{1,0:T(8,128)(2,1)}) custom-call(bf16[256,2048]{1,0:T(8,128)(2,1)} %collective-permute-done.28.refs_0_.refs_2_, bf16[256,2048]{1,0:T(8,128)(2,1)} %collective-permute-done.38.refs_1_.refs_3_, bf16[256,2048]{1,0:T(8,128)(2,1)} %collective-permute-done.18.refs_2_, ...), custom_call_target="tpu_custom_call" | custom-call | flops 12884901888 | bytes 35651584 | tf_op jit(solution)/shard_map/feed_rows/pallas_call | solution.py:547
  326.9 14.0 %rows_nt.10 = (bf16[256,2048]{1,0:T(8,128)(2,1)}, bf16[256,2048]{1,0:T(8,128)(2,1)}) custom-call(bf16[512,2048]{1,0:T(8,128)(2,1)} %get-tuple-element.298.refs_0_.refs_1_.refs_9_, bf16[512,2048]{1,0:T(8,128)(2,1)} %get-tuple-element.298.refs_0_.refs_1_.refs_9_, bf16[512,2048]{1,0:T(8,128)(2,1)} %get-tuple-element.299.refs_2_.refs_3_.refs_9_, ...), custom_call_target="tpu_custom_call" | custom-call | flops 8589934592 | bytes 23068672 | tf_op jit(solution)/shard_map/rows_nt/pallas_call | solution.py:616
  341.0 13.5 %collective-permute-done.47.one_ref = bf16[256,2048]{1,0:T(8,128)(2,1)S(1)} collective-permute-done((bf16[256,2048]{1,0:T(8,128)(2,1)}, bf16[256,2048]{1,0:T(8,128)(2,1)S(1)}, u32[]{:S(2)}, u32[]{:S(2)}) %collective-permute-start.47) | collective-permute-done | bytes 1048608 | tf_op jit(solution)/shard_map/ppermute | solution.py:40
  364.5 16.0 %product.5 = bf16[1024,2048]{1,0:T(8,128)(2,1)} custom-call(s32[1]{0:T(128)} %bitcast.31.first_ref, bf16[256,2048]{1,0:T(8,128)(2,1)} %bitcast.63, bf16[256,2048]{1,0:T(8,128)(2,1)} %collective-permute-done.11.refs_3_.refs_1_, bf16[256,2048]{1,0:T(8,128)(2,1)} %collective-permute-done.18.refs_2_, bf16[256,2048]{1,0:T(8,128)(2,1)} %collective-permute-done.29.refs_3_, ...), custom_call_target="tpu_custom_call" | custom-call | flops 8589934592 | bytes 20971520 | tf_op jit(solution)/shard_map/product/pallas_call | solution.py:732
  388.5 9.1 %rows_nt.12 = (bf16[256,2048]{1,0:T(8,128)(2,1)}, bf16[256,2048]{1,0:T(8,128)(2,1)}) custom-call(bf16[512,2048]{1,0:T(8,128)(2,1)} %get-tuple-element.315.refs_9_.refs_0_, bf16[512,2048]{1,0:T(8,128)(2,1)} %get-tuple-element.314.refs_0_.refs_8_.refs_1_, bf16[2048,2048]{1,0:T(8,128)(2,1)} %all-gather.8.cloned.1.call-done.refs_6_.refs_1_.refs_2_), custom_call_target="tpu_custom_call" | custom-call | flops 4294967296 | bytes 12582912 | tf_op jit(solution)/shard_map/rows_nt/pallas_call | solution.py:616
  397.6 16.5 %product.6.refs_12_ = bf16[1024,4096]{1,0:T(8,128)(2,1)} custom-call(s32[1]{0:T(128)} %bitcast.31.first_ref, bf16[256,2048]{1,0:T(8,128)(2,1)} %get-tuple-element.325.refs_0_, bf16[256,2048]{1,0:T(8,128)(2,1)} %copy-done.29, bf16[256,2048]{1,0:T(8,128)(2,1)} %collective-permute-done.28.refs_0_.refs_2_, ...), custom_call_target="tpu_custom_call" | custom-call | flops 8589934592 | bytes 20971520 | tf_op jit(solution)/shard_map/product/pallas_call | solution.py:732
  422.0 7.0 %split_columns.1 = (bf16[256,512]{1,0:T(8,128)(2,1)}, bf16[256,512]{1,0:T(8,128)(2,1)}, bf16[256,512]{1,0:T(8,128)(2,1)}, bf16[256,512]{1,0:T(8,128)(2,1)}) custom-call(bf16[256,2048]{1,0:T(8,128)(2,1)} %get-tuple-element.350.rows_ref.refs_0_, bf16[2048,4096]{1,0:T(8,128)(2,1)} %all-gather.6.cloned.1.call-done.refs_4_.refs_5_.weight_ref), custom_call_target="tpu_custom_call" | custom-call | flops 2147483648 | bytes 10485760 | tf_op jit(solution)/shard_map/split_columns/pallas_call | solution.py:665
  439.6 16.0 %product.8 = bf16[1024,4096]{1,0:T(8,128)(2,1)} custom-call(s32[1]{0:T(128)} %bitcast.31.first_ref, bf16[256,2048]{1,0:T(8,128)(2,1)} %get-tuple-element.325.refs_0_, bf16[256,2048]{1,0:T(8,128)(2,1)} %copy-done.29, bf16[256,2048]{1,0:T(8,128)(2,1)} %collective-permute-done.28.refs_0_.refs_2_, ...), custom_call_target="tpu_custom_call", output_to_operand_aliasing={{}: (13, {})} | custom-call | flops 858993472 | bytes 2097152 | tf_op jit(solution)/shard_map/product/pallas_call | solution.py:732
  460.4 26.2 %attend_back.2 = (bf16[4,192,512]{2,1,0:T(8,128)(2,1)}, f32[4,192,256]{2,1,0:T(8,128)}, f32[4,192,256]{2,1,0:T(8,128)}, bf16[4,192,256]{2,1,0:T(8,128)(2,1)}, bf...) custom-call(s32[16]{0:T(128)} %stack.92.refs_0_, s32[4,1,256]{2,1,0:T(1,128)} %broadcast_in_dim.27.refs_1_, ...), custom_call_target="tpu_custom_call" | custom-call | flops 16106127360 | bytes 6291456 | tf_op jit(solution)/shard_map/attend_back/pallas_call | solution.py:389
  492.4 10.2 %attend_back.3 = (bf16[4,64,512]{2,1,0:T(8,128)(2,1)}, f32[4,64,256]{2,1,0:T(8,128)}, bf16[4,64,256]{2,1,0:T(8,128)(2,1)}, bf16[4,64,256]{2,1,0:T(8,128)(2,1)}, ...) custom-call(s32[16]{0:T(128)} %stack.92.refs_0_, s32[4,1,256]{2,1,0:T(1,128)} %broadcast_in_dim.27.refs_1_, ...), custom_call_target="tpu_custom_call" | custom-call | flops 5368709120 | bytes 2097152 | tf_op jit(solution)/shard_map/attend_back/pallas_call | solution.py:389
  503.6 8.1 %collective-permute-done.61.refs_4_ = bf16[4,192,256]{2,1,0:T(8,128)(2,1)S(1)} collective-permute-done((bf16[4,192,256]{2,1,0:T(8,128)(2,1)S(1)}, bf16[4,192,256]{2,1,0:T(8,128)(2,1)S(1)}, u32[]{:S(2)}, u32[]{:S(2)}) %collective-permute-start.61) | collective-permute-done | bytes 393248 | tf_op jit(solution)/shard_map/ppermute | solution.py:45
  526.4 7.1 %rows_nt.13 = (bf16[256,2048]{1,0:T(8,128)(2,1)}, bf16[256,2048]{1,0:T(8,128)(2,1)}, bf16[256,2048]{1,0:T(8,128)(2,1)}, bf16[256,2048]{1,0:T(8,128)(2,1)}) custom-call(bf16[1024,768]{1,0:T(8,128)(2,1)} %get-tuple-element.418.refs_0_.refs_1_.refs_2_.refs_3_.refs_8_, bf16[1024,768]{1,0:T(8,128)(2,1)} %get-tuple-element.418.refs_0_.refs_1_.refs_2_.refs_3_.refs_8_, ...), custom_call_target="tpu_custom_call" | custom-call | flops 3221225472 | bytes 8912896 | tf_op jit(solution)/shard_map/rows_nt/pallas_call | solution.py:616
  545.0 9.7 %product.9 = bf16[1024,768]{1,0:T(8,128)(2,1)} custom-call(s32[1]{0:T(128)} %bitcast.31.first_ref, bf16[256,2048]{1,0:T(8,128)(2,1)} %copy-done.9, bf16[256,2048]{1,0:T(8,128)(2,1)} %copy-done.23, bf16[256,2048]{1,0:T(8,128)(2,1)} %collective-permute-done.3.refs_2_, bf16[256,2048]{1,0:T(8,128)(2,1)} %collective-permute-done.4.refs_3_, ...), custom_call_target="tpu_custom_call" | custom-call | flops 3221225472 | bytes 13107200 | tf_op jit(solution)/shard_map/product/pallas_call | solution.py:732
  566.7 24.8 %collective-permute-done.73 = f32[1152]{0:T(1024)S(1)} collective-permute-done((f32[1152]{0:T(1024)S(1)}, f32[1152]{0:T(1024)S(1)}, u32[]{:S(2)}, u32[]{:S(2)}) %collective-permute-start.73) | collective-permute-done | bytes 4640 | tf_op jit(solution)/shard_map/ppermute | solution.py:75
  620.8 15.2 %collective-permute-done.75.one_ref = bf16[256,2048]{1,0:T(8,128)(2,1)} collective-permute-done((bf16[256,2048]{1,0:T(8,128)(2,1)}, bf16[256,2048]{1,0:T(8,128)(2,1)}, u32[]{:S(2)}, u32[]{:S(2)}) %collective-permute-start.75) | collective-permute-done | bytes 1048608 | tf_op jit(solution)/shard_map/ppermute | solution.py:40
  (404 shorter events, 271.3 us)
Async XLA Ops:
  7.2 83.5 %all-gather.4.cloned.1.call-start = ((), (), s32[]{:S(2)}) async-start(), calls=%async_computation.4 | async-start | bytes 12976128 | tf_op jit(solution)/shard_map/all_gather | solution.py:67
  11.5 185.2 %all-gather.6.cloned.1.call-start = ((), (), s32[]{:S(2)}) async-start(), calls=%async_computation.5 | async-start | bytes 18874368 | tf_op jit(solution)/shard_map/all_gather | solution.py:67
  12.8 35.6 %collective-permute-start = (bf16[256,2048]{1,0:T(8,128)(2,1)S(1)}, bf16[256,2048]{1,0:T(8,128)(2,1)S(1)}, u32[]{:S(2)}, u32[]{:S(2)}) collective-permute-start(bf16[256,2048]{1,0:T(8,128)(2,1)S(1)} %multiply_convert_fusion.refs_0_), channel_id=1, source_target_pairs={{0,1},{1,2},{2,3},{3,0},{4,5},{5,6},{6,7},{7,4},{8,9},{9,10},{10,1... | collective-permute-start | bytes 3145736 | tf_op jit(solution)/shard_map/ppermute | solution.py:40
  15.9 30.2 %collective-permute-start.1 = (bf16[256,512]{1,0:T(8,128)(2,1)S(1)}, bf16[256,512]{1,0:T(8,128)(2,1)S(1)}, u32[]{:S(2)}, u32[]{:S(2)}) collective-permute-start(bf16[256,512]{1,0:T(8,128)(2,1)S(1)} %bitcast.68), channel_id=1, source_target_pairs={{0,3},{1,0},{2,1},{3,2},{4,7},{5,4},{6,5},{7,6},{8,11},{9,8},{10,9... | collective-permute-start | bytes 786440 | tf_op jit(solution)/shard_map/ppermute | solution.py:82
  63.2 182.4 %all-gather.8.cloned.1.call-start = ((), (), s32[]{:S(2)}) async-start(), calls=%async_computation.6 | async-start | bytes 9437184 | tf_op jit(solution)/shard_map/all_gather | solution.py:67
  116.1 370.7 %reduce-scatter.5.cloned.1.call-start = ((), (), s32[]{:S(2)}) async-start(), calls=%async_computation.7 | async-start | bytes 5242880 | tf_op jit(solution)/shard_map/reduce_scatter | solution.py:859
  174.8 35.6 %collective-permute-start.30 = (bf16[256,2048]{1,0:T(8,128)(2,1)S(1)}, bf16[256,2048]{1,0:T(8,128)(2,1)}, u32[]{:S(2)}, u32[]{:S(2)}) collective-permute-start(bf16[256,2048]{1,0:T(8,128)(2,1)S(1)} %bitcast.66), channel_id=1, source_target_pairs={{0,4},{4,0},{8,12},{12,8},{1,5},{5,1},{9,13},{13,9},{2,6},{6,2},{1... | collective-permute-start | bytes 3145736 | tf_op jit(solution)/shard_map/ppermute | solution.py:45
  174.8 36.1 %collective-permute-start.31 = (bf16[256,2048]{1,0:T(8,128)(2,1)}, bf16[256,2048]{1,0:T(8,128)(2,1)}, u32[]{:S(2)}, u32[]{:S(2)}) collective-permute-start(bf16[256,2048]{1,0:T(8,128)(2,1)} %collective-permute-done.11.refs_3_.refs_1_), channel_id=1, source_target_pairs={{0,4},{4,0},{8,12},{12,8},{1,5},{5,1},{9,13},{13,9},{2,6},{6,2},{1... | collective-permute-start | bytes 3145736 | tf_op jit(solution)/shard_map/ppermute | solution.py:45
  208.4 36.9 %collective-permute-start.27 = (bf16[256,2048]{1,0:T(8,128)(2,1)}, bf16[256,2048]{1,0:T(8,128)(2,1)S(1)}, u32[]{:S(2)}, u32[]{:S(2)}) collective-permute-start(bf16[256,2048]{1,0:T(8,128)(2,1)} %get-tuple-element.325.refs_0_), channel_id=1, source_target_pairs={{0,1},{1,2},{2,3},{3,0},{4,5},{5,6},{6,7},{7,4},{8,9},{9,10},{10,1... | collective-permute-start | bytes 3145736 | tf_op jit(solution)/shard_map/ppermute | solution.py:40
  210.9 56.0 %collective-permute-start.36 = (bf16[256,512]{1,0:T(8,128)(2,1)S(1)}, bf16[256,512]{1,0:T(8,128)(2,1)S(1)}, u32[]{:S(2)}, u32[]{:S(2)}) collective-permute-start(bf16[256,512]{1,0:T(8,128)(2,1)S(1)} %copy-done.19), channel_id=1, source_target_pairs={{0,4},{4,0},{8,12},{12,8},{1,5},{5,1},{9,13},{13,9},{2,6},{6,2},{1... | collective-permute-start | bytes 786440 | tf_op jit(solution)/shard_map/ppermute | solution.py:45
  211.9 55.0 %collective-permute-start.37 = (bf16[256,512]{1,0:T(8,128)(2,1)S(1)}, bf16[256,512]{1,0:T(8,128)(2,1)S(1)}, u32[]{:S(2)}, u32[]{:S(2)}) collective-permute-start(bf16[256,512]{1,0:T(8,128)(2,1)S(1)} %copy-done.21), channel_id=1, source_target_pairs={{0,4},{4,0},{8,12},{12,8},{1,5},{5,1},{9,13},{13,9},{2,6},{6,2},{1... | collective-permute-start | bytes 786440 | tf_op jit(solution)/shard_map/ppermute | solution.py:45
  212.3 54.7 %collective-permute-start.32 = (bf16[256,2048]{1,0:T(8,128)(2,1)}, bf16[256,2048]{1,0:T(8,128)(2,1)}, u32[]{:S(2)}, u32[]{:S(2)}) collective-permute-start(bf16[256,2048]{1,0:T(8,128)(2,1)} %collective-permute-done.18.refs_2_), channel_id=1, source_target_pairs={{0,4},{4,0},{8,12},{12,8},{1,5},{5,1},{9,13},{13,9},{2,6},{6,2},{1... | collective-permute-start | bytes 3145736 | tf_op jit(solution)/shard_map/ppermute | solution.py:45
  224.7 42.3 %collective-permute-start.33 = (bf16[256,2048]{1,0:T(8,128)(2,1)}, bf16[256,2048]{1,0:T(8,128)(2,1)}, u32[]{:S(2)}, u32[]{:S(2)}) collective-permute-start(bf16[256,2048]{1,0:T(8,128)(2,1)} %collective-permute-done.29.refs_3_), channel_id=1, source_target_pairs={{0,4},{4,0},{8,12},{12,8},{1,5},{5,1},{9,13},{13,9},{2,6},{6,2},{1... | collective-permute-start | bytes 3145736 | tf_op jit(solution)/shard_map/ppermute | solution.py:45
  270.9 28.7 %collective-permute-start.41 = (bf16[512,2048]{1,0:T(8,128)(2,1)}, bf16[512,2048]{1,0:T(8,128)(2,1)S(1)}, u32[]{:S(2)}, u32[]{:S(2)}) collective-permute-start(bf16[512,2048]{1,0:T(8,128)(2,1)} %get-tuple-element.348.refs_2_.refs_3_.refs_8_), channel_id=1, source_target_pairs={{0,4},{4,0},{8,12},{12,8},{1,5},{5,1},{9,13},{13,9},{2,6},{6,2},{1... | collective-permute-start | bytes 6291464 | tf_op jit(solution)/shard_map/ppermute | solution.py:45
  271.4 49.5 %collective-permute-start.43 = (bf16[256,2048]{1,0:T(8,128)(2,1)}, bf16[256,2048]{1,0:T(8,128)(2,1)}, u32[]{:S(2)}, u32[]{:S(2)}) collective-permute-start(bf16[256,2048]{1,0:T(8,128)(2,1)} %get-tuple-element.325.refs_0_), channel_id=1, source_target_pairs={{0,4},{4,0},{8,12},{12,8},{1,5},{5,1},{9,13},{13,9},{2,6},{6,2},{1... | collective-permute-start | bytes 3145736 | tf_op jit(solution)/shard_map/ppermute | solution.py:45
  326.9 37.6 %collective-permute-start.49 = (bf16[512,2048]{1,0:T(8,128)(2,1)}, bf16[512,2048]{1,0:T(8,128)(2,1)}, u32[]{:S(2)}, u32[]{:S(2)}) collective-permute-start(bf16[512,2048]{1,0:T(8,128)(2,1)} %get-tuple-element.315.refs_9_.refs_0_), channel_id=1, source_target_pairs={{0,4},{4,0},{8,12},{12,8},{1,5},{5,1},{9,13},{13,9},{2,6},{6,2},{1... | collective-permute-start | bytes 6291464 | tf_op jit(solution)/shard_map/ppermute | solution.py:45
  385.5 138.9 %reduce-scatter.7.cloned.1.call-start = ((), (), s32[]{:S(2)}) async-start(), calls=%async_computation.8 | async-start | bytes 5242880 | tf_op jit(solution)/shard_map/reduce_scatter | solution.py:859
  385.5 54.1 %collective-permute-start.56 = (bf16[512,2048]{1,0:T(8,128)(2,1)S(1)}, bf16[512,2048]{1,0:T(8,128)(2,1)}, u32[]{:S(2)}, u32[]{:S(2)}) collective-permute-start(bf16[512,2048]{1,0:T(8,128)(2,1)S(1)} %copy-done), channel_id=1, source_target_pairs={{0,4},{4,0},{8,12},{12,8},{1,5},{5,1},{9,13},{13,9},{2,6},{6,2},{1... | collective-permute-start | bytes 6291464 | tf_op jit(solution)/shard_map/ppermute | solution.py:45
  456.4 149.0 %reduce-scatter.9.cloned.1.call-start = ((), (), s32[]{:S(2)}) async-start(), calls=%async_computation.9 | async-start | bytes 10485760 | tf_op jit(solution)/shard_map/reduce_scatter | solution.py:859
  456.9 191.1 %reduce-scatter.11.cloned.1.call-start = ((), (), s32[]{:S(2)}) async-start(), calls=%async_computation.10 | async-start | bytes 2293760 | tf_op jit(solution)/shard_map/reduce_scatter | solution.py:859
  490.1 34.3 %collective-permute-start.58 = (bf16[256,2048]{1,0:T(8,128)(2,1)}, bf16[256,2048]{1,0:T(8,128)(2,1)S(1)}, u32[]{:S(2)}, u32[]{:S(2)}) collective-permute-start(bf16[256,2048]{1,0:T(8,128)(2,1)} %add_rows.9), channel_id=1, source_target_pairs={{0,1},{1,2},{2,3},{3,0},{4,5},{5,6},{6,7},{7,4},{8,9},{9,10},{10,1... | collective-permute-start | bytes 3145736 | tf_op jit(solution)/shard_map/ppermute | solution.py:40
  563.5 35.2 %collective-permute-start.71 = (bf16[256,2048]{1,0:T(8,128)(2,1)}, bf16[256,2048]{1,0:T(8,128)(2,1)S(1)}, u32[]{:S(2)}, u32[]{:S(2)}) collective-permute-start(bf16[256,2048]{1,0:T(8,128)(2,1)} %add_rows.10), channel_id=1, source_target_pairs={{0,1},{1,2},{2,3},{3,0},{4,5},{5,6},{6,7},{7,4},{8,9},{9,10},{10,1... | collective-permute-start | bytes 3145736 | tf_op jit(solution)/shard_map/ppermute | solution.py:40
  563.6 34.1 %collective-permute-start.72 = (bf16[256,512]{1,0:T(8,128)(2,1)S(1)}, bf16[256,512]{1,0:T(8,128)(2,1)S(1)}, u32[]{:S(2)}, u32[]{:S(2)}) collective-permute-start(bf16[256,512]{1,0:T(8,128)(2,1)S(1)} %add_convert_fusion.3), channel_id=1, source_target_pairs={{0,1},{1,2},{2,3},{3,0},{4,5},{5,6},{6,7},{7,4},{8,9},{9,10},{10,1... | collective-permute-start | bytes 786440 | tf_op jit(solution)/shard_map/ppermute | solution.py:40
  611.4 34.6 %collective-permute-start.77 = (bf16[256,512]{1,0:T(8,128)(2,1)S(1)}, bf16[256,512]{1,0:T(8,128)(2,1)S(1)}, u32[]{:S(2)}, u32[]{:S(2)}) collective-permute-start(bf16[256,512]{1,0:T(8,128)(2,1)S(1)} %add_convert_fusion.2), channel_id=1, source_target_pairs={{0,1},{1,2},{2,3},{3,0},{4,5},{5,6},{6,7},{7,4},{8,9},{9,10},{10,1... | collective-permute-start | bytes 786440 | tf_op jit(solution)/shard_map/ppermute | solution.py:40
  (130 other events, 1942.7 us)
Sparse Core Ops, SparseCore 0:
  11.7 70.3 all-gather.3
  84.5 98.2 all-gather.5
  185.3 54.3 all-gather.7
  384.6 50.3 reduce-scatter.4
  455.9 60.0 reduce-scatter.6
  518.9 86.4 reduce-scatter.8
  608.7 33.0 reduce-scatter.10

commit v7 on v6

--- a/solution.py
+++ b/solution.py
@@ -1100,11 +1100,10 @@
         return total.astype(jnp.bfloat16) if place else total
 
     met_qkv = meet([grad_qkv])
-    row_terms = rows_nt(
-        [([[(grad_qkv, place)] for place in places], (late_qkv, 0))], jnp.bfloat16, tp_count, rows
-    )
+    (first_term,) = rows_nt([([[(grad_qkv, order[0])]], (late_qkv, 0))], jnp.bfloat16, 1, rows)
     head_sums = jnp.stack([query_gain_sum, key_gain_sum]).sum(axis=1).reshape(2, 2, HD).sum(axis=1)
-    total, met_qkv = together(row_terms[1], met_qkv)
+    total, met_qkv, grad_qkv = together(first_term, met_qkv, grad_qkv)
+    lines = [[(grad_qkv, place)] for place in order[1:]]
     out_total = out_shard[:, back_places[1] * q_cols : (back_places[1] + 1) * q_cols]
     for step, place in enumerate(order[1:]):
         came = ring_hop(total)
@@ -1118,9 +1117,11 @@
             head_sums = all_sum(head_sums, (CTX, "dp"))
             qkv_product = grad_product(met_normed, [met_qkv], tile=qkv_cols)
             attention_sum = jnp.sum(qkv_product.astype(jnp.float32) * mine_qkv.astype(jnp.float32), axis=1)
-            came, head_sums, qkv_product, attention_sum = together(
-                came, head_sums, qkv_product, attention_sum
+            row_terms = rows_nt([(lines, (late_qkv, 0))], jnp.bfloat16, len(lines), rows)
+            came, head_sums, qkv_product, attention_sum, row_terms = together(
+                came, head_sums, qkv_product, attention_sum, row_terms
             )
+            row_terms = dict(zip(order[1:], row_terms))
             small_sums = jnp.concatenate([attention_sum, head_sums.reshape(-1)])
         if step == 1:
             small_sums = all_sum(small_sums, ("tp",))

time: 668 us -> 669 us (level)
    pallas_call x7 -> x8, Pallas kernels: 64.8 us -> 69.3 us  [rows_nt(): pl.pallas_call(functools.partial(rows_nt_kernel, layouts), grid=(width //...]
    unnamed x145 -> x159, local copies, waits for them, and re-layouts: 15 us -> 11.6 us
  transfers between devices with their start and end apart: 86 -> 86, of which waited for: 32 -> 31; matrix products, arithmetic and copies ran while one was open for 8% -> 8% of each run, Pallas kernels for 42% -> 43%
where the time goes in v7:
time: 669 us; the launch traced here: 660 us
  Pallas kernels  283 us (42%)
  waiting for transfers between devices  238 us (36%)
  starting transfers between devices  56.8 us (8%)
  other arithmetic  25.8 us (4%)
  local copies, waits for them, and re-layouts  23.6 us (4%)
  matrix products  17 us (3%)
  between operations  15.6 us (2%)
    ppermute x21, waiting for transfers between devices, ring_hop(): lax.ppermute(values, 'tp', [(i, (i + 1) % count) for i in range(count)])  106 us
    pallas_call x8, Pallas kernels, rows_nt(): pl.pallas_call(functools.partial(rows_nt_kernel, layouts), grid=(width //...  69.3 us
    pallas_call x5, Pallas kernels, product(): pl.pallas_call(functools.partial(product_kernel, len(left), [len(parts) f...  65.1 us
    ppermute x9, waiting for transfers between devices, shift(): lax.ppermute(values, 'tp', [(i, (i + places) % count) for i in range(coun...  58.1 us
    pallas_call x2, Pallas kernels, feed_rows(): pl.pallas_call(functools.partial(feed_kernel, count), grid=(steps,), out_...  41.6 us
    ppermute x5, waiting for transfers between devices, all_sum(): lax.ppermute(values, axis, [(i, i ^ bit) for i in range(count)])  38.1 us
    pallas_call x2, Pallas kernels, attend_back(): pl.pallas_call(functools.partial(attend_back_kernel, places, blocks, plac...  36.1 us
    ppermute x42, waiting for transfers between devices, ctx_swap(): return lax.ppermute(values, CTX, [(i, i ^ mask) for i in range(count)])  27.5 us
  transfers between devices with their start and end apart: 86, of which 31 were waited for; matrix products, arithmetic and copies ran while one was open for 8% of the time, Pallas kernels for 43%

profile of v7, /device:TPU:0, one launch (start us, length us, event | category | flops | bytes accessed | tf_op | source)
XLA Modules:
  0.0 660.4 jit_solution(5127064126815747903)
XLA Ops:
  18.8 28.2 %collective-permute-done.1 = bf16[256,512]{1,0:T(8,128)(2,1)S(1)} collective-permute-done((bf16[256,512]{1,0:T(8,128)(2,1)S(1)}, bf16[256,512]{1,0:T(8,128)(2,1)S(1)}, u32[]{:S(2)}, u32[]{:S(2)}) %collective-permute-start.1) | collective-permute-done | bytes 262176 | tf_op jit(solution)/shard_map/ppermute | solution.py:82
  69.9 19.8 %collective-permute-done.3.refs_2_ = bf16[256,2048]{1,0:T(8,128)(2,1)} collective-permute-done((bf16[256,2048]{1,0:T(8,128)(2,1)}, bf16[256,2048]{1,0:T(8,128)(2,1)}, u32[]{:S(2)}, u32[]{:S(2)}) %collective-permute-start.3) | collective-permute-done | bytes 1048608 | tf_op jit(solution)/shard_map/ppermute | solution.py:40
  109.1 6.9 %collective-permute-done.8.refs_12_.refs_28_ = bf16[256,256]{1,0:T(8,128)(2,1)S(1)} collective-permute-done((bf16[256,256]{1,0:T(8,128)(2,1)}, bf16[256,256]{1,0:T(8,128)(2,1)S(1)}, u32[]{:S(2)}, u32[]{:S(2)}) %collective-permute-start.8) | collective-permute-done | bytes 131104 | tf_op jit(solution)/shard_map/ppermute | solution.py:45
  135.1 7.1 %collective-permute-done.15.refs_14_.refs_30_ = bf16[256,256]{1,0:T(8,128)(2,1)S(1)} collective-permute-done((bf16[256,256]{1,0:T(8,128)(2,1)}, bf16[256,256]{1,0:T(8,128)(2,1)S(1)}, u32[]{:S(2)}, u32[]{:S(2)}) %collective-permute-start.15) | collective-permute-done | bytes 131104 | tf_op jit(solution)/shard_map/ppermute | solution.py:45
  150.8 18.1 %attend.1 = (bf16[256,512]{1,0:T(8,128)(2,1)}, bf16[256,512]{1,0:T(8,128)(2,1)}, bf16[256,512]{1,0:T(8,128)(2,1)}, bf16[256,512]{1,0:T(8,128)(2,1)}, f32[4,4,512]{2,1,0:T(4,128)}) custom-call(s32[16]{0:T(128)} %stack.92.refs_0_, s32[4,1,256]{2,1,0:T(1,128)} %broadcast_in_dim.27.refs_1_, s32[1,1,256]{2,1,0:T(1,128)} %bitcast.69, ...), custom_call_target="tpu_custom_call" | custom-call | flops 8589934592 | bytes 4194304 | tf_op jit(solution)/shard_map/attend/pallas_call | solution.py:242
  180.9 16.3 %collective-permute-done.24.refs_2_.refs_6_ = bf16[256,512]{1,0:T(8,128)(2,1)S(1)} collective-permute-done((bf16[256,512]{1,0:T(8,128)(2,1)}, bf16[256,512]{1,0:T(8,128)(2,1)S(1)}, u32[]{:S(2)}, u32[]{:S(2)}) %collective-permute-start.24) | collective-permute-done | bytes 262176 | tf_op jit(solution)/shard_map/ppermute | solution.py:82
  198.0 6.9 %rows_nt.8.more_ref = f32[256,2048]{1,0:T(8,128)} custom-call(bf16[256,512]{1,0:T(8,128)(2,1)} %get-tuple-element.354.refs_0_.refs_2_.refs_19_, bf16[256,512]{1,0:T(8,128)(2,1)} %copy-done.16, bf16[256,512]{1,0:T(8,128)(2,1)} %copy-done.18, bf16[256,512]{1,0:T(8,128)(2,1)} %copy-done.20, ...), custom_call_target="tpu_custom_call" | custom-call | flops 2147483648 | bytes 10485760 | tf_op jit(solution)/shard_map/rows_nt/pallas_call | solution.py:616
  213.6 11.8 %collective-permute-done.29.refs_3_ = bf16[256,2048]{1,0:T(8,128)(2,1)} collective-permute-done((bf16[256,2048]{1,0:T(8,128)(2,1)}, bf16[256,2048]{1,0:T(8,128)(2,1)}, u32[]{:S(2)}, u32[]{:S(2)}) %collective-permute-start.29) | collective-permute-done | bytes 1048608 | tf_op jit(solution)/shard_map/ppermute | solution.py:40
  225.5 20.4 %collective-permute-done.27.refs_1_ = bf16[256,2048]{1,0:T(8,128)(2,1)S(1)} collective-permute-done((bf16[256,2048]{1,0:T(8,128)(2,1)}, bf16[256,2048]{1,0:T(8,128)(2,1)S(1)}, u32[]{:S(2)}, u32[]{:S(2)}) %collective-permute-start.27) | collective-permute-done | bytes 1048608 | tf_op jit(solution)/shard_map/ppermute | solution.py:40
  246.8 20.5 %feed_rows.2 = (bf16[512,2048]{1,0:T(8,128)(2,1)}, bf16[512,2048]{1,0:T(8,128)(2,1)}, bf16[512,2048]{1,0:T(8,128)(2,1)}) custom-call(bf16[256,2048]{1,0:T(8,128)(2,1)} %get-tuple-element.328.refs_0_, bf16[256,2048]{1,0:T(8,128)(2,1)} %copy-done.28, bf16[256,2048]{1,0:T(8,128)(2,1)} %bitcast.61, bf16[256,2048]{1,0:T(8,128)(2,1)} %collective-permute-done.11.refs_3_.refs_1_, ...), custom_call_target="tpu_custom_call" | custom-call | flops 12884901888 | bytes 35651584 | tf_op jit(solution)/shard_map/feed_rows/pallas_call | solution.py:547
  279.0 14.0 %rows_nt.9 = (bf16[256,2048]{1,0:T(8,128)(2,1)}, bf16[256,2048]{1,0:T(8,128)(2,1)}) custom-call(bf16[512,2048]{1,0:T(8,128)(2,1)} %get-tuple-element.336.refs_0_.refs_1_.refs_8_, bf16[512,2048]{1,0:T(8,128)(2,1)} %get-tuple-element.336.refs_0_.refs_1_.refs_8_, bf16[512,2048]{1,0:T(8,128)(2,1)} %get-tuple-element.351.refs_2_.refs_3_.refs_8_, ...), custom_call_target="tpu_custom_call" | custom-call | flops 8589934592 | bytes 23068672 | tf_op jit(solution)/shard_map/rows_nt/pallas_call | solution.py:616
  300.1 21.1 %feed_rows.3 = (bf16[512,2048]{1,0:T(8,128)(2,1)}, bf16[512,2048]{1,0:T(8,128)(2,1)}, bf16[512,2048]{1,0:T(8,128)(2,1)}) custom-call(bf16[256,2048]{1,0:T(8,128)(2,1)} %collective-permute-done.28.refs_0_.refs_2_, bf16[256,2048]{1,0:T(8,128)(2,1)} %collective-permute-done.38.refs_1_.refs_3_, bf16[256,2048]{1,0:T(8,128)(2,1)} %collective-permute-done.18.refs_2_, ...), custom_call_target="tpu_custom_call" | custom-call | flops 12884901888 | bytes 35651584 | tf_op jit(solution)/shard_map/feed_rows/pallas_call | solution.py:547
  327.2 14.0 %rows_nt.11 = (bf16[256,2048]{1,0:T(8,128)(2,1)}, bf16[256,2048]{1,0:T(8,128)(2,1)}) custom-call(bf16[512,2048]{1,0:T(8,128)(2,1)} %get-tuple-element.301.refs_0_.refs_1_.refs_9_, bf16[512,2048]{1,0:T(8,128)(2,1)} %get-tuple-element.301.refs_0_.refs_1_.refs_9_, bf16[512,2048]{1,0:T(8,128)(2,1)} %get-tuple-element.302.refs_2_.refs_3_.refs_9_, ...), custom_call_target="tpu_custom_call" | custom-call | flops 8589934592 | bytes 23068672 | tf_op jit(solution)/shard_map/rows_nt/pallas_call | solution.py:616
  341.2 13.5 %collective-permute-done.47.one_ref = bf16[256,2048]{1,0:T(8,128)(2,1)S(1)} collective-permute-done((bf16[256,2048]{1,0:T(8,128)(2,1)}, bf16[256,2048]{1,0:T(8,128)(2,1)S(1)}, u32[]{:S(2)}, u32[]{:S(2)}) %collective-permute-start.47) | collective-permute-done | bytes 1048608 | tf_op jit(solution)/shard_map/ppermute | solution.py:40
  364.8 16.0 %product.5 = bf16[1024,2048]{1,0:T(8,128)(2,1)} custom-call(s32[1]{0:T(128)} %bitcast.31.first_ref, bf16[256,2048]{1,0:T(8,128)(2,1)} %bitcast.62, bf16[256,2048]{1,0:T(8,128)(2,1)} %collective-permute-done.11.refs_3_.refs_1_, bf16[256,2048]{1,0:T(8,128)(2,1)} %collective-permute-done.18.refs_2_, bf16[256,2048]{1,0:T(8,128)(2,1)} %collective-permute-done.29.refs_3_, ...), custom_call_target="tpu_custom_call" | custom-call | flops 8589934592 | bytes 20971520 | tf_op jit(solution)/shard_map/product/pallas_call | solution.py:732
  388.8 9.5 %rows_nt.13 = (bf16[256,2048]{1,0:T(8,128)(2,1)}, bf16[256,2048]{1,0:T(8,128)(2,1)}) custom-call(bf16[512,2048]{1,0:T(8,128)(2,1)} %get-tuple-element.318.refs_9_.refs_0_, bf16[512,2048]{1,0:T(8,128)(2,1)} %get-tuple-element.317.refs_0_.refs_8_.refs_1_, bf16[2048,2048]{1,0:T(8,128)(2,1)} %all-gather.8.cloned.1.call-done.refs_6_.refs_1_.refs_2_), custom_call_target="tpu_custom_call" | custom-call | flops 4294967296 | bytes 12582912 | tf_op jit(solution)/shard_map/rows_nt/pallas_call | solution.py:616
  398.3 16.6 %product.6.refs_12_ = bf16[1024,4096]{1,0:T(8,128)(2,1)} custom-call(s32[1]{0:T(128)} %bitcast.31.first_ref, bf16[256,2048]{1,0:T(8,128)(2,1)} %get-tuple-element.328.refs_0_, bf16[256,2048]{1,0:T(8,128)(2,1)} %copy-done.28, bf16[256,2048]{1,0:T(8,128)(2,1)} %collective-permute-done.28.refs_0_.refs_2_, ...), custom_call_target="tpu_custom_call" | custom-call | flops 8589934592 | bytes 20971520 | tf_op jit(solution)/shard_map/product/pallas_call | solution.py:732
  422.0 6.9 %split_columns.1 = (bf16[256,512]{1,0:T(8,128)(2,1)}, bf16[256,512]{1,0:T(8,128)(2,1)}, bf16[256,512]{1,0:T(8,128)(2,1)}, bf16[256,512]{1,0:T(8,128)(2,1)}) custom-call(bf16[256,2048]{1,0:T(8,128)(2,1)} %get-tuple-element.353.rows_ref.refs_0_, bf16[2048,4096]{1,0:T(8,128)(2,1)} %all-gather.6.cloned.1.call-done.refs_4_.refs_5_.weight_ref), custom_call_target="tpu_custom_call" | custom-call | flops 2147483648 | bytes 10485760 | tf_op jit(solution)/shard_map/split_columns/pallas_call | solution.py:665
  439.6 16.0 %product.8 = bf16[1024,4096]{1,0:T(8,128)(2,1)} custom-call(s32[1]{0:T(128)} %bitcast.31.first_ref, bf16[256,2048]{1,0:T(8,128)(2,1)} %get-tuple-element.328.refs_0_, bf16[256,2048]{1,0:T(8,128)(2,1)} %copy-done.28, bf16[256,2048]{1,0:T(8,128)(2,1)} %collective-permute-done.28.refs_0_.refs_2_, ...), custom_call_target="tpu_custom_call", output_to_operand_aliasing={{}: (13, {})} | custom-call | flops 858993472 | bytes 2097152 | tf_op jit(solution)/shard_map/product/pallas_call | solution.py:732
  461.3 26.2 %attend_back.2 = (bf16[4,192,512]{2,1,0:T(8,128)(2,1)}, f32[4,192,256]{2,1,0:T(8,128)}, f32[4,192,256]{2,1,0:T(8,128)}, bf16[4,192,256]{2,1,0:T(8,128)(2,1)}, bf...) custom-call(s32[16]{0:T(128)} %stack.92.refs_0_, s32[4,1,256]{2,1,0:T(1,128)} %broadcast_in_dim.27.refs_1_, ...), custom_call_target="tpu_custom_call" | custom-call | flops 16106127360 | bytes 6291456 | tf_op jit(solution)/shard_map/attend_back/pallas_call | solution.py:389
  493.2 9.9 %attend_back.3 = (bf16[4,64,512]{2,1,0:T(8,128)(2,1)}, f32[4,64,256]{2,1,0:T(8,128)}, bf16[4,64,256]{2,1,0:T(8,128)(2,1)}, bf16[4,64,256]{2,1,0:T(8,128)(2,1)}, ...) custom-call(s32[16]{0:T(128)} %stack.92.refs_0_, s32[4,1,256]{2,1,0:T(1,128)} %broadcast_in_dim.27.refs_1_, ...), custom_call_target="tpu_custom_call" | custom-call | flops 5368709120 | bytes 2097152 | tf_op jit(solution)/shard_map/attend_back/pallas_call | solution.py:389
  549.0 9.6 %product.9 = bf16[1024,768]{1,0:T(8,128)(2,1)} custom-call(s32[1]{0:T(128)} %bitcast.31.first_ref, bf16[256,2048]{1,0:T(8,128)(2,1)} %multiply_convert_fusion.refs_0_, bf16[256,2048]{1,0:T(8,128)(2,1)} %collective-permute-done.refs_1_, bf16[256,2048]{1,0:T(8,128)(2,1)} %collective-permute-done.3.refs_2_, bf16[256,2048]{1,0:T(8,128)(2,1)} %collective-permute-done.4.refs_3_, ...), custom_call_target="tpu_custom_call" | custom-call | flops 3221225472 | bytes 13107200 | tf_op jit(solution)/shard_map/product/pallas_call | solution.py:732
  566.1 28.7 %collective-permute-done.73 = f32[1152]{0:T(1024)S(1)} collective-permute-done((f32[1152]{0:T(1024)S(1)}, f32[1152]{0:T(1024)S(1)}, u32[]{:S(2)}, u32[]{:S(2)}) %collective-permute-start.73) | collective-permute-done | bytes 4640 | tf_op jit(solution)/shard_map/ppermute | solution.py:75
  621.7 15.2 %collective-permute-done.75.one_ref = bf16[256,2048]{1,0:T(8,128)(2,1)} collective-permute-done((bf16[256,2048]{1,0:T(8,128)(2,1)}, bf16[256,2048]{1,0:T(8,128)(2,1)}, u32[]{:S(2)}, u32[]{:S(2)}) %collective-permute-start.75) | collective-permute-done | bytes 1048608 | tf_op jit(solution)/shard_map/ppermute | solution.py:40
  (419 shorter events, 271.2 us)
Async XLA Ops:
  7.2 84.7 %all-gather.4.cloned.1.call-start = ((), (), s32[]{:S(2)}) async-start(), calls=%async_computation.4 | async-start | bytes 12976128 | tf_op jit(solution)/shard_map/all_gather | solution.py:67
  11.5 186.4 %all-gather.6.cloned.1.call-start = ((), (), s32[]{:S(2)}) async-start(), calls=%async_computation.5 | async-start | bytes 18874368 | tf_op jit(solution)/shard_map/all_gather | solution.py:67
  13.7 35.7 %collective-permute-start = (bf16[256,2048]{1,0:T(8,128)(2,1)}, bf16[256,2048]{1,0:T(8,128)(2,1)}, u32[]{:S(2)}, u32[]{:S(2)}) collective-permute-start(bf16[256,2048]{1,0:T(8,128)(2,1)} %multiply_convert_fusion.refs_0_), channel_id=1, source_target_pairs={{0,1},{1,2},{2,3},{3,0},{4,5},{5,6},{6,7},{7,4},{8,9},{9,10},{10,1... | collective-permute-start | bytes 3145736 | tf_op jit(solution)/shard_map/ppermute | solution.py:40
  16.7 30.2 %collective-permute-start.1 = (bf16[256,512]{1,0:T(8,128)(2,1)S(1)}, bf16[256,512]{1,0:T(8,128)(2,1)S(1)}, u32[]{:S(2)}, u32[]{:S(2)}) collective-permute-start(bf16[256,512]{1,0:T(8,128)(2,1)S(1)} %bitcast.66), channel_id=1, source_target_pairs={{0,3},{1,0},{2,1},{3,2},{4,7},{5,4},{6,5},{7,6},{8,11},{9,8},{10,9... | collective-permute-start | bytes 786440 | tf_op jit(solution)/shard_map/ppermute | solution.py:82
  64.0 182.1 %all-gather.8.cloned.1.call-start = ((), (), s32[]{:S(2)}) async-start(), calls=%async_computation.6 | async-start | bytes 9437184 | tf_op jit(solution)/shard_map/all_gather | solution.py:67
  117.5 370.0 %reduce-scatter.5.cloned.1.call-start = ((), (), s32[]{:S(2)}) async-start(), calls=%async_computation.7 | async-start | bytes 5242880 | tf_op jit(solution)/shard_map/reduce_scatter | solution.py:859
  176.1 35.5 %collective-permute-start.30 = (bf16[256,2048]{1,0:T(8,128)(2,1)}, bf16[256,2048]{1,0:T(8,128)(2,1)}, u32[]{:S(2)}, u32[]{:S(2)}) collective-permute-start(bf16[256,2048]{1,0:T(8,128)(2,1)} %bitcast.60), channel_id=1, source_target_pairs={{0,4},{4,0},{8,12},{12,8},{1,5},{5,1},{9,13},{13,9},{2,6},{6,2},{1... | collective-permute-start | bytes 3145736 | tf_op jit(solution)/shard_map/ppermute | solution.py:45
  176.1 36.0 %collective-permute-start.31 = (bf16[256,2048]{1,0:T(8,128)(2,1)}, bf16[256,2048]{1,0:T(8,128)(2,1)}, u32[]{:S(2)}, u32[]{:S(2)}) collective-permute-start(bf16[256,2048]{1,0:T(8,128)(2,1)} %collective-permute-done.11.refs_3_.refs_1_), channel_id=1, source_target_pairs={{0,4},{4,0},{8,12},{12,8},{1,5},{5,1},{9,13},{13,9},{2,6},{6,2},{1... | collective-permute-start | bytes 3145736 | tf_op jit(solution)/shard_map/ppermute | solution.py:45
  209.3 36.6 %collective-permute-start.27 = (bf16[256,2048]{1,0:T(8,128)(2,1)}, bf16[256,2048]{1,0:T(8,128)(2,1)S(1)}, u32[]{:S(2)}, u32[]{:S(2)}) collective-permute-start(bf16[256,2048]{1,0:T(8,128)(2,1)} %get-tuple-element.328.refs_0_), channel_id=1, source_target_pairs={{0,1},{1,2},{2,3},{3,0},{4,5},{5,6},{6,7},{7,4},{8,9},{9,10},{10,1... | collective-permute-start | bytes 3145736 | tf_op jit(solution)/shard_map/ppermute | solution.py:40
  212.1 55.3 %collective-permute-start.36 = (bf16[256,512]{1,0:T(8,128)(2,1)S(1)}, bf16[256,512]{1,0:T(8,128)(2,1)}, u32[]{:S(2)}, u32[]{:S(2)}) collective-permute-start(bf16[256,512]{1,0:T(8,128)(2,1)S(1)} %copy-done.19), channel_id=1, source_target_pairs={{0,4},{4,0},{8,12},{12,8},{1,5},{5,1},{9,13},{13,9},{2,6},{6,2},{1... | collective-permute-start | bytes 786440 | tf_op jit(solution)/shard_map/ppermute | solution.py:45
  213.1 54.3 %collective-permute-start.37 = (bf16[256,512]{1,0:T(8,128)(2,1)S(1)}, bf16[256,512]{1,0:T(8,128)(2,1)S(1)}, u32[]{:S(2)}, u32[]{:S(2)}) collective-permute-start(bf16[256,512]{1,0:T(8,128)(2,1)S(1)} %copy-done.21), channel_id=1, source_target_pairs={{0,4},{4,0},{8,12},{12,8},{1,5},{5,1},{9,13},{13,9},{2,6},{6,2},{1... | collective-permute-start | bytes 786440 | tf_op jit(solution)/shard_map/ppermute | solution.py:45
  213.5 53.9 %collective-permute-start.32 = (bf16[256,2048]{1,0:T(8,128)(2,1)}, bf16[256,2048]{1,0:T(8,128)(2,1)}, u32[]{:S(2)}, u32[]{:S(2)}) collective-permute-start(bf16[256,2048]{1,0:T(8,128)(2,1)} %collective-permute-done.18.refs_2_), channel_id=1, source_target_pairs={{0,4},{4,0},{8,12},{12,8},{1,5},{5,1},{9,13},{13,9},{2,6},{6,2},{1... | collective-permute-start | bytes 3145736 | tf_op jit(solution)/shard_map/ppermute | solution.py:45
  225.5 41.9 %collective-permute-start.33 = (bf16[256,2048]{1,0:T(8,128)(2,1)}, bf16[256,2048]{1,0:T(8,128)(2,1)}, u32[]{:S(2)}, u32[]{:S(2)}) collective-permute-start(bf16[256,2048]{1,0:T(8,128)(2,1)} %collective-permute-done.29.refs_3_), channel_id=1, source_target_pairs={{0,4},{4,0},{8,12},{12,8},{1,5},{5,1},{9,13},{13,9},{2,6},{6,2},{1... | collective-permute-start | bytes 3145736 | tf_op jit(solution)/shard_map/ppermute | solution.py:45
  271.7 49.5 %collective-permute-start.43 = (bf16[256,2048]{1,0:T(8,128)(2,1)S(1)}, bf16[256,2048]{1,0:T(8,128)(2,1)}, u32[]{:S(2)}, u32[]{:S(2)}) collective-permute-start(bf16[256,2048]{1,0:T(8,128)(2,1)S(1)} %copy-done.27), channel_id=1, source_target_pairs={{0,4},{4,0},{8,12},{12,8},{1,5},{5,1},{9,13},{13,9},{2,6},{6,2},{1... | collective-permute-start | bytes 3145736 | tf_op jit(solution)/shard_map/ppermute | solution.py:45
  327.2 37.7 %collective-permute-start.49 = (bf16[512,2048]{1,0:T(8,128)(2,1)}, bf16[512,2048]{1,0:T(8,128)(2,1)}, u32[]{:S(2)}, u32[]{:S(2)}) collective-permute-start(bf16[512,2048]{1,0:T(8,128)(2,1)} %get-tuple-element.318.refs_9_.refs_0_), channel_id=1, source_target_pairs={{0,4},{4,0},{8,12},{12,8},{1,5},{5,1},{9,13},{13,9},{2,6},{6,2},{1... | collective-permute-start | bytes 6291464 | tf_op jit(solution)/shard_map/ppermute | solution.py:45
  385.8 138.3 %reduce-scatter.7.cloned.1.call-start = ((), (), s32[]{:S(2)}) async-start(), calls=%async_computation.8 | async-start | bytes 5242880 | tf_op jit(solution)/shard_map/reduce_scatter | solution.py:859
  385.8 53.8 %collective-permute-start.56 = (bf16[512,2048]{1,0:T(8,128)(2,1)S(1)}, bf16[512,2048]{1,0:T(8,128)(2,1)}, u32[]{:S(2)}, u32[]{:S(2)}) collective-permute-start(bf16[512,2048]{1,0:T(8,128)(2,1)S(1)} %copy-done.1), channel_id=1, source_target_pairs={{0,4},{4,0},{8,12},{12,8},{1,5},{5,1},{9,13},{13,9},{2,6},{6,2},{1... | collective-permute-start | bytes 6291464 | tf_op jit(solution)/shard_map/ppermute | solution.py:45
  456.3 149.9 %reduce-scatter.9.cloned.1.call-start = ((), (), s32[]{:S(2)}) async-start(), calls=%async_computation.9 | async-start | bytes 10485760 | tf_op jit(solution)/shard_map/reduce_scatter | solution.py:859
  456.9 192.0 %reduce-scatter.11.cloned.1.call-start = ((), (), s32[]{:S(2)}) async-start(), calls=%async_computation.10 | async-start | bytes 2293760 | tf_op jit(solution)/shard_map/reduce_scatter | solution.py:859
  490.9 33.2 %collective-permute-start.58 = (bf16[256,2048]{1,0:T(8,128)(2,1)}, bf16[256,2048]{1,0:T(8,128)(2,1)S(1)}, u32[]{:S(2)}, u32[]{:S(2)}) collective-permute-start(bf16[256,2048]{1,0:T(8,128)(2,1)} %add_rows.9), channel_id=1, source_target_pairs={{0,1},{1,2},{2,3},{3,0},{4,5},{5,6},{6,7},{7,4},{8,9},{9,10},{10,1... | collective-permute-start | bytes 3145736 | tf_op jit(solution)/shard_map/ppermute | solution.py:40
  531.0 29.5 %collective-permute-start.66 = (bf16[256,2048]{1,0:T(8,128)(2,1)}, bf16[256,2048]{1,0:T(8,128)(2,1)}, u32[]{:S(2)}, u32[]{:S(2)}) collective-permute-start(bf16[256,2048]{1,0:T(8,128)(2,1)} %rows_nt.14), channel_id=1, source_target_pairs={{0,1},{1,2},{2,3},{3,0},{4,5},{5,6},{6,7},{7,4},{8,9},{9,10},{10,1... | collective-permute-start | bytes 3145736 | tf_op jit(solution)/shard_map/ppermute | solution.py:40
  563.2 37.2 %collective-permute-start.71 = (bf16[256,2048]{1,0:T(8,128)(2,1)}, bf16[256,2048]{1,0:T(8,128)(2,1)S(1)}, u32[]{:S(2)}, u32[]{:S(2)}) collective-permute-start(bf16[256,2048]{1,0:T(8,128)(2,1)} %add_rows.10), channel_id=1, source_target_pairs={{0,1},{1,2},{2,3},{3,0},{4,5},{5,6},{6,7},{7,4},{8,9},{9,10},{10,1... | collective-permute-start | bytes 3145736 | tf_op jit(solution)/shard_map/ppermute | solution.py:40
  565.1 34.3 %collective-permute-start.72 = (bf16[256,512]{1,0:T(8,128)(2,1)S(1)}, bf16[256,512]{1,0:T(8,128)(2,1)S(1)}, u32[]{:S(2)}, u32[]{:S(2)}) collective-permute-start(bf16[256,512]{1,0:T(8,128)(2,1)S(1)} %add_convert_fusion.3), channel_id=1, source_target_pairs={{0,1},{1,2},{2,3},{3,0},{4,5},{5,6},{6,7},{7,4},{8,9},{9,10},{10,1... | collective-permute-start | bytes 786440 | tf_op jit(solution)/shard_map/ppermute | solution.py:40
  612.3 34.6 %collective-permute-start.77 = (bf16[256,512]{1,0:T(8,128)(2,1)S(1)}, bf16[256,512]{1,0:T(8,128)(2,1)S(1)}, u32[]{:S(2)}, u32[]{:S(2)}) collective-permute-start(bf16[256,512]{1,0:T(8,128)(2,1)S(1)} %add_convert_fusion.2), channel_id=1, source_target_pairs={{0,1},{1,2},{2,3},{3,0},{4,5},{5,6},{6,7},{7,4},{8,9},{9,10},{10,1... | collective-permute-start | bytes 786440 | tf_op jit(solution)/shard_map/ppermute | solution.py:40
  (137 other events, 1785.8 us)
Sparse Core Ops, SparseCore 0:
  11.7 70.3 all-gather.3
  84.5 98.2 all-gather.5
  185.3 54.3 all-gather.7
  385.0 50.9 reduce-scatter.4
  455.8 59.8 reduce-scatter.6
  518.6 87.5 reduce-scatter.8
  609.6 33.0 reduce-scatter.10
